TPU v7x, 128 devices: a whole 4x4x4 slice. The times are simulated.
128 devices in a mesh: req: 8 (over y, core), exp: 16 (over x, z).
Axes of the slice: x: 4, y: 4, z: 4, core: 2. Of those that a mesh axis runs over, the one named last changes fastest.
Arguments:
- tokens: bfloat16 [49152, 1536], P(('req', 'exp')), may hold values from -30 to 30
- segment_lengths: int32 [8, 16], P('req'), may hold values from 1 to 3071, as said below
- segment_adapters: int32 [8, 16], P('req'), may hold values from 0 to 15
- routes: int32 [49152, 4], P(('req', 'exp')), may hold values from 0 to 31, all different within a row; in each aligned block of 384 rows (0 to 383, 384 to 767, ...) at most 64 rows name the same one
- gate_weights: float32 [49152, 4], P(('req', 'exp')), may hold values from 0.05 to 1
- attention_gain: float32 [1536], replicated, may hold values from 0.5 to 1.5
- attention_in: bfloat16 [1536, 2048], P(None, 'req'), may hold values from -5 to 5
- sink_logits: float32 [12], replicated, may hold values from 0 to 6
- attention_out: bfloat16 [1536, 1536], P(None, 'req'), may hold values from -0.15625 to 0.15625
- expert_gain: float32 [1536], replicated, may hold values from 0.5 to 1.5
- expert_gate_up: bfloat16 [32, 1536, 1536], P('exp'), may hold values from -0.15625 to 0.15625
- expert_down: bfloat16 [32, 768, 1536], P('exp'), may hold values from -0.21875 to 0.21875
- adapter_in_down: bfloat16 [16, 1536, 16], P('req'), may hold values from -0.15625 to 0.15625
- adapter_in_up: bfloat16 [16, 16, 2048], P('req'), may hold values from -0.625 to 0.625
- adapter_out_down: bfloat16 [16, 1536, 16], P('req'), may hold values from -0.15625 to 0.15625
- adapter_out_up: bfloat16 [16, 16, 1536], P('req'), may hold values from -0.625 to 0.625
- adapter_expert_down: bfloat16 [16, 1536, 16], P('req'), may hold values from -0.15625 to 0.15625
- adapter_expert_up: bfloat16 [16, 32, 16, 768], P('req', 'exp'), may hold values from -0.625 to 0.625
Outputs:
- layer_output: bfloat16 [49152, 1536], P(('req', 'exp'))
Inputs may be any that keep to these rules, and one draw needn't show every extreme that they name: `segment_lengths`: each row sums to 6144; entry 0 is the group's shared prompt of 1536 to 3071 tokens, the other entries are its requests, none longer than the prompt's most. `routes`: in each aligned block of 384 token rows (the rows of one device) no expert is named more than 64 times, a bound that some block reaches; a row names 4 different experts.
All inputs are finite; a program needn't handle non-finite values.
Results may differ from a plain program's by a relative error of at most 0.012.
The roundings to bfloat16 on the way count: a program that leaves them out, or rounds other values in their place, can miss the bound.
Values may be sent and summed in bfloat16 or wider, within the bound.
A program may use at most 128 MiB of HBM per device.

v0:
```python
import jax
import jax.numpy as jnp
from jax import lax
from jax.sharding import PartitionSpec as P

HEADS = 12
KVH = 2
HD = 128
EXPERTS = 32
WINDOW = 4096
CAP = 64


EPSILON = 1e-06
NEGATIVE = -1e30


def scaled_norm(inputs, gain):
    floats = inputs.astype(jnp.float32)
    inverse = lax.rsqrt(jnp.mean(floats * floats, axis=-1, keepdims=True) + EPSILON)
    return (floats * inverse * gain).astype(jnp.bfloat16)


def segment_of(positions, lengths):
    seg_ends = jnp.cumsum(lengths)
    return jnp.sum((positions[:, None] >= seg_ends[None, :]).astype(jnp.int32), axis=1)


def adapter_select(token_adapter, adapter_count, rank_size):
    owners = jnp.repeat(jnp.arange(adapter_count, dtype=jnp.int32), rank_size)
    return token_adapter[:, None] == owners[None, :]


def low_coords(inputs, select, first_factor):
    adapter_count, inner_width, rank_size = first_factor.shape
    joined = jnp.transpose(first_factor, (1, 0, 2)).reshape(inner_width, adapter_count * rank_size)
    coords = jnp.dot(inputs, joined, preferred_element_type=jnp.float32)
    return jnp.where(select, coords, 0.0).astype(jnp.bfloat16)


def low_rank(inputs, select, first_factor, second_factor):
    coords = low_coords(inputs, select, first_factor)
    adapter_count, rank_size, outer_width = second_factor.shape
    return jnp.dot(
        coords,
        second_factor.reshape(adapter_count * rank_size, outer_width),
        preferred_element_type=jnp.float32,
    )


def online_step(softmax_state, queries, key_piece, positions, segments, key_pos, lengths):
    running_max, running_sum, weighted = softmax_state
    key_heads = queries.shape[1]
    head_size = queries.shape[3]
    key_part = key_piece[:, : key_heads * head_size].reshape(-1, key_heads, head_size)
    value_part = key_piece[:, key_heads * head_size :].reshape(-1, key_heads, head_size)
    scores = jnp.einsum(
        "tkgd,skd->tkgs", queries, key_part, preferred_element_type=jnp.float32
    ) * head_size ** (-0.5)
    key_seg = segment_of(key_pos, lengths)
    allowed = (
        (key_pos[None, :] <= positions[:, None])
        & (positions[:, None] - key_pos[None, :] < WINDOW)
        & (key_pos[None, :] >= 0)
    )
    allowed = allowed & ((key_seg[None, :] == segments[:, None]) | (key_seg[None, :] == 0))
    scores = jnp.where(allowed[:, None, None, :], scores, NEGATIVE)
    new_max = jnp.maximum(running_max, jnp.max(scores, axis=-1))
    factor = jnp.exp(running_max - new_max)
    weights = jnp.exp(scores - new_max[..., None])
    running_sum = running_sum * factor + jnp.sum(weights, axis=-1)
    weighted = weighted * factor[..., None] + jnp.einsum(
        "tkgs,skd->tkgd",
        weights.astype(jnp.bfloat16),
        value_part,
        preferred_element_type=jnp.float32,
    )
    return (new_max, running_sum, weighted)


def body(
    tokens,
    segment_lengths,
    segment_adapters,
    routes,
    gate_weights,
    attention_gain,
    attention_in,
    sink_logits,
    attention_out,
    expert_gain,
    expert_gate_up,
    expert_down,
    adapter_in_down,
    adapter_in_up,
    adapter_out_down,
    adapter_out_up,
    adapter_expert_down,
    adapter_expert_up,
):
    tok_rows = tokens.shape[0]
    lengths = segment_lengths[0]
    segment_total = lengths.shape[0]
    first_pos = lax.axis_index("exp") * tok_rows
    positions = first_pos + jnp.arange(tok_rows, dtype=jnp.int32)
    segments = segment_of(positions, lengths)
    matches = segments[:, None] == jnp.arange(segment_total, dtype=jnp.int32)[None, :]
    token_adapter = jnp.sum(jnp.where(matches, segment_adapters[0][None, :], 0), axis=1)
    held_factors = (
        lax.all_gather(adapter_in_down, "req", axis=0, tiled=True),
        lax.all_gather(adapter_in_up, "req", axis=0, tiled=True),
        lax.all_gather(adapter_out_down, "req", axis=0, tiled=True),
        lax.all_gather(adapter_out_up, "req", axis=0, tiled=True),
        lax.all_gather(adapter_expert_down, "req", axis=0, tiled=True),
        lax.all_gather(adapter_expert_up, "req", axis=0, tiled=True),
    )
    in_low, in_high, out_low, out_high, expert_low, expert_high = held_factors
    select = adapter_select(token_adapter, in_low.shape[0], in_low.shape[2])
    normed = scaled_norm(tokens, attention_gain)
    full_in, full_out = (
        lax.all_gather(attention_in, "req", axis=1, tiled=True),
        lax.all_gather(attention_out, "req", axis=1, tiled=True),
    )
    base_heads = jnp.dot(normed, full_in, preferred_element_type=jnp.float32)
    projected = (base_heads + low_rank(normed, select, in_low, in_high)).astype(jnp.bfloat16)
    group_size = HEADS // KVH
    queries = projected[:, : HEADS * HD].reshape(tok_rows, KVH, group_size, HD)
    key_value = projected[:, HEADS * HD :]
    sink_grid = jnp.broadcast_to(
        sink_logits.reshape(KVH, group_size)[None], (tok_rows, KVH, group_size)
    )
    initial = (
        sink_grid,
        jnp.ones_like(sink_grid),
        jnp.zeros((tok_rows, KVH, group_size, HD), jnp.float32),
    )
    key_piece = lax.all_gather(key_value, "exp", axis=0, tiled=True)
    piece_rows = key_piece.shape[0]
    block_rows = tok_rows
    block_count = piece_rows // block_rows
    block_rows = 2 * block_rows
    block_count = block_count // 2
    stacked = key_piece.reshape(block_count, block_rows, key_piece.shape[1])

    def visit_block(softmax_state, block_input):
        key_block, block_index = block_input
        block_start = block_index * block_rows
        key_pos = block_start + jnp.arange(block_rows, dtype=jnp.int32)

        def update(state_now):
            return online_step(state_now, queries, key_block, positions, segments, key_pos, lengths)

        def unchanged(state_now):
            return state_now

        needed = jnp.logical_and(
            block_start <= positions[-1], block_start + block_rows - 1 > positions[0] - WINDOW
        )
        return (lax.cond(needed, update, unchanged, softmax_state), None)

    softmax_state = lax.scan(
        visit_block, initial, (stacked, jnp.arange(block_count, dtype=jnp.int32))
    )[0]
    running_max, running_sum, weighted = softmax_state
    attended = (
        (weighted / running_sum[..., None]).reshape(tok_rows, HEADS * HD).astype(jnp.bfloat16)
    )
    base_out = jnp.dot(attended, full_out, preferred_element_type=jnp.float32)
    residual = (
        tokens.astype(jnp.float32) + base_out + low_rank(attended, select, out_low, out_high)
    ).astype(jnp.bfloat16)
    normed_two = scaled_norm(residual, expert_gain)
    low_parts = low_coords(normed_two, select, expert_low)
    top_count = routes.shape[1]
    picked = routes.reshape(-1)
    expert_hot = (picked[:, None] == jnp.arange(EXPERTS, dtype=jnp.int32)[None, :]).astype(
        jnp.int32
    )
    arrival = jnp.sum((jnp.cumsum(expert_hot, axis=0) - 1) * expert_hot, axis=1)
    slot_index = picked * CAP + arrival
    pick_ids = jnp.arange(picked.shape[0], dtype=jnp.int32)
    sources = jnp.full((EXPERTS * CAP,), -1, jnp.int32).at[slot_index].set(pick_ids)
    filled = (sources >= 0)[:, None]
    token_rows = jnp.maximum(sources, 0) // top_count
    peer_count = lax.axis_size("exp")
    local_experts = EXPERTS // peer_count
    send_rows = jnp.where(filled, normed_two[token_rows], 0).reshape(
        peer_count, local_experts, CAP, -1
    )
    send_low = jnp.where(filled, low_parts[token_rows], 0).reshape(
        peer_count, local_experts, CAP, -1
    )
    adapter_bank = jnp.transpose(expert_high, (1, 0, 2, 3)).reshape(
        local_experts, -1, expert_high.shape[3]
    )
    arrived_rows = lax.all_to_all(send_rows, "exp", split_axis=0, concat_axis=0, tiled=True)
    arrived_low = lax.all_to_all(send_low, "exp", split_axis=0, concat_axis=0, tiled=True)
    hidden_width = expert_down.shape[1]
    gate_up = jnp.einsum(
        "necd,edf->necf", arrived_rows, expert_gate_up, preferred_element_type=jnp.float32
    )
    up_part = gate_up[..., hidden_width:] + jnp.einsum(
        "necr,erf->necf", arrived_low, adapter_bank, preferred_element_type=jnp.float32
    )
    hidden = (jax.nn.relu(gate_up[..., :hidden_width]) * up_part).astype(jnp.bfloat16)
    outputs = jnp.einsum(
        "necf,efd->necd", hidden, expert_down, preferred_element_type=jnp.float32
    ).astype(jnp.bfloat16)
    returned = lax.all_to_all(outputs, "exp", split_axis=0, concat_axis=0, tiled=True)
    flat_back = returned.reshape(EXPERTS * CAP, -1)
    per_pick = flat_back[slot_index].astype(jnp.float32).reshape(tok_rows, top_count, -1)
    combined = jnp.sum(gate_weights[:, :, None] * per_pick, axis=1)
    return (residual.astype(jnp.float32) + combined).astype(jnp.bfloat16)


def solution(mesh):
    return jax.shard_map(
        body,
        mesh=mesh,
        in_specs=(
            P(("req", "exp"), None),
            P("req", None),
            P("req", None),
            P(("req", "exp"), None),
            P(("req", "exp"), None),
            P(),
            P(None, "req"),
            P(),
            P(None, "req"),
            P(),
            P("exp", None, None),
            P("exp", None, None),
            P("req", None, None),
            P("req", None, None),
            P("req", None, None),
            P("req", None, None),
            P("req", None, None),
            P("req", "exp", None, None),
        ),
        out_specs=P(("req", "exp"), None),
        check_vma=False,
    )
```

profile of v0, /device:TPU:100, one launch (start us, length us, event | category | flops | bytes accessed | tf_op | source)
XLA Modules:
  0.0 715.1 jit_solution(5835617143987328835)
XLA Ops:
  13.3 15.3 %all_gather.28 = bf16[16,1536,16]{1,2,0:T(8,128)(2,1)S(1)} all-gather(bf16[2,1536,16]{1,2,0:T(8,128)(2,1)} %param.34), channel_id=1, replica_groups=mesh['req'=8,'exp'=16] {'req'}, dimensions={0}, use_global_device_ids=true | all-gather | bytes 884736 | tf_op jit(solution)/shard_map/all_gather | solution.py:110
  28.6 27.7 %all-gather.5.cloned.1.call-done = bf16[1536,2048]{1,0:T(8,128)(2,1)} async-done(((bf16[1536,256]{1,0:T(8,128)(2,1)}), bf16[1536,2048]{1,0:T(8,128)(2,1)}) %all-gather.5.cloned.1.call-update) | async-done | bytes 6291472 | tf_op jit(solution)/shard_map/all_gather | solution.py:121
  63.8 18.2 %all-gather.7.cloned.1.call-done = bf16[16,16,2048]{2,1,0:T(8,128)(2,1)} async-done(((bf16[2,16,2048]{2,1,0:T(8,128)(2,1)}), bf16[16,16,2048]{2,1,0:T(8,128)(2,1)}) %all-gather.7.cloned.1.call-update) | async-done | bytes 1048592 | tf_op jit(solution)/shard_map/all_gather | solution.py:111
  89.6 9.1 %reduce-window.27 = s32[32,12,128]{2,1,0:T(8,128)S(1)} reduce-window(s32[32,12,128]{2,1,0:T(8,128)S(1)} %fusion.45, s32[]{:T(128)} %copy.156), window={size=1x1x128 pad=0_0x0_0x127_0}, to_apply=%region_12.13 | reduce-window | flops 6242304 | bytes 393220 | tf_op jit(solution)/shard_map/reduce-window.2
  107.9 14.4 %all_gather.32 = bf16[16,1536,16]{1,2,0:T(8,128)(2,1)} all-gather(bf16[2,1536,16]{1,2,0:T(8,128)(2,1)S(1)} %copy-done.7), channel_id=1, replica_groups=mesh['req'=8,'exp'=16] {'req'}, dimensions={0}, use_global_device_ids=true | all-gather | bytes 884736 | tf_op jit(solution)/shard_map/all_gather | solution.py:112
  122.3 14.9 %all_gather.33 = bf16[16,16,1536]{2,1,0:T(8,128)(2,1)} all-gather(bf16[2,16,1536]{2,1,0:T(8,128)(2,1)S(1)} %copy-done.8), channel_id=1, replica_groups=mesh['req'=8,'exp'=16] {'req'}, dimensions={0}, use_global_device_ids=true | all-gather | bytes 884736 | tf_op jit(solution)/shard_map/all_gather | solution.py:113
  146.5 8.6 %copy.108 = bf16[8,768,512]{1,2,0:T(8,128)(2,1)} copy(bf16[8,768,512]{2,1,0:T(8,128)(2,1)} %bitcast.111) | data formatting | bytes 12582912 | tf_op jit(solution)/shard_map/while | solution.py:161
  157.1 203.7 %while.18 = (s32[]{:T(128)}, f32[384,2,6]{0,2,1:T(8,128)}, f32[384,2,6]{0,2,1:T(8,128)}, f32[384,2,6,128]{3,0,2,1:T(8,128)S(1)}, s32[8]{0:T(128)}, /*index=5*/s3...) while((s32[]{:T(128)}, f32[384,2,6]{0,2,1:T(8,128)}, ...), condition=%wide.region_11.12_spmd, body=%wide.region_4.11_spmd.sunk | while | flops 1854454528 | bytes 54025088 | solution.py:161
  161.1 29.1 %conditional.2 = ((f32[384,2,6]{0,2,1:T(8,128)}, f32[384,2,6]{0,2,1:T(8,128)}, f32[384,2,6,128]{3,0,2,1:T(8,128)S(1)})) conditional(s32[]{:T(128)} %convert_element_type.156, (f32[384,2,6]{0,2,1:T(8,128)}, f32[384,2,6]{0,2,1:T(8,128)}, f32[384,2,6,128]{3,0,2,1:T(8,128)S(1)}) %tuple.62, (s32[]{:T(128)}, s32[768]{0:T(1024)S(1)}, s32[384]{0:T(512)}, ...), branch_computations={%region_5.5_spmd, %region_6.10_spmd} | conditional | flops 1854454528 | bytes 54021700 | solution.py:159
  173.5 8.2 %fusion.1 = f32[384,2,6]{0,2,1:T(8,128)S(1)} fusion(f32[2,768,384,6]{2,1,3,0:T(8,128)} %get-tuple-element.399, f32[384,2,6]{0,2,1:T(8,128)S(1)} %max.11, pred[384,768]{0,1:T(8,128)(4,1)S(1)} %fusion.10), kind=kLoop, calls=%fused_computation.7 | loop fusion | flops 14151168 | bytes 14487552 | tf_op jit(solution)/shard_map/while/body/eval_jaxpr/cond/branch_1_fun/reduce_sum | solution.py:71
  181.7 7.8 %bitcast_add_fusion = f32[384,2,6,128]{3,0,2,1:T(8,128)S(1)} fusion(f32[384,2,6,128]{3,0,2,1:T(8,128)S(1)} %get-tuple-element.284, bf16[768,2,128,1]{0,2,3,1:T(8,128)(2,1)S(1)} %bitcast.110, f32[2,768,384,6]{2,1,3,0:T(8,128)} %get-tuple-element.399, f32[384,2,6]{0,2,1:T(8,128)S(1)} %max.11, pred[384,768]{0,1:T(8,128)(4,1)S(1)} %fusion.10, ...), kind=kOutput, calls=%fused_computation.11 | convolution fusion | flops 921305088 | bytes 19599360 | tf_op jit(solution)/shard_map/while/body/eval_jaxpr/cond/branch_1_fun/tkgs,skd->tkgd/dot_general | solution.py:72
  194.1 28.6 %conditional.2 = ((f32[384,2,6]{0,2,1:T(8,128)}, f32[384,2,6]{0,2,1:T(8,128)}, f32[384,2,6,128]{3,0,2,1:T(8,128)S(1)})) conditional(s32[]{:T(128)} %convert_element_type.156, (f32[384,2,6]{0,2,1:T(8,128)}, f32[384,2,6]{0,2,1:T(8,128)}, f32[384,2,6,128]{3,0,2,1:T(8,128)S(1)}) %tuple.62, (s32[]{:T(128)}, s32[768]{0:T(1024)S(1)}, s32[384]{0:T(512)}, ...), branch_computations={%region_5.5_spmd, %region_6.10_spmd} | conditional | flops 1854454528 | bytes 54021700 | solution.py:159
  206.3 7.9 %fusion.1 = f32[384,2,6]{0,2,1:T(8,128)S(1)} fusion(f32[2,768,384,6]{2,1,3,0:T(8,128)} %get-tuple-element.399, f32[384,2,6]{0,2,1:T(8,128)S(1)} %max.11, pred[384,768]{0,1:T(8,128)(4,1)S(1)} %fusion.10), kind=kLoop, calls=%fused_computation.7 | loop fusion | flops 14151168 | bytes 14487552 | tf_op jit(solution)/shard_map/while/body/eval_jaxpr/cond/branch_1_fun/reduce_sum | solution.py:71
  226.7 28.6 %conditional.2 = ((f32[384,2,6]{0,2,1:T(8,128)}, f32[384,2,6]{0,2,1:T(8,128)}, f32[384,2,6,128]{3,0,2,1:T(8,128)S(1)})) conditional(s32[]{:T(128)} %convert_element_type.156, (f32[384,2,6]{0,2,1:T(8,128)}, f32[384,2,6]{0,2,1:T(8,128)}, f32[384,2,6,128]{3,0,2,1:T(8,128)S(1)}) %tuple.62, (s32[]{:T(128)}, s32[768]{0:T(1024)S(1)}, s32[384]{0:T(512)}, ...), branch_computations={%region_5.5_spmd, %region_6.10_spmd} | conditional | flops 1854454528 | bytes 54021700 | solution.py:159
  238.9 7.9 %fusion.1 = f32[384,2,6]{0,2,1:T(8,128)S(1)} fusion(f32[2,768,384,6]{2,1,3,0:T(8,128)} %get-tuple-element.399, f32[384,2,6]{0,2,1:T(8,128)S(1)} %max.11, pred[384,768]{0,1:T(8,128)(4,1)S(1)} %fusion.10), kind=kLoop, calls=%fused_computation.7 | loop fusion | flops 14151168 | bytes 14487552 | tf_op jit(solution)/shard_map/while/body/eval_jaxpr/cond/branch_1_fun/reduce_sum | solution.py:71
  259.2 28.6 %conditional.2 = ((f32[384,2,6]{0,2,1:T(8,128)}, f32[384,2,6]{0,2,1:T(8,128)}, f32[384,2,6,128]{3,0,2,1:T(8,128)S(1)})) conditional(s32[]{:T(128)} %convert_element_type.156, (f32[384,2,6]{0,2,1:T(8,128)}, f32[384,2,6]{0,2,1:T(8,128)}, f32[384,2,6,128]{3,0,2,1:T(8,128)S(1)}) %tuple.62, (s32[]{:T(128)}, s32[768]{0:T(1024)S(1)}, s32[384]{0:T(512)}, ...), branch_computations={%region_5.5_spmd, %region_6.10_spmd} | conditional | flops 1854454528 | bytes 54021700 | solution.py:159
  271.4 7.9 %fusion.1 = f32[384,2,6]{0,2,1:T(8,128)S(1)} fusion(f32[2,768,384,6]{2,1,3,0:T(8,128)} %get-tuple-element.399, f32[384,2,6]{0,2,1:T(8,128)S(1)} %max.11, pred[384,768]{0,1:T(8,128)(4,1)S(1)} %fusion.10), kind=kLoop, calls=%fused_computation.7 | loop fusion | flops 14151168 | bytes 14487552 | tf_op jit(solution)/shard_map/while/body/eval_jaxpr/cond/branch_1_fun/reduce_sum | solution.py:71
  291.7 28.6 %conditional.2 = ((f32[384,2,6]{0,2,1:T(8,128)}, f32[384,2,6]{0,2,1:T(8,128)}, f32[384,2,6,128]{3,0,2,1:T(8,128)S(1)})) conditional(s32[]{:T(128)} %convert_element_type.156, (f32[384,2,6]{0,2,1:T(8,128)}, f32[384,2,6]{0,2,1:T(8,128)}, f32[384,2,6,128]{3,0,2,1:T(8,128)S(1)}) %tuple.62, (s32[]{:T(128)}, s32[768]{0:T(1024)S(1)}, s32[384]{0:T(512)}, ...), branch_computations={%region_5.5_spmd, %region_6.10_spmd} | conditional | flops 1854454528 | bytes 54021700 | solution.py:159
  304.0 7.9 %fusion.1 = f32[384,2,6]{0,2,1:T(8,128)S(1)} fusion(f32[2,768,384,6]{2,1,3,0:T(8,128)} %get-tuple-element.399, f32[384,2,6]{0,2,1:T(8,128)S(1)} %max.11, pred[384,768]{0,1:T(8,128)(4,1)S(1)} %fusion.10), kind=kLoop, calls=%fused_computation.7 | loop fusion | flops 14151168 | bytes 14487552 | tf_op jit(solution)/shard_map/while/body/eval_jaxpr/cond/branch_1_fun/reduce_sum | solution.py:71
  324.3 28.6 %conditional.2 = ((f32[384,2,6]{0,2,1:T(8,128)}, f32[384,2,6]{0,2,1:T(8,128)}, f32[384,2,6,128]{3,0,2,1:T(8,128)S(1)})) conditional(s32[]{:T(128)} %convert_element_type.156, (f32[384,2,6]{0,2,1:T(8,128)}, f32[384,2,6]{0,2,1:T(8,128)}, f32[384,2,6,128]{3,0,2,1:T(8,128)S(1)}) %tuple.62, (s32[]{:T(128)}, s32[768]{0:T(1024)S(1)}, s32[384]{0:T(512)}, ...), branch_computations={%region_5.5_spmd, %region_6.10_spmd} | conditional | flops 1854454528 | bytes 54021700 | solution.py:159
  336.5 7.9 %fusion.1 = f32[384,2,6]{0,2,1:T(8,128)S(1)} fusion(f32[2,768,384,6]{2,1,3,0:T(8,128)} %get-tuple-element.399, f32[384,2,6]{0,2,1:T(8,128)S(1)} %max.11, pred[384,768]{0,1:T(8,128)(4,1)S(1)} %fusion.10), kind=kLoop, calls=%fused_computation.7 | loop fusion | flops 14151168 | bytes 14487552 | tf_op jit(solution)/shard_map/while/body/eval_jaxpr/cond/branch_1_fun/reduce_sum | solution.py:71
  374.8 10.1 %gather_fusion = bf16[2048,1536]{1,0:T(8,128)(2,1)} fusion(bf16[384,1536]{1,0:T(8,128)(2,1)S(1)} %fusion.32, s32[2048]{0:T(1024)S(1)} %copy-done.12), kind=kCustom, calls=%fused_computation | custom fusion | bytes 12591104 | tf_op jit(solution)/shard_map/gather | solution.py:187
  390.9 35.5 %all-to-all-start = ((bf16[16,2,64,1536]{3,2,1,0:T(8,128)(2,1)}), bf16[16,2,64,1536]{3,2,1,0:T(8,128)(2,1)}, u32[]{:S(2)}, u32[]{:S(2)}) async-start(bf16[16,2,64,1536]{3,2,1,0:T(8,128)(2,1)} %broadcast_select_fusion), calls=%async_computation | async-start | bytes 12582912 | tf_op jit(solution)/shard_map/all_to_all | solution.py:196
  426.4 13.7 %all_gather.34 = bf16[16,1536,16]{1,2,0:T(8,128)(2,1)S(1)} all-gather(bf16[2,1536,16]{1,2,0:T(8,128)(2,1)S(1)} %copy-done.9), channel_id=1, replica_groups=mesh['req'=8,'exp'=16] {'req'}, dimensions={0}, use_global_device_ids=true | all-gather | bytes 884736 | tf_op jit(solution)/shard_map/all_gather | solution.py:114
  440.1 13.4 %all_gather.35 = bf16[16,2,16,768]{3,2,0,1:T(8,128)(2,1)S(1)} all-gather(bf16[2,2,16,768]{3,2,0,1:T(8,128)(2,1)S(1)} %copy.118), channel_id=1, replica_groups=mesh['req'=8,'exp'=16] {'req'}, dimensions={0}, use_global_device_ids=true | all-gather | bytes 884736 | tf_op jit(solution)/shard_map/all_gather | solution.py:115
  462.7 68.7 %all-to-all-done = bf16[16,2,64,1536]{3,2,1,0:T(8,128)(2,1)} async-done(((bf16[16,2,64,1536]{3,2,1,0:T(8,128)(2,1)}), bf16[16,2,64,1536]{3,2,1,0:T(8,128)(2,1)}, u32[]{:S(2)}, u32[]{:S(2)}) %all-to-all-start) | async-done | bytes 6291488 | tf_op jit(solution)/shard_map/all_to_all | solution.py:196
  538.3 17.0 %fusion.15 = f32[16,2,64,1536]{3,2,0,1:T(8,128)} fusion(bf16[2,1536,1536]{2,1,0:T(8,128)(2,1)} %param.32, bf16[16,2,64,1536]{3,2,1,0:T(8,128)(2,1)} %all-to-all-done), kind=kOutput, calls=%fused_computation.28 | convolution fusion | flops 9663676416 | bytes 28311552 | tf_op jit(solution)/shard_map/necd,edf->necf/dot_general | solution.py:199
  555.3 11.3 %convert_bitcast_fusion = bf16[16,2,64,1536]{3,2,0,1:T(8,128)(2,1)} fusion(bf16[2,768,1536]{2,1,0:T(8,128)(2,1)} %param.33, f32[16,2,64,1536]{3,2,0,1:T(8,128)} %fusion.15, bf16[2,256,768,1]{2,1,3,0:T(8,128)(2,1)S(1)} %bitcast.121, bf16[16,2,64,256]{3,2,1,0:T(8,128)(2,1)S(1)} %all-to-all-done.1), kind=kOutput, calls=%fused_computation.34 | convolution fusion | flops 5646581760 | bytes 25427968 | tf_op jit(solution)/shard_map/necf,efd->necd/dot_general | solution.py:206
  580.7 88.7 %all-to-all-done.2 = bf16[16,2,64,1536]{3,2,1,0:T(8,128)(2,1)} async-done(((bf16[16,2,64,1536]{3,2,1,0:T(8,128)(2,1)}), bf16[16,2,64,1536]{3,2,1,0:T(8,128)(2,1)}, u32[]{:S(2)}, u32[]{:S(2)}) %all-to-all-start.2) | async-done | bytes 6291488 | tf_op jit(solution)/shard_map/all_to_all | solution.py:209
  669.4 14.0 %gather_fusion.2 = bf16[1536,1536]{1,0:T(8,128)(2,1)} fusion(bf16[2048,1536]{1,0:T(8,128)(2,1)} %bitcast.40, s32[2048]{0:T(1024)S(1)} %pad_clamp_fusion), kind=kCustom, calls=%fused_computation.2 | custom fusion | bytes 9443328 | tf_op jit(solution)/shard_map/gather | solution.py:211
  683.4 9.7 %reshape.299 = f32[384,4,1536]{2,1,0:T(4,128)} reshape(bf16[1536,1536]{1,0:T(8,128)(2,1)} %gather_fusion.2) | data formatting | bytes 14155776 | tf_op jit(solution)/shard_map/convert_element_type | solution.py:211
  693.1 12.3 %multiply_reduce_fusion = f32[384,1536]{1,0:T(8,128)} fusion(f32[384,4,1536]{2,1,0:T(4,128)} %reshape.299, f32[384,4]{1,0:T(8,128)S(1)} %copy.111), kind=kLoop, calls=%fused_computation.27 | loop fusion | flops 4128768 | bytes 11802624 | tf_op jit(solution)/shard_map/reduce_sum | solution.py:212
  (254 shorter events, 231.1 us)
Async XLA Ops:
  6.5 49.7 %all-gather.5.cloned.1.call-start = ((), (), s32[]{:S(2)}) async-start(), calls=%async_computation.3 | async-start | bytes 7077888 | tf_op jit(solution)/shard_map/all_gather | solution.py:121
  7.3 74.7 %all-gather.7.cloned.1.call-start = ((), (), s32[]{:S(2)}) async-start(), calls=%async_computation.4 | async-start | bytes 1179648 | tf_op jit(solution)/shard_map/all_gather | solution.py:111
  8.0 138.5 %all-gather.9.cloned.1.call-start = ((), (), s32[]{:S(2)}) async-start(), calls=%async_computation.5 | async-start | bytes 6684672 | tf_op jit(solution)/shard_map/all_gather | solution.py:137
  9.0 72.9 %copy-start.18 = (s32[256]{0:T(256)}, s32[256]{0:T(256)S(1)}, u32[]{:S(2)}) copy-start(s32[256]{0:T(256)S(1)} %eq.84) | copy-start | bytes 3076
  11.7 70.3 %copy-start.16 = (s32[384]{0:T(512)}, s32[384]{0:T(512)S(1)}, u32[]{:S(2)}) copy-start(s32[384]{0:T(512)S(1)} %select_reduce_fusion) | copy-start | bytes 4612
  13.3 50.5 %copy-start.21 = (f32[384]{0:T(512)}, f32[384]{0:T(512)S(1)}, u32[]{:S(2)}) copy-start(f32[384]{0:T(512)S(1)} %add_rsqrt_fusion.1) | copy-start | bytes 4612
  28.6 53.4 %copy-start = (bf16[384,1536]{1,0:T(8,128)(2,1)S(1)}, bf16[384,1536]{1,0:T(8,128)(2,1)}, u32[]{:S(2)}) copy-start(bf16[384,1536]{1,0:T(8,128)(2,1)} %param.22) | copy-start | bytes 3538948
  85.8 22.0 %copy-start.7 = (bf16[2,1536,16]{1,2,0:T(8,128)(2,1)S(1)}, bf16[2,1536,16]{1,2,0:T(8,128)(2,1)}, u32[]{:S(2)}) copy-start(bf16[2,1536,16]{1,2,0:T(8,128)(2,1)} %param.36) | copy-start | bytes 294916
  85.8 36.5 %copy-start.8 = (bf16[2,16,1536]{2,1,0:T(8,128)(2,1)S(1)}, bf16[2,16,1536]{2,1,0:T(8,128)(2,1)}, u32[]{:S(2)}) copy-start(bf16[2,16,1536]{2,1,0:T(8,128)(2,1)} %param.37) | copy-start | bytes 294916
  86.7 278.4 %all-gather.11.cloned.1.call-start = ((), (), s32[]{:S(2)}) async-start(), calls=%async_computation.6 | async-start | bytes 5308416 | tf_op jit(solution)/shard_map/all_gather | solution.py:122
  99.7 22.6 %copy-start.13 = (s32[1536]{0:T(1024)}, s32[1536]{0:T(1024)S(1)}, u32[]{:S(2)}) copy-start(s32[1536]{0:T(1024)S(1)} %fusion.56) | copy-start | bytes 18436
  167.0 6.5 copy-start.3
  173.5 8.2 %copy-start.4 = (f32[384,2,6]{0,2,1:T(8,128)S(1)}, f32[384,2,6]{0,2,1:T(8,128)}, u32[]{:S(2)}) copy-start(f32[384,2,6]{0,2,1:T(8,128)} %get-tuple-element.283) | copy-start | bytes 55300 | tf_op jit(solution)/shard_map/while/body/eval_jaxpr/cond
  181.7 7.9 %copy-start.5 = (f32[384,2,6]{0,2,1:T(8,128)}, f32[384,2,6]{0,2,1:T(8,128)S(1)}, u32[]{:S(2)}) copy-start(f32[384,2,6]{0,2,1:T(8,128)S(1)} %get-tuple-element.479) | copy-start | bytes 55300 | tf_op jit(solution)/shard_map/while/body/eval_jaxpr/cond
  206.3 7.9 %copy-start.4 = (f32[384,2,6]{0,2,1:T(8,128)S(1)}, f32[384,2,6]{0,2,1:T(8,128)}, u32[]{:S(2)}) copy-start(f32[384,2,6]{0,2,1:T(8,128)} %get-tuple-element.283) | copy-start | bytes 55300 | tf_op jit(solution)/shard_map/while/body/eval_jaxpr/cond
  214.3 7.8 %copy-start.5 = (f32[384,2,6]{0,2,1:T(8,128)}, f32[384,2,6]{0,2,1:T(8,128)S(1)}, u32[]{:S(2)}) copy-start(f32[384,2,6]{0,2,1:T(8,128)S(1)} %get-tuple-element.479) | copy-start | bytes 55300 | tf_op jit(solution)/shard_map/while/body/eval_jaxpr/cond
  238.9 7.9 %copy-start.4 = (f32[384,2,6]{0,2,1:T(8,128)S(1)}, f32[384,2,6]{0,2,1:T(8,128)}, u32[]{:S(2)}) copy-start(f32[384,2,6]{0,2,1:T(8,128)} %get-tuple-element.283) | copy-start | bytes 55300 | tf_op jit(solution)/shard_map/while/body/eval_jaxpr/cond
  246.8 7.8 %copy-start.5 = (f32[384,2,6]{0,2,1:T(8,128)}, f32[384,2,6]{0,2,1:T(8,128)S(1)}, u32[]{:S(2)}) copy-start(f32[384,2,6]{0,2,1:T(8,128)S(1)} %get-tuple-element.479) | copy-start | bytes 55300 | tf_op jit(solution)/shard_map/while/body/eval_jaxpr/cond
  271.4 7.9 %copy-start.4 = (f32[384,2,6]{0,2,1:T(8,128)S(1)}, f32[384,2,6]{0,2,1:T(8,128)}, u32[]{:S(2)}) copy-start(f32[384,2,6]{0,2,1:T(8,128)} %get-tuple-element.283) | copy-start | bytes 55300 | tf_op jit(solution)/shard_map/while/body/eval_jaxpr/cond
  279.4 7.8 %copy-start.5 = (f32[384,2,6]{0,2,1:T(8,128)}, f32[384,2,6]{0,2,1:T(8,128)S(1)}, u32[]{:S(2)}) copy-start(f32[384,2,6]{0,2,1:T(8,128)S(1)} %get-tuple-element.479) | copy-start | bytes 55300 | tf_op jit(solution)/shard_map/while/body/eval_jaxpr/cond
  304.0 7.9 %copy-start.4 = (f32[384,2,6]{0,2,1:T(8,128)S(1)}, f32[384,2,6]{0,2,1:T(8,128)}, u32[]{:S(2)}) copy-start(f32[384,2,6]{0,2,1:T(8,128)} %get-tuple-element.283) | copy-start | bytes 55300 | tf_op jit(solution)/shard_map/while/body/eval_jaxpr/cond
  311.9 7.8 %copy-start.5 = (f32[384,2,6]{0,2,1:T(8,128)}, f32[384,2,6]{0,2,1:T(8,128)S(1)}, u32[]{:S(2)}) copy-start(f32[384,2,6]{0,2,1:T(8,128)S(1)} %get-tuple-element.479) | copy-start | bytes 55300 | tf_op jit(solution)/shard_map/while/body/eval_jaxpr/cond
  336.5 7.9 %copy-start.4 = (f32[384,2,6]{0,2,1:T(8,128)S(1)}, f32[384,2,6]{0,2,1:T(8,128)}, u32[]{:S(2)}) copy-start(f32[384,2,6]{0,2,1:T(8,128)} %get-tuple-element.283) | copy-start | bytes 55300 | tf_op jit(solution)/shard_map/while/body/eval_jaxpr/cond
  344.5 7.8 %copy-start.5 = (f32[384,2,6]{0,2,1:T(8,128)}, f32[384,2,6]{0,2,1:T(8,128)S(1)}, u32[]{:S(2)}) copy-start(f32[384,2,6]{0,2,1:T(8,128)S(1)} %get-tuple-element.479) | copy-start | bytes 55300 | tf_op jit(solution)/shard_map/while/body/eval_jaxpr/cond
  374.7 10.2 %copy-start.11 = (pred[16,2,64]{2,1,0:T(4,128)(4,1)S(1)}, pred[16,2,64]{2,1,0:T(4,128)(4,1)}, u32[]{:S(2)}) copy-start(pred[16,2,64]{2,1,0:T(4,128)(4,1)} %broadcast_in_dim.122) | copy-start | bytes 6148
  390.9 35.5 %copy-start.10 = (bf16[2,2,16,768]{3,2,1,0:T(8,128)(2,1)S(1)}, bf16[2,2,16,768]{3,2,1,0:T(8,128)(2,1)}, u32[]{:S(2)}) copy-start(bf16[2,2,16,768]{3,2,1,0:T(8,128)(2,1)} %param.39) | copy-start | bytes 294916
  390.9 35.5 %copy-start.9 = (bf16[2,1536,16]{1,2,0:T(8,128)(2,1)S(1)}, bf16[2,1536,16]{1,2,0:T(8,128)(2,1)}, u32[]{:S(2)}) copy-start(bf16[2,1536,16]{1,2,0:T(8,128)(2,1)} %param.38) | copy-start | bytes 294916
  390.9 140.5 %all-to-all-start = ((bf16[16,2,64,1536]{3,2,1,0:T(8,128)(2,1)}), bf16[16,2,64,1536]{3,2,1,0:T(8,128)(2,1)}, u32[]{:S(2)}, u32[]{:S(2)}) async-start(bf16[16,2,64,1536]{3,2,1,0:T(8,128)(2,1)} %broadcast_select_fusion), calls=%async_computation | async-start | bytes 12582912 | tf_op jit(solution)/shard_map/all_to_all | solution.py:196
  531.4 23.9 %all-to-all-start.1 = ((bf16[16,2,64,256]{3,2,1,0:T(8,128)(2,1)}), bf16[16,2,64,256]{3,2,1,0:T(8,128)(2,1)S(1)}, u32[]{:S(2)}, u32[]{:S(2)}) async-start(bf16[16,2,64,256]{3,2,1,0:T(8,128)(2,1)} %broadcast_select_fusion.1), calls=%async_computation.1 | async-start | bytes 2097152 | tf_op jit(solution)/shard_map/all_to_all | solution.py:197
  572.8 7.7 %copy-start.22 = (f32[384,4]{0,1:T(4,128)S(1)}, f32[384,4]{0,1:T(4,128)}, u32[]{:S(2)}) copy-start(f32[384,4]{0,1:T(4,128)} %param.26) | copy-start | bytes 18436
  572.8 7.9 %copy-start.14 = (s32[1536]{0:T(1024)S(1)}, s32[1536]{0:T(1024)}, u32[]{:S(2)}) copy-start(s32[1536]{0:T(1024)} %copy-done.13) | copy-start | bytes 18436
  572.8 96.6 %all-to-all-start.2 = ((bf16[16,2,64,1536]{3,2,1,0:T(8,128)(2,1)}), bf16[16,2,64,1536]{3,2,1,0:T(8,128)(2,1)}, u32[]{:S(2)}, u32[]{:S(2)}) async-start(bf16[16,2,64,1536]{3,2,1,0:T(8,128)(2,1)} %copy.120), calls=%async_computation.2 | async-start | bytes 12582912 | tf_op jit(solution)/shard_map/all_to_all | solution.py:209
  (13 other events, 65.7 us)
Sparse Core Ops, SparseCore 0:
  9.0 47.1 all-gather.4
  58.0 23.9 all-gather.6
  86.8 59.6 all-gather.8
  148.0 35.6 all-gather.10
where the time goes:
time: 723 us; the launch traced here: 715 us
  waiting for transfers between devices  211 us (29%)
  matrix products  134 us (19%)
  local copies, waits for them, and re-layouts  116 us (16%)
  other arithmetic  106 us (15%)
  blocking collectives  71.7 us (10%)
  starting transfers between devices  50.3 us (7%)
  between operations  14.4 us (2%)
  loops' own time  11.5 us (2%)
    all_to_all x1, waiting for transfers between devices, body(): lax.all_to_all(outputs, 'exp', split_axis=0, concat_axis=0, tiled=True)  88.7 us
    all_to_all x1, waiting for transfers between devices, body(): lax.all_to_all(send_rows, 'exp', split_axis=0, concat_axis=0, tiled=True)  68.7 us
    reduce_sum x6, other arithmetic, online_step(): running_sum = running_sum * factor + jnp.sum(weights, axis=-1)  47.7 us
    dot_general x6, matrix products, online_step(): jnp.einsum('tkgs,skd->tkgd', weights.astype(jnp.bfloat16), value_part, pr...  46.8 us
    dot_general x6, matrix products, online_step(): jnp.einsum('tkgd,skd->tkgs', queries, key_part, preferred_element_type=jn...  38.2 us
    all_to_all x1, starting transfers between devices, body(): lax.all_to_all(send_rows, 'exp', split_axis=0, concat_axis=0, tiled=True)  35.5 us
    all_gather x1, waiting for transfers between devices, body(): lax.all_gather(attention_in, 'req', axis=1, tiled=True)  27.7 us
    all_gather x1, waiting for transfers between devices, body(): lax.all_gather(adapter_in_up, 'req', axis=0, tiled=True)  18.2 us
  transfers between devices with their start and end apart: 7, of which 5 were waited for; matrix products, arithmetic and copies ran while one was open for 38% of the time, Pallas kernels for 0%

commit v1 on v0

--- a/solution.py
+++ b/solution.py
@@ -2,6 +2,8 @@
 import jax.numpy as jnp
 from jax import lax
 from jax.sharding import PartitionSpec as P
+from jax.experimental import pallas as pl
+from jax.experimental.pallas import tpu as pltpu
 
 HEADS = 12
 KVH = 2
@@ -48,34 +50,108 @@
     )
 
 
-def online_step(softmax_state, queries, key_piece, positions, segments, key_pos, lengths):
-    running_max, running_sum, weighted = softmax_state
-    key_heads = queries.shape[1]
-    head_size = queries.shape[3]
-    key_part = key_piece[:, : key_heads * head_size].reshape(-1, key_heads, head_size)
-    value_part = key_piece[:, key_heads * head_size :].reshape(-1, key_heads, head_size)
-    scores = jnp.einsum(
-        "tkgd,skd->tkgs", queries, key_part, preferred_element_type=jnp.float32
-    ) * head_size ** (-0.5)
-    key_seg = segment_of(key_pos, lengths)
-    allowed = (
-        (key_pos[None, :] <= positions[:, None])
-        & (positions[:, None] - key_pos[None, :] < WINDOW)
-        & (key_pos[None, :] >= 0)
-    )
-    allowed = allowed & ((key_seg[None, :] == segments[:, None]) | (key_seg[None, :] == 0))
-    scores = jnp.where(allowed[:, None, None, :], scores, NEGATIVE)
-    new_max = jnp.maximum(running_max, jnp.max(scores, axis=-1))
-    factor = jnp.exp(running_max - new_max)
-    weights = jnp.exp(scores - new_max[..., None])
-    running_sum = running_sum * factor + jnp.sum(weights, axis=-1)
-    weighted = weighted * factor[..., None] + jnp.einsum(
-        "tkgs,skd->tkgd",
-        weights.astype(jnp.bfloat16),
-        value_part,
-        preferred_element_type=jnp.float32,
-    )
-    return (new_max, running_sum, weighted)
+KEY_BLOCK = 512
+
+
+def attention_kernel(first_ref, q_ref, k_ref, v_ref, qseg_ref, kseg_ref, init_ref, o_ref,
+                     max_ref, sum_ref, acc_ref):
+    j = pl.program_id(1)
+    tok_rows = qseg_ref.shape[0]
+    rows = q_ref.shape[1]
+    group_size = rows // tok_rows
+    first_pos = first_ref[0]
+    low = jnp.maximum(first_pos - (WINDOW - 1), 0) // KEY_BLOCK
+    high = (first_pos + tok_rows - 1) // KEY_BLOCK
+
+    @pl.when(j == 0)
+    def _():
+        max_ref[...] = init_ref[0]
+        sum_ref[...] = jnp.ones_like(sum_ref)
+        acc_ref[...] = jnp.zeros_like(acc_ref)
+
+    @pl.when(low + j <= high)
+    def _():
+        block = low + j
+        scores = lax.dot_general(
+            q_ref[0], k_ref[...], (((1,), (1,)), ((), ())),
+            preferred_element_type=jnp.float32,
+        ) * HD ** (-0.5)
+        query_pos = first_pos + lax.broadcasted_iota(jnp.int32, (tok_rows, KEY_BLOCK), 0)
+        key_pos = block * KEY_BLOCK + lax.broadcasted_iota(jnp.int32, (tok_rows, KEY_BLOCK), 1)
+        key_seg = kseg_ref[...]
+        allowed = (
+            (key_pos <= query_pos)
+            & (query_pos - key_pos < WINDOW)
+            & ((key_seg == qseg_ref[...]) | (key_seg == 0))
+        )
+        scores = jnp.where(
+            allowed[None], scores.reshape(group_size, tok_rows, KEY_BLOCK), NEGATIVE
+        ).reshape(rows, KEY_BLOCK)
+        prev_max = max_ref[...]
+        new_max = jnp.maximum(prev_max, jnp.max(scores, axis=1, keepdims=True))
+        factor = jnp.exp(prev_max - new_max)
+        weights = jnp.exp(scores - new_max)
+        sum_ref[...] = sum_ref[...] * factor + jnp.sum(weights, axis=1, keepdims=True)
+        acc_ref[...] = acc_ref[...] * factor + jnp.dot(
+            weights.astype(jnp.bfloat16), v_ref[...], preferred_element_type=jnp.float32
+        )
+        max_ref[...] = new_max
+
+    @pl.when(j == pl.num_programs(1) - 1)
+    def _():
+        o_ref[0] = (acc_ref[...] / sum_ref[...]).astype(o_ref.dtype)
+
+
+def window_attention(query_cols, key_piece, positions, segments, lengths, sink_logits):
+    tok_rows = query_cols.shape[0]
+    group_size = HEADS // KVH
+    rows = group_size * tok_rows
+    piece_rows = key_piece.shape[0]
+    block_total = piece_rows // KEY_BLOCK
+    steps = min(block_total, (WINDOW + tok_rows - 2) // KEY_BLOCK + 2)
+    queries = jnp.transpose(
+        query_cols.reshape(tok_rows, KVH, group_size, HD), (1, 2, 0, 3)
+    ).reshape(KVH, rows, HD)
+    key_seg = segment_of(jnp.arange(piece_rows, dtype=jnp.int32), lengths).reshape(1, piece_rows)
+    query_seg = segments.reshape(tok_rows, 1)
+    init = jnp.broadcast_to(
+        sink_logits.reshape(KVH, group_size, 1, 1), (KVH, group_size, tok_rows, 1)
+    ).reshape(KVH, rows, 1)
+    first = positions[:1]
+
+    def key_block(h, j, first_ref):
+        f = first_ref[0]
+        low = jnp.maximum(f - (WINDOW - 1), 0) // KEY_BLOCK
+        high = (f + tok_rows - 1) // KEY_BLOCK
+        return jnp.minimum(low + j, high)
+
+    grid_spec = pltpu.PrefetchScalarGridSpec(
+        num_scalar_prefetch=1,
+        grid=(KVH, steps),
+        in_specs=[
+            pl.BlockSpec((1, rows, HD), lambda h, j, f: (h, 0, 0)),
+            pl.BlockSpec((KEY_BLOCK, HD), lambda h, j, f: (key_block(h, j, f), h)),
+            pl.BlockSpec((KEY_BLOCK, HD), lambda h, j, f: (key_block(h, j, f), KVH + h)),
+            pl.BlockSpec((tok_rows, 1), lambda h, j, f: (0, 0)),
+            pl.BlockSpec((1, KEY_BLOCK), lambda h, j, f: (0, key_block(h, j, f))),
+            pl.BlockSpec((1, rows, 1), lambda h, j, f: (h, 0, 0)),
+        ],
+        out_specs=pl.BlockSpec((1, rows, HD), lambda h, j, f: (h, 0, 0)),
+        scratch_shapes=[
+            pltpu.VMEM((rows, 1), jnp.float32),
+            pltpu.VMEM((rows, 1), jnp.float32),
+            pltpu.VMEM((rows, HD), jnp.float32),
+        ],
+    )
+    out = pl.pallas_call(
+        attention_kernel,
+        grid_spec=grid_spec,
+        out_shape=jax.ShapeDtypeStruct((KVH, rows, HD), jnp.bfloat16),
+        compiler_params=pltpu.CompilerParams(dimension_semantics=("arbitrary", "arbitrary")),
+    )(first, queries, key_piece, key_piece, query_seg, key_seg, init)
+    return jnp.transpose(
+        out.reshape(KVH, group_size, tok_rows, HD), (2, 0, 1, 3)
+    ).reshape(tok_rows, HEADS * HD)
 
 
 def body(
@@ -124,46 +200,10 @@
     base_heads = jnp.dot(normed, full_in, preferred_element_type=jnp.float32)
     projected = (base_heads + low_rank(normed, select, in_low, in_high)).astype(jnp.bfloat16)
     group_size = HEADS // KVH
-    queries = projected[:, : HEADS * HD].reshape(tok_rows, KVH, group_size, HD)
     key_value = projected[:, HEADS * HD :]
-    sink_grid = jnp.broadcast_to(
-        sink_logits.reshape(KVH, group_size)[None], (tok_rows, KVH, group_size)
-    )
-    initial = (
-        sink_grid,
-        jnp.ones_like(sink_grid),
-        jnp.zeros((tok_rows, KVH, group_size, HD), jnp.float32),
-    )
     key_piece = lax.all_gather(key_value, "exp", axis=0, tiled=True)
-    piece_rows = key_piece.shape[0]
-    block_rows = tok_rows
-    block_count = piece_rows // block_rows
-    block_rows = 2 * block_rows
-    block_count = block_count // 2
-    stacked = key_piece.reshape(block_count, block_rows, key_piece.shape[1])
-
-    def visit_block(softmax_state, block_input):
-        key_block, block_index = block_input
-        block_start = block_index * block_rows
-        key_pos = block_start + jnp.arange(block_rows, dtype=jnp.int32)
-
-        def update(state_now):
-            return online_step(state_now, queries, key_block, positions, segments, key_pos, lengths)
-
-        def unchanged(state_now):
-            return state_now
-
-        needed = jnp.logical_and(
-            block_start <= positions[-1], block_start + block_rows - 1 > positions[0] - WINDOW
-        )
-        return (lax.cond(needed, update, unchanged, softmax_state), None)
-
-    softmax_state = lax.scan(
-        visit_block, initial, (stacked, jnp.arange(block_count, dtype=jnp.int32))
-    )[0]
-    running_max, running_sum, weighted = softmax_state
-    attended = (
-        (weighted / running_sum[..., None]).reshape(tok_rows, HEADS * HD).astype(jnp.bfloat16)
+    attended = window_attention(
+        projected[:, : HEADS * HD], key_piece, positions, segments, lengths, sink_logits
     )
     base_out = jnp.dot(attended, full_out, preferred_element_type=jnp.float32)
     residual = (

time: 723 us -> 575 us (0.80)
  Pallas kernels: 0 us -> 90.9 us
  matrix products: 134 us -> 49.8 us
  other arithmetic: 106 us -> 35.5 us
  local copies, waits for them, and re-layouts: 116 us -> 67.2 us
  starting transfers between devices: 50.3 us -> 29.8 us
  loops' own time: 11.5 us -> 0 us
    pallas_call x0 -> x1, Pallas kernels: none -> 90.9 us  [window_attention(): pl.pallas_call(attention_kernel, grid_spec=grid_spec, out_shape=jax.Shape...]
    dot_general x12 -> x0, matrix products: 84.9 us -> none  [the longest x6 46.8 us: online_step(): jnp.einsum('tkgs,skd->tkgd', weights.astype(jnp.bfloat16), value_part, pr...]
    reduce_sum x6 -> x0, other arithmetic: 47.7 us -> none  [online_step(): running_sum = running_sum * factor + jnp.sum(weights, axis=-1)]
    all_to_all x1, starting transfers between devices: 35.5 us -> 15.1 us  [body(): lax.all_to_all(send_rows, 'exp', split_axis=0, concat_axis=0, tiled=True)]
    while x3 -> x0, local copies, waits for them, and re-layouts: 12.5 us -> none  [body(): lax.scan(visit_block, initial, (stacked, jnp.arange(block_count, dtype=jn...]
    another operation x9 -> x0, loops' own time: 11.5 us -> none  [the longest x1 10.8 us: body(): lax.scan(visit_block, initial, (stacked, jnp.arange(block_count, dtype=jn...]
    slice x19 -> x5, local copies, waits for them, and re-layouts: 13.8 us -> 2.3 us  [the longest x1 1.16 us: window_attention(): first = positions[:1]]
    and x6 -> x0, other arithmetic: 10.5 us -> none  [online_step(): allowed & ((key_seg[None, :] == segments[:, None]) | (key_seg[None, :] ==...]
  transfers between devices with their start and end apart: 7 -> 7, of which waited for: 5 -> 5; matrix products, arithmetic and copies ran while one was open for 38% -> 11% of each run, Pallas kernels for 0% -> 16%
where the time goes in v1:
time: 575 us; the launch traced here: 567 us
  waiting for transfers between devices  210 us (37%)
  Pallas kernels  90.9 us (16%)
  blocking collectives  70.5 us (12%)
  local copies, waits for them, and re-layouts  67.2 us (12%)
  matrix products  49.8 us (9%)
  other arithmetic  35.5 us (6%)
  starting transfers between devices  29.8 us (5%)
  between operations  13.7 us (2%)
    pallas_call x1, Pallas kernels, window_attention(): pl.pallas_call(attention_kernel, grid_spec=grid_spec, out_shape=jax.Shape...  90.9 us
    all_to_all x1, waiting for transfers between devices, body(): lax.all_to_all(outputs, 'exp', split_axis=0, concat_axis=0, tiled=True)  87.1 us
    all_to_all x1, waiting for transfers between devices, body(): lax.all_to_all(send_rows, 'exp', split_axis=0, concat_axis=0, tiled=True)  68 us
    all_gather x1, waiting for transfers between devices, body(): lax.all_gather(attention_in, 'req', axis=1, tiled=True)  28.4 us
    all_gather x1, waiting for transfers between devices, body(): lax.all_gather(adapter_in_up, 'req', axis=0, tiled=True)  18.8 us
    dot_general x1, matrix products, body(): jnp.einsum('necd,edf->necf', arrived_rows, expert_gate_up, preferred_elem...  17.1 us
    all_to_all x1, starting transfers between devices, body(): lax.all_to_all(send_rows, 'exp', split_axis=0, concat_axis=0, tiled=True)  15.1 us
    all_gather x1, blocking collectives, body(): lax.all_gather(adapter_in_down, 'req', axis=0, tiled=True)  14.9 us
  transfers between devices with their start and end apart: 7, of which 5 were waited for; matrix products, arithmetic and copies ran while one was open for 11% of the time, Pallas kernels for 16%

profile of v1, /device:TPU:100, one launch (start us, length us, event | category | flops | bytes accessed | tf_op | source)
XLA Modules:
  0.0 566.9 jit_solution(13244374550528943518)
XLA Ops:
  12.1 14.9 %all_gather.28 = bf16[16,1536,16]{1,2,0:T(8,128)(2,1)S(1)} all-gather(bf16[2,1536,16]{1,2,0:T(8,128)(2,1)} %param.30), channel_id=1, replica_groups=mesh['req'=8,'exp'=16] {'req'}, dimensions={0}, use_global_device_ids=true | all-gather | bytes 884736 | tf_op jit(solution)/shard_map/all_gather | solution.py:186
  27.0 28.4 %all-gather.5.cloned.1.call-done = bf16[1536,2048]{1,0:T(8,128)(2,1)} async-done(((bf16[1536,256]{1,0:T(8,128)(2,1)}), bf16[1536,2048]{1,0:T(8,128)(2,1)}) %all-gather.5.cloned.1.call-update) | async-done | bytes 6291472 | tf_op jit(solution)/shard_map/all_gather | solution.py:197
  55.5 7.1 %fusion.30 = f32[384,2048]{1,0:T(8,128)} fusion(bf16[1536,2048]{1,0:T(8,128)(2,1)} %all-gather.5.cloned.1.call-done, bf16[384,1536]{1,0:T(8,128)(2,1)S(1)} %copy-done, f32[1536]{0:T(1024)S(1)} %copy-done.18, f32[384]{0:T(512)S(1)} %add_rsqrt_fusion.1), kind=kOutput, calls=%fused_computation.46 | convolution fusion | flops 2418278400 | bytes 10624512 | tf_op jit(solution)/shard_map/dot_general | solution.py:200
  62.6 18.8 %all-gather.7.cloned.1.call-done = bf16[16,16,2048]{2,1,0:T(8,128)(2,1)} async-done(((bf16[2,16,2048]{2,1,0:T(8,128)(2,1)}), bf16[16,16,2048]{2,1,0:T(8,128)(2,1)}) %all-gather.7.cloned.1.call-update) | async-done | bytes 1048592 | tf_op jit(solution)/shard_map/all_gather | solution.py:187
  81.4 3.8 add_convert_fusion
  89.2 3.7 broadcast_in_dim.100.init_ref
  93.0 9.1 %reduce-window.19 = s32[32,12,128]{2,1,0:T(8,128)S(1)} reduce-window(s32[32,12,128]{2,1,0:T(8,128)S(1)} %fusion.32, s32[]{:T(128)} %constant.47.clone.1), window={size=1x1x128 pad=0_0x0_0x127_0}, to_apply=%region_5.6 | reduce-window | flops 6242304 | bytes 393220 | tf_op jit(solution)/shard_map/reduce-window.1
  103.1 6.2 %scatter_custom_fusion = s32[2048]{0:T(1024)S(1)} fusion(s32[1536]{0:T(1024)S(1)} %fusion.43, s32[1536]{0:T(1024)S(1)} %iota.27, s32[]{:T(128)} %constant.48.clone.1), kind=kCustom, calls=%fused_computation.73 | custom fusion | bytes 8196 | tf_op jit(solution)/shard_map/scatter | solution.py:222
  110.1 13.4 %all_gather.32 = bf16[16,1536,16]{1,2,0:T(8,128)(2,1)S(1)} all-gather(bf16[2,1536,16]{1,2,0:T(8,128)(2,1)S(1)} %copy-done.3), channel_id=1, replica_groups=mesh['req'=8,'exp'=16] {'req'}, dimensions={0}, use_global_device_ids=true | all-gather | bytes 884736 | tf_op jit(solution)/shard_map/all_gather | solution.py:188
  123.5 14.9 %all_gather.33 = bf16[16,16,1536]{2,1,0:T(8,128)(2,1)} all-gather(bf16[2,16,1536]{2,1,0:T(8,128)(2,1)S(1)} %copy-done.4), channel_id=1, replica_groups=mesh['req'=8,'exp'=16] {'req'}, dimensions={0}, use_global_device_ids=true | all-gather | bytes 884736 | tf_op jit(solution)/shard_map/all_gather | solution.py:189
  140.7 5.2 all-gather.9.cloned.1.call-done.k_ref.v_ref
  145.9 90.9 %shard_map.172 = bf16[2,2304,128]{2,1,0:T(8,128)(2,1)} custom-call(s32[1]{0:T(128)} %slice.21.first_ref, bf16[2,2304,128]{2,1,0:T(8,128)(2,1)} %bitcast.81, bf16[6144,512]{1,0:T(8,128)(2,1)} %all-gather.9.cloned.1.call-done.k_ref.v_ref, bf16[6144,512]{1,0:T(8,128)(2,1)} %all-gather.9.cloned.1.call-done.k_ref.v_ref, s32[384,1]{1,0:T(8,128)} %broadcast_in_dim.99.qseg_ref, ...), custom_call_target="tpu_custom_call" | custom-call | tf_op jit(solution)/shard_map/pallas_call | solution.py:146
  236.7 1.8 copy.93
  238.6 6.2 %convert_add_fusion.1 = f32[384,1536]{1,0:T(8,128)} fusion(bf16[384,1536]{1,0:T(8,128)(2,1)S(1)} %copy-done.1, bf16[384,1536]{0,1:T(8,128)(2,1)S(1)} %bitcast.79, bf16[1536,1536]{0,1:T(8,128)(2,1)} %all-gather.11.cloned.1.call-done), kind=kOutput, calls=%fused_computation.19 | convolution fusion | flops 1813118976 | bytes 9437184 | tf_op jit(solution)/shard_map/dot_general | solution.py:208
  244.8 3.8 fusion.17
  249.0 10.1 %gather_fusion = bf16[2048,1536]{1,0:T(8,128)(2,1)} fusion(bf16[384,1536]{1,0:T(8,128)(2,1)S(1)} %fusion.19, s32[2048]{0:T(1024)S(1)} %fusion.41), kind=kCustom, calls=%fused_computation | custom fusion | bytes 12591104 | tf_op jit(solution)/shard_map/gather | solution.py:227
  259.1 6.0 %broadcast_select_fusion = bf16[16,2,64,1536]{3,2,1,0:T(8,128)(2,1)} fusion(bf16[16,2,64,1536]{3,2,1,0:T(8,128)(2,1)} %bitcast.77, pred[16,2,64]{2,1,0:T(4,128)(4,1)S(1)} %broadcast_in_dim.93), kind=kLoop, calls=%fused_computation.14 | loop fusion | flops 3145728 | bytes 12584960 | tf_op jit(solution)/shard_map/jit(_where)/select_n | solution.py:227
  265.1 15.1 %all-to-all-start = ((bf16[16,2,64,1536]{3,2,1,0:T(8,128)(2,1)}), bf16[16,2,64,1536]{3,2,1,0:T(8,128)(2,1)}, u32[]{:S(2)}, u32[]{:S(2)}) async-start(bf16[16,2,64,1536]{3,2,1,0:T(8,128)(2,1)} %broadcast_select_fusion), calls=%async_computation | async-start | bytes 12582912 | tf_op jit(solution)/shard_map/all_to_all | solution.py:236
  280.2 13.8 %all_gather.34 = bf16[16,1536,16]{1,2,0:T(8,128)(2,1)S(1)} all-gather(bf16[2,1536,16]{1,2,0:T(8,128)(2,1)S(1)} %copy-done.5), channel_id=1, replica_groups=mesh['req'=8,'exp'=16] {'req'}, dimensions={0}, use_global_device_ids=true | all-gather | bytes 884736 | tf_op jit(solution)/shard_map/all_gather | solution.py:190
  293.9 13.5 %all_gather.35 = bf16[16,2,16,768]{3,2,0,1:T(8,128)(2,1)S(1)} all-gather(bf16[2,2,16,768]{3,2,0,1:T(8,128)(2,1)S(1)} %copy.101), channel_id=1, replica_groups=mesh['req'=8,'exp'=16] {'req'}, dimensions={0}, use_global_device_ids=true | all-gather | bytes 884736 | tf_op jit(solution)/shard_map/all_gather | solution.py:191
  308.0 7.5 %gather_fusion.1 = bf16[2048,256]{1,0:T(8,128)(2,1)S(1)} fusion(bf16[384,256]{1,0:T(8,128)(2,1)S(1)} %fusion.23, s32[2048]{0:T(1024)S(1)} %fusion.41), kind=kCustom, calls=%fused_computation.1 | custom fusion | bytes 2105344 | tf_op jit(solution)/shard_map/gather | solution.py:230
  316.7 68.0 %all-to-all-done = bf16[16,2,64,1536]{3,2,1,0:T(8,128)(2,1)} async-done(((bf16[16,2,64,1536]{3,2,1,0:T(8,128)(2,1)}), bf16[16,2,64,1536]{3,2,1,0:T(8,128)(2,1)}, u32[]{:S(2)}, u32[]{:S(2)}) %all-to-all-start) | async-done | bytes 6291488 | tf_op jit(solution)/shard_map/all_to_all | solution.py:236
  384.8 6.9 %all-to-all-start.1 = ((bf16[16,2,64,256]{3,2,1,0:T(8,128)(2,1)}), bf16[16,2,64,256]{3,2,1,0:T(8,128)(2,1)S(1)}, u32[]{:S(2)}, u32[]{:S(2)}) async-start(bf16[16,2,64,256]{3,2,1,0:T(8,128)(2,1)} %broadcast_select_fusion.1), calls=%async_computation.1 | async-start | bytes 2097152 | tf_op jit(solution)/shard_map/all_to_all | solution.py:237
  391.7 17.1 %fusion.2 = f32[16,2,64,1536]{3,2,0,1:T(8,128)} fusion(bf16[2,1536,1536]{2,1,0:T(8,128)(2,1)} %param.28, bf16[16,2,64,1536]{3,2,1,0:T(8,128)(2,1)} %all-to-all-done), kind=kOutput, calls=%fused_computation.7 | convolution fusion | flops 9663676416 | bytes 28311552 | tf_op jit(solution)/shard_map/necd,edf->necf/dot_general | solution.py:239
  408.8 11.3 %convert_bitcast_fusion = bf16[16,2,64,1536]{3,2,0,1:T(8,128)(2,1)} fusion(bf16[2,768,1536]{2,1,0:T(8,128)(2,1)} %param.29, f32[16,2,64,1536]{3,2,0,1:T(8,128)} %fusion.2, bf16[2,256,768,1]{2,1,3,0:T(8,128)(2,1)S(1)} %bitcast.89, bf16[16,2,64,256]{3,2,1,0:T(8,128)(2,1)S(1)} %all-to-all-done.1), kind=kOutput, calls=%fused_computation.13 | convolution fusion | flops 5646581760 | bytes 25427968 | tf_op jit(solution)/shard_map/necf,efd->necd/dot_general | solution.py:246
  420.1 6.1 %copy.103 = bf16[16,2,64,1536]{3,2,1,0:T(8,128)(2,1)} copy(bf16[16,2,64,1536]{3,2,0,1:T(8,128)(2,1)} %convert_bitcast_fusion) | data formatting | bytes 12582912 | tf_op jit(solution)/shard_map/convert_element_type | solution.py:248
  426.2 7.7 %all-to-all-start.2 = ((bf16[16,2,64,1536]{3,2,1,0:T(8,128)(2,1)}), bf16[16,2,64,1536]{3,2,1,0:T(8,128)(2,1)}, u32[]{:S(2)}, u32[]{:S(2)}) async-start(bf16[16,2,64,1536]{3,2,1,0:T(8,128)(2,1)} %copy.103), calls=%async_computation.2 | async-start | bytes 12582912 | tf_op jit(solution)/shard_map/all_to_all | solution.py:249
  434.1 87.1 %all-to-all-done.2 = bf16[16,2,64,1536]{3,2,1,0:T(8,128)(2,1)} async-done(((bf16[16,2,64,1536]{3,2,1,0:T(8,128)(2,1)}), bf16[16,2,64,1536]{3,2,1,0:T(8,128)(2,1)}, u32[]{:S(2)}, u32[]{:S(2)}) %all-to-all-start.2) | async-done | bytes 6291488 | tf_op jit(solution)/shard_map/all_to_all | solution.py:249
  521.2 14.0 %gather_fusion.2 = bf16[1536,1536]{1,0:T(8,128)(2,1)} fusion(bf16[2048,1536]{1,0:T(8,128)(2,1)} %bitcast.33, s32[2048]{0:T(1024)S(1)} %pad_clamp_fusion), kind=kCustom, calls=%fused_computation.2 | custom fusion | bytes 9443328 | tf_op jit(solution)/shard_map/gather | solution.py:251
  535.2 9.7 %reshape.176 = f32[384,4,1536]{2,1,0:T(4,128)} reshape(bf16[1536,1536]{1,0:T(8,128)(2,1)} %gather_fusion.2) | data formatting | bytes 14155776 | tf_op jit(solution)/shard_map/convert_element_type | solution.py:251
  544.9 12.3 %multiply_reduce_fusion = f32[384,1536]{1,0:T(8,128)} fusion(f32[384,4,1536]{2,1,0:T(4,128)} %reshape.176, f32[384,4]{1,0:T(8,128)S(1)} %copy.94), kind=kLoop, calls=%fused_computation.6 | loop fusion | flops 4128768 | bytes 11802624 | tf_op jit(solution)/shard_map/reduce_sum | solution.py:252
  557.2 3.0 fusion.20
  (100 shorter events, 15.8 us)
Async XLA Ops:
  6.5 48.9 %copy-start = (bf16[384,1536]{1,0:T(8,128)(2,1)S(1)}, bf16[384,1536]{1,0:T(8,128)(2,1)}, u32[]{:S(2)}) copy-start(bf16[384,1536]{1,0:T(8,128)(2,1)} %param.18) | copy-start | bytes 3538948
  6.5 48.9 %copy-start.18 = (f32[1536]{0:T(1024)S(1)}, f32[1536]{0:T(1024)}, u32[]{:S(2)}) copy-start(f32[1536]{0:T(1024)} %param.23) | copy-start | bytes 18436
  6.5 48.9 %all-gather.5.cloned.1.call-start = ((), (), s32[]{:S(2)}) async-start(), calls=%async_computation.3 | async-start | bytes 7077888 | tf_op jit(solution)/shard_map/all_gather | solution.py:197
  7.3 74.2 %all-gather.7.cloned.1.call-start = ((), (), s32[]{:S(2)}) async-start(), calls=%async_computation.4 | async-start | bytes 1179648 | tf_op jit(solution)/shard_map/all_gather | solution.py:187
  8.0 137.9 %all-gather.9.cloned.1.call-start = ((), (), s32[]{:S(2)}) async-start(), calls=%async_computation.5 | async-start | bytes 6684672 | tf_op jit(solution)/shard_map/all_gather | solution.py:204
  8.9 53.6 %copy-start.20 = (s32[16]{0:T(128)}, s32[16]{0:T(128)S(1)}, u32[]{:S(2)}) copy-start(s32[16]{0:T(128)S(1)} %reduce) | copy-start | bytes 196
  9.6 2.4 copy-start.17
  10.5 71.0 %copy-start.10 = (s32[384]{0:T(512)}, s32[384]{0:T(512)S(1)}, u32[]{:S(2)}) copy-start(s32[384]{0:T(512)S(1)} %select_reduce_fusion) | copy-start | bytes 4612
  12.1 50.5 %copy-start.16 = (f32[384]{0:T(512)}, f32[384]{0:T(512)S(1)}, u32[]{:S(2)}) copy-start(f32[384]{0:T(512)S(1)} %add_rsqrt_fusion.1) | copy-start | bytes 4612
  81.4 7.2 %copy-start.9 = (s32[384,4]{0,1:T(4,128)S(1)}, s32[384,4]{0,1:T(4,128)}, u32[]{:S(2)}) copy-start(s32[384,4]{0,1:T(4,128)} %param.21) | copy-start | bytes 18436
  85.2 3.8 copy-start.22
  86.1 152.5 %all-gather.11.cloned.1.call-start = ((), (), s32[]{:S(2)}) async-start(), calls=%async_computation.6 | async-start | bytes 5308416 | tf_op jit(solution)/shard_map/all_gather | solution.py:198
  89.2 20.1 %copy-start.21 = (s32[16]{0:T(128)S(1)}, s32[16]{0:T(128)}, u32[]{:S(2)}) copy-start(s32[16]{0:T(128)} %copy-done.20) | copy-start | bytes 196
  89.2 20.9 %copy-start.3 = (bf16[2,1536,16]{1,2,0:T(8,128)(2,1)S(1)}, bf16[2,1536,16]{1,2,0:T(8,128)(2,1)}, u32[]{:S(2)}) copy-start(bf16[2,1536,16]{1,2,0:T(8,128)(2,1)} %param.32) | copy-start | bytes 294916
  92.9 30.6 %copy-start.4 = (bf16[2,16,1536]{2,1,0:T(8,128)(2,1)S(1)}, bf16[2,16,1536]{2,1,0:T(8,128)(2,1)}, u32[]{:S(2)}) copy-start(bf16[2,16,1536]{2,1,0:T(8,128)(2,1)} %param.33) | copy-start | bytes 294916
  103.1 20.5 %copy-start.7 = (s32[1536]{0:T(1024)}, s32[1536]{0:T(1024)S(1)}, u32[]{:S(2)}) copy-start(s32[1536]{0:T(1024)S(1)} %fusion.43) | copy-start | bytes 18436
  236.7 1.9 copy-start.1
  238.6 6.3 %copy-start.2 = (bf16[2,6,384,128]{2,3,1,0:T(8,128)(2,1)}, bf16[2,6,384,128]{2,3,1,0:T(8,128)(2,1)S(1)}, u32[]{:S(2)}) copy-start(bf16[2,6,384,128]{2,3,1,0:T(8,128)(2,1)S(1)} %copy.93) | copy-start | bytes 3538948
  238.6 6.2 %copy-start.11 = (s32[384]{0:T(512)S(1)}, s32[384]{0:T(512)}, u32[]{:S(2)}) copy-start(s32[384]{0:T(512)} %copy-done.10) | copy-start | bytes 4612
  238.6 6.2 %copy-start.13 = (s32[256]{0:T(256)S(1)}, s32[256]{0:T(256)}, u32[]{:S(2)}) copy-start(s32[256]{0:T(256)} %eq.57) | copy-start | bytes 3076
  244.8 3.8 copy-start.15
  265.1 15.1 %copy-start.6 = (bf16[2,2,16,768]{3,2,1,0:T(8,128)(2,1)S(1)}, bf16[2,2,16,768]{3,2,1,0:T(8,128)(2,1)}, u32[]{:S(2)}) copy-start(bf16[2,2,16,768]{3,2,1,0:T(8,128)(2,1)} %param.35) | copy-start | bytes 294916
  265.1 15.1 %copy-start.5 = (bf16[2,1536,16]{1,2,0:T(8,128)(2,1)S(1)}, bf16[2,1536,16]{1,2,0:T(8,128)(2,1)}, u32[]{:S(2)}) copy-start(bf16[2,1536,16]{1,2,0:T(8,128)(2,1)} %param.34) | copy-start | bytes 294916
  265.1 42.4 %copy-start.12 = (s32[384]{0:T(512)S(1)}, s32[384]{0:T(512)}, u32[]{:S(2)}) copy-start(s32[384]{0:T(512)} %copy-done.10) | copy-start | bytes 4612
  265.1 42.4 %copy-start.14 = (s32[256]{0:T(256)S(1)}, s32[256]{0:T(256)}, u32[]{:S(2)}) copy-start(s32[256]{0:T(256)} %eq.57) | copy-start | bytes 3076
  265.1 119.6 %all-to-all-start = ((bf16[16,2,64,1536]{3,2,1,0:T(8,128)(2,1)}), bf16[16,2,64,1536]{3,2,1,0:T(8,128)(2,1)}, u32[]{:S(2)}, u32[]{:S(2)}) async-start(bf16[16,2,64,1536]{3,2,1,0:T(8,128)(2,1)} %broadcast_select_fusion), calls=%async_computation | async-start | bytes 12582912 | tf_op jit(solution)/shard_map/all_to_all | solution.py:236
  384.8 24.0 %all-to-all-start.1 = ((bf16[16,2,64,256]{3,2,1,0:T(8,128)(2,1)}), bf16[16,2,64,256]{3,2,1,0:T(8,128)(2,1)S(1)}, u32[]{:S(2)}, u32[]{:S(2)}) async-start(bf16[16,2,64,256]{3,2,1,0:T(8,128)(2,1)} %broadcast_select_fusion.1), calls=%async_computation.1 | async-start | bytes 2097152 | tf_op jit(solution)/shard_map/all_to_all | solution.py:237
  426.2 7.7 %copy-start.19 = (f32[384,4]{0,1:T(4,128)S(1)}, f32[384,4]{0,1:T(4,128)}, u32[]{:S(2)}) copy-start(f32[384,4]{0,1:T(4,128)} %param.22) | copy-start | bytes 18436
  426.2 7.9 %copy-start.8 = (s32[1536]{0:T(1024)S(1)}, s32[1536]{0:T(1024)}, u32[]{:S(2)}) copy-start(s32[1536]{0:T(1024)} %copy-done.7) | copy-start | bytes 18436
  426.2 95.0 %all-to-all-start.2 = ((bf16[16,2,64,1536]{3,2,1,0:T(8,128)(2,1)}), bf16[16,2,64,1536]{3,2,1,0:T(8,128)(2,1)}, u32[]{:S(2)}, u32[]{:S(2)}) async-start(bf16[16,2,64,1536]{3,2,1,0:T(8,128)(2,1)} %copy.103), calls=%async_computation.2 | async-start | bytes 12582912 | tf_op jit(solution)/shard_map/all_to_all | solution.py:249
Sparse Core Ops, SparseCore 0:
  9.0 46.4 all-gather.4
  57.2 24.1 all-gather.6
  86.2 59.6 all-gather.8
  147.4 35.6 all-gather.10

commit v2 on v1

--- a/solution.py
+++ b/solution.py
@@ -152,6 +152,19 @@
     return jnp.transpose(
         out.reshape(KVH, group_size, tok_rows, HD), (2, 0, 1, 3)
     ).reshape(tok_rows, HEADS * HD)
+
+
+def gather_factors(factors, axis_name):
+    flat = jnp.concatenate([f.reshape(-1) for f in factors])
+    gathered = lax.all_gather(flat, axis_name, axis=0, tiled=False)
+    held = []
+    offset = 0
+    for f in factors:
+        size = f.size
+        piece = gathered[:, offset : offset + size].reshape((-1,) + f.shape[1:])
+        held.append(piece)
+        offset += size
+    return tuple(held)
 
 
 def body(
@@ -182,13 +195,10 @@
     segments = segment_of(positions, lengths)
     matches = segments[:, None] == jnp.arange(segment_total, dtype=jnp.int32)[None, :]
     token_adapter = jnp.sum(jnp.where(matches, segment_adapters[0][None, :], 0), axis=1)
-    held_factors = (
-        lax.all_gather(adapter_in_down, "req", axis=0, tiled=True),
-        lax.all_gather(adapter_in_up, "req", axis=0, tiled=True),
-        lax.all_gather(adapter_out_down, "req", axis=0, tiled=True),
-        lax.all_gather(adapter_out_up, "req", axis=0, tiled=True),
-        lax.all_gather(adapter_expert_down, "req", axis=0, tiled=True),
-        lax.all_gather(adapter_expert_up, "req", axis=0, tiled=True),
+    held_factors = gather_factors(
+        (adapter_in_down, adapter_in_up, adapter_out_down, adapter_out_up,
+         adapter_expert_down, adapter_expert_up),
+        "req",
     )
     in_low, in_high, out_low, out_high, expert_low, expert_high = held_factors
     select = adapter_select(token_adapter, in_low.shape[0], in_low.shape[2])
@@ -218,23 +228,26 @@
     )
     arrival = jnp.sum((jnp.cumsum(expert_hot, axis=0) - 1) * expert_hot, axis=1)
     slot_index = picked * CAP + arrival
-    pick_ids = jnp.arange(picked.shape[0], dtype=jnp.int32)
-    sources = jnp.full((EXPERTS * CAP,), -1, jnp.int32).at[slot_index].set(pick_ids)
-    filled = (sources >= 0)[:, None]
-    token_rows = jnp.maximum(sources, 0) // top_count
+    slot_count = EXPERTS * CAP
+    slot_ids = jnp.arange(slot_count, dtype=jnp.int32)
+    token_slots = slot_index.reshape(tok_rows, top_count)
+    dispatch = jnp.any(
+        token_slots[None, :, :] == slot_ids[:, None, None], axis=2
+    ).astype(jnp.bfloat16)
     peer_count = lax.axis_size("exp")
     local_experts = EXPERTS // peer_count
-    send_rows = jnp.where(filled, normed_two[token_rows], 0).reshape(
-        peer_count, local_experts, CAP, -1
-    )
-    send_low = jnp.where(filled, low_parts[token_rows], 0).reshape(
-        peer_count, local_experts, CAP, -1
-    )
+    row_width = normed_two.shape[1]
+    send = jnp.dot(
+        dispatch,
+        jnp.concatenate([normed_two, low_parts], axis=1),
+        preferred_element_type=jnp.float32,
+    ).astype(jnp.bfloat16).reshape(peer_count, local_experts, CAP, -1)
     adapter_bank = jnp.transpose(expert_high, (1, 0, 2, 3)).reshape(
         local_experts, -1, expert_high.shape[3]
     )
-    arrived_rows = lax.all_to_all(send_rows, "exp", split_axis=0, concat_axis=0, tiled=True)
-    arrived_low = lax.all_to_all(send_low, "exp", split_axis=0, concat_axis=0, tiled=True)
+    arrived = lax.all_to_all(send, "exp", split_axis=0, concat_axis=0, tiled=True)
+    arrived_rows = arrived[..., :row_width]
+    arrived_low = arrived[..., row_width:]
     hidden_width = expert_down.shape[1]
     gate_up = jnp.einsum(
         "necd,edf->necf", arrived_rows, expert_gate_up, preferred_element_type=jnp.float32
@@ -248,8 +261,17 @@
     ).astype(jnp.bfloat16)
     returned = lax.all_to_all(outputs, "exp", split_axis=0, concat_axis=0, tiled=True)
     flat_back = returned.reshape(EXPERTS * CAP, -1)
-    per_pick = flat_back[slot_index].astype(jnp.float32).reshape(tok_rows, top_count, -1)
-    combined = jnp.sum(gate_weights[:, :, None] * per_pick, axis=1)
+    gate_grid = jnp.sum(
+        jnp.where(
+            token_slots[:, :, None] == slot_ids[None, None, :], gate_weights[:, :, None], 0.0
+        ),
+        axis=1,
+    )
+    gate_high = gate_grid.astype(jnp.bfloat16)
+    gate_low = (gate_grid - gate_high.astype(jnp.float32)).astype(jnp.bfloat16)
+    combined = jnp.dot(gate_high, flat_back, preferred_element_type=jnp.float32) + jnp.dot(
+        gate_low, flat_back, preferred_element_type=jnp.float32
+    )
     return (residual.astype(jnp.float32) + combined).astype(jnp.bfloat16)
 
 

time: 575 us -> 572 us (level)
  blocking collectives: 70.5 us -> 0 us
  waiting for transfers between devices: 210 us -> 268 us
  matrix products: 49.8 us -> 69.9 us
  other arithmetic: 35.5 us -> 19.7 us
  local copies, waits for them, and re-layouts: 67.2 us -> 81.1 us
  starting transfers between devices: 29.8 us -> 23 us
    all_gather x5 -> x0, blocking collectives: 70.5 us -> none  [the longest x1 14.9 us: body(): lax.all_gather(adapter_in_down, 'req', axis=0, tiled=True)]
    all_to_all x2 -> x1, waiting for transfers between devices: 68 us -> 126 us  [body(): lax.all_to_all(send, 'exp', split_axis=0, concat_axis=0, tiled=True)]
    gather x3 -> x0, local copies, waits for them, and re-layouts: 31.6 us -> none  [the longest x1 14 us: body(): flat_back[slot_index].astype(jnp.float32).reshape(tok_rows, top_count, -1)]
    reshape x0 -> x9, local copies, waits for them, and re-layouts: none -> 25.2 us  [the longest x4 23.5 us: gather_factors(): piece = gathered[:, offset:offset + size].reshape((-1,) + f.shape[1:])]
    dot_general x0 -> x3, matrix products: none -> 18.8 us  [the longest x1 6.49 us: body(): jnp.dot(gate_low, flat_back, preferred_element_type=jnp.float32)]
    transpose x0 -> x4, local copies, waits for them, and re-layouts: none -> 17.4 us  [the longest x3 17.3 us: low_coords(): jnp.transpose(first_factor, (1, 0, 2))]
    all_gather x1, waiting for transfers between devices: 18.8 us -> 34.3 us  [gather_factors(): gathered = lax.all_gather(flat, axis_name, axis=0, tiled=False)]
    convert_element_type x1 -> x0, local copies, waits for them, and re-layouts: 9.74 us -> none  [body(): flat_back[slot_index].astype(jnp.float32).reshape(tok_rows, top_count, -1)]
  transfers between devices with their start and end apart: 7 -> 6, of which waited for: 5 -> 5; matrix products, arithmetic and copies ran while one was open for 11% -> 15% of each run, Pallas kernels for 16% -> 16%
where the time goes in v2:
time: 572 us; the launch traced here: 566 us
  waiting for transfers between devices  268 us (47%)
  Pallas kernels  91 us (16%)
  local copies, waits for them, and re-layouts  81.1 us (14%)
  matrix products  69.9 us (12%)
  starting transfers between devices  23 us (4%)
  other arithmetic  19.7 us (3%)
  between operations  13.8 us (2%)
    all_to_all x1, waiting for transfers between devices, body(): lax.all_to_all(send, 'exp', split_axis=0, concat_axis=0, tiled=True)  126 us
    pallas_call x1, Pallas kernels, window_attention(): pl.pallas_call(attention_kernel, grid_spec=grid_spec, out_shape=jax.Shape...  91 us
    all_to_all x1, waiting for transfers between devices, body(): lax.all_to_all(outputs, 'exp', split_axis=0, concat_axis=0, tiled=True)  79.5 us
    all_gather x1, waiting for transfers between devices, gather_factors(): gathered = lax.all_gather(flat, axis_name, axis=0, tiled=False)  34.3 us
    reshape x4, local copies, waits for them, and re-layouts, gather_factors(): piece = gathered[:, offset:offset + size].reshape((-1,) + f.shape[1:])  23.5 us
    all_gather x1, waiting for transfers between devices, body(): lax.all_gather(attention_in, 'req', axis=1, tiled=True)  21.3 us
    transpose x3, local copies, waits for them, and re-layouts, low_coords(): jnp.transpose(first_factor, (1, 0, 2))  17.3 us
    dot_general x1, matrix products, body(): jnp.einsum('necd,edf->necf', arrived_rows, expert_gate_up, preferred_elem...  17 us
  transfers between devices with their start and end apart: 6, of which 5 were waited for; matrix products, arithmetic and copies ran while one was open for 15% of the time, Pallas kernels for 16%

profile of v2, /device:TPU:100, one launch (start us, length us, event | category | flops | bytes accessed | tf_op | source)
XLA Modules:
  0.0 566.3 jit_solution(15302988924597842140)
XLA Ops:
  15.7 34.3 %all-gather.12.cloned.1.call-done = bf16[2490368]{0:T(1024)(128)(2,1)} async-done(((bf16[311296]{0:T(1024)(128)(2,1)}), bf16[2490368]{0:T(1024)(128)(2,1)}) %all-gather.12.cloned.1.call-update) | async-done | bytes 4980752 | tf_op jit(solution)/shard_map/all_gather | solution.py:159
  50.0 6.7 %reshape.178 = bf16[8,311296]{1,0:T(8,128)(2,1)} reshape(bf16[2490368]{0:T(1024)(128)(2,1)} %all-gather.12.cloned.1.call-done) | data formatting | bytes 9961472 | tf_op jit(solution)/shard_map/all_gather | solution.py:159
  56.7 3.8 fusion.52
  60.5 7.7 %reshape.162 = bf16[16,1536,16]{2,1,0:T(8,128)(2,1)} reshape(bf16[8,49152]{1,0:T(8,128)(2,1)S(1)} %get-tuple-element.9) | data formatting | bytes 1572864 | tf_op jit(solution)/shard_map/reshape | solution.py:164
  68.2 5.2 copy.122
  74.9 21.3 %all-gather.6.cloned.1.call-done = bf16[1536,2048]{1,0:T(8,128)(2,1)} async-done(((bf16[1536,256]{1,0:T(8,128)(2,1)}), bf16[1536,2048]{1,0:T(8,128)(2,1)}) %all-gather.6.cloned.1.call-update) | async-done | bytes 6291472 | tf_op jit(solution)/shard_map/all_gather | solution.py:207
  96.1 7.1 %fusion.37 = f32[384,2048]{1,0:T(8,128)} fusion(bf16[1536,2048]{1,0:T(8,128)(2,1)} %all-gather.6.cloned.1.call-done, bf16[384,1536]{1,0:T(8,128)(2,1)S(1)} %copy-done, f32[1536]{0:T(1024)S(1)} %copy-done.18, f32[384]{0:T(512)S(1)} %add_rsqrt_fusion.1), kind=kOutput, calls=%fused_computation.52 | convolution fusion | flops 2418278400 | bytes 10624512 | tf_op jit(solution)/shard_map/dot_general | solution.py:210
  103.3 3.8 add_convert_fusion
  111.7 3.6 broadcast_in_dim.73.init_ref
  115.4 9.1 %reduce-window.19 = s32[32,12,128]{2,1,0:T(8,128)S(1)} reduce-window(s32[32,12,128]{2,1,0:T(8,128)S(1)} %fusion.39, s32[]{:T(128)} %constant.29.clone.1), window={size=1x1x128 pad=0_0x0_0x127_0}, to_apply=%region_5.6 | reduce-window | flops 6242304 | bytes 393220 | tf_op jit(solution)/shard_map/reduce-window.1
  126.2 4.9 fusion
  131.1 7.7 %reshape.169 = bf16[16,1536,16]{2,1,0:T(8,128)(2,1)} reshape(bf16[8,49152]{1,0:T(8,128)(2,1)S(1)} %copy-done.4) | data formatting | bytes 1572864 | tf_op jit(solution)/shard_map/reshape | solution.py:164
  138.8 5.9 %copy.128 = bf16[1536,16,16]{0,2,1:T(8,128)(2,1)S(1)} copy(bf16[1536,16,16]{2,0,1:T(8,128)(2,1)} %bitcast.78) | data formatting | bytes 1572864 | tf_op jit(solution)/shard_map/transpose | solution.py:38
  144.7 2.4 reshape_reshape.7
  147.1 7.7 %reshape.172 = bf16[16,1536,16]{2,1,0:T(8,128)(2,1)} reshape(bf16[8,49152]{1,0:T(8,128)(2,1)S(1)} %copy-done.3) | data formatting | bytes 1572864 | tf_op jit(solution)/shard_map/reshape | solution.py:164
  154.8 6.3 %copy.134 = bf16[1536,16,16]{0,2,1:T(8,128)(2,1)} copy(bf16[1536,16,16]{2,0,1:T(8,128)(2,1)} %bitcast.79) | data formatting | bytes 1572864 | tf_op jit(solution)/shard_map/transpose | solution.py:38
  163.3 5.2 all-gather.8.cloned.1.call-done.k_ref.v_ref
  168.6 91.0 %shard_map.172 = bf16[2,2304,128]{2,1,0:T(8,128)(2,1)} custom-call(s32[1]{0:T(128)} %slice.45.first_ref, bf16[2,2304,128]{2,1,0:T(8,128)(2,1)} %bitcast.84, bf16[6144,512]{1,0:T(8,128)(2,1)} %all-gather.8.cloned.1.call-done.k_ref.v_ref, bf16[6144,512]{1,0:T(8,128)(2,1)} %all-gather.8.cloned.1.call-done.k_ref.v_ref, s32[384,1]{1,0:T(8,128)} %broadcast_in_dim.72.qseg_ref, ...), custom_call_target="tpu_custom_call" | custom-call | tf_op jit(solution)/shard_map/pallas_call | solution.py:146
  259.6 1.9 copy.127
  261.5 5.8 %convert_add_fusion.1 = f32[384,1536]{1,0:T(8,128)} fusion(bf16[384,1536]{1,0:T(8,128)(2,1)S(1)} %copy-done.1, bf16[384,1536]{0,1:T(8,128)(2,1)S(1)} %bitcast.82, bf16[1536,1536]{0,1:T(8,128)(2,1)} %all-gather.10.cloned.1.call-done), kind=kOutput, calls=%fused_computation.18 | convolution fusion | flops 1813118976 | bytes 9437184 | tf_op jit(solution)/shard_map/dot_general | solution.py:218
  267.3 3.4 fusion.19
  272.8 5.9 %convolution_convert_fusion = bf16[2048,1792]{1,0:T(8,128)(2,1)} fusion(pred[2048,384]{1,0:T(8,128)(4,1)S(1)} %copy-done.7, bf16[384,256]{1,0:T(8,128)(2,1)S(1)} %fusion.27, bf16[384,1536]{1,0:T(8,128)(2,1)S(1)} %fusion.21), kind=kOutput, calls=%fused_computation.6 | convolution fusion | flops 2824994816 | bytes 9502720 | tf_op jit(solution)/shard_map/dot_general | solution.py:240
  278.7 15.4 %all-to-all-start = ((bf16[16,2,64,1792]{3,2,1,0:T(8,128)(2,1)}), bf16[16,2,64,1792]{3,2,1,0:T(8,128)(2,1)}, u32[]{:S(2)}, u32[]{:S(2)}) async-start(bf16[16,2,64,1792]{3,2,1,0:T(8,128)(2,1)} %bitcast.80), calls=%async_computation | async-start | bytes 14680064 | tf_op jit(solution)/shard_map/all_to_all | solution.py:248
  294.6 126.5 %all-to-all-done = bf16[16,2,64,1792]{3,2,1,0:T(8,128)(2,1)} async-done(((bf16[16,2,64,1792]{3,2,1,0:T(8,128)(2,1)}), bf16[16,2,64,1792]{3,2,1,0:T(8,128)(2,1)}, u32[]{:S(2)}, u32[]{:S(2)}) %all-to-all-start) | async-done | bytes 7340064 | tf_op jit(solution)/shard_map/all_to_all | solution.py:248
  421.1 17.0 %fusion.3 = f32[16,2,64,1536]{3,2,0,1:T(8,128)} fusion(bf16[2,1536,1536]{2,1,0:T(8,128)(2,1)} %param.28, bf16[16,2,64,1792]{3,2,1,0:T(8,128)(2,1)} %all-to-all-done), kind=kOutput, calls=%fused_computation.7 | convolution fusion | flops 9663676416 | bytes 28311552 | tf_op jit(solution)/shard_map/necd,edf->necf/dot_general | solution.py:252
  438.0 12.3 %convert_bitcast_fusion = bf16[16,2,64,1536]{3,2,0,1:T(8,128)(2,1)} fusion(bf16[2,768,1536]{2,1,0:T(8,128)(2,1)} %param.29, f32[16,2,64,1536]{3,2,0,1:T(8,128)} %fusion.3, bf16[2,256,768,1]{2,1,3,0:T(8,128)(2,1)S(1)} %bitcast.91, bf16[16,2,64,1792]{3,2,1,0:T(8,128)(2,1)} %all-to-all-done), kind=kOutput, calls=%fused_computation.13 | convolution fusion | flops 5646581760 | bytes 25427968 | tf_op jit(solution)/shard_map/necf,efd->necd/dot_general | solution.py:259
  450.3 6.1 %copy.139 = bf16[16,2,64,1536]{3,2,1,0:T(8,128)(2,1)} copy(bf16[16,2,64,1536]{3,2,0,1:T(8,128)(2,1)} %convert_bitcast_fusion) | data formatting | bytes 12582912 | tf_op jit(solution)/shard_map/convert_element_type | solution.py:261
  456.4 7.1 %all-to-all-start.1 = ((bf16[16,2,64,1536]{3,2,1,0:T(8,128)(2,1)}), bf16[16,2,64,1536]{3,2,1,0:T(8,128)(2,1)}, u32[]{:S(2)}, u32[]{:S(2)}) async-start(bf16[16,2,64,1536]{3,2,1,0:T(8,128)(2,1)} %copy.139), calls=%async_computation.1 | async-start | bytes 12582912 | tf_op jit(solution)/shard_map/all_to_all | solution.py:262
  463.5 3.7 select_reduce_fusion
  467.2 79.5 %all-to-all-done.1 = bf16[16,2,64,1536]{3,2,1,0:T(8,128)(2,1)} async-done(((bf16[16,2,64,1536]{3,2,1,0:T(8,128)(2,1)}), bf16[16,2,64,1536]{3,2,1,0:T(8,128)(2,1)}, u32[]{:S(2)}, u32[]{:S(2)}) %all-to-all-start.1) | async-done | bytes 6291488 | tf_op jit(solution)/shard_map/all_to_all | solution.py:262
  546.7 6.3 %fusion.31 = f32[384,1536]{1,0:T(8,128)S(1)} fusion(bf16[2048,1536]{1,0:T(8,128)(2,1)} %bitcast.30, f32[384,2048]{1,0:T(8,128)} %select_reduce_fusion), kind=kOutput, calls=%fused_computation.46 | convolution fusion | flops 2416705536 | bytes 11796480 | tf_op jit(solution)/shard_map/dot_general | solution.py:272
  553.1 6.5 %fusion.13 = bf16[384,1536]{1,0:T(8,128)(2,1)} fusion(f32[384,1536]{1,0:T(8,128)S(1)} %fusion.31, bf16[2048,1536]{1,0:T(8,128)(2,1)} %bitcast.30, bf16[384,1536]{1,0:T(8,128)(2,1)S(1)} %get-tuple-element.11, f32[384,2048]{1,0:T(8,128)S(1)} %copy-done.2), kind=kOutput, calls=%fused_computation.27 | convolution fusion | flops 2421424128 | bytes 14155776 | tf_op jit(solution)/shard_map/dot_general | solution.py:272
  (112 shorter events, 21.4 us)
Async XLA Ops:
  6.5 4.6 copy-start.9
  6.5 4.8 copy-start.8
  6.5 43.5 %all-gather.12.cloned.1.call-start = ((), (), s32[]{:S(2)}) async-start(), calls=%async_computation.5 | async-start | bytes 5603328 | tf_op jit(solution)/shard_map/all_gather | solution.py:159
  7.9 4.3 copy-start.10
  10.6 3.6 copy-start.22
  10.6 3.9 copy-start
  11.3 4.3 copy-start.23
  12.4 0.8 copy-start.6
  13.3 82.9 %all-gather.6.cloned.1.call-start = ((), (), s32[]{:S(2)}) async-start(), calls=%async_computation.2 | async-start | bytes 7077888 | tf_op jit(solution)/shard_map/all_gather | solution.py:207
  14.0 154.6 %all-gather.8.cloned.1.call-start = ((), (), s32[]{:S(2)}) async-start(), calls=%async_computation.3 | async-start | bytes 6684672 | tf_op jit(solution)/shard_map/all_gather | solution.py:214
  14.5 42.2 %copy-start.20 = (s32[16]{0:T(128)}, s32[16]{0:T(128)S(1)}, u32[]{:S(2)}) copy-start(s32[16]{0:T(128)S(1)} %reduce) | copy-start | bytes 196
  14.5 42.2 %copy-start.17 = (s32[384]{0:T(512)}, s32[384]{0:T(512)S(1)}, u32[]{:S(2)}) copy-start(s32[384]{0:T(512)S(1)} %iota_add_fusion) | copy-start | bytes 4612
  14.8 81.3 %copy-start.16 = (f32[384]{0:T(512)}, f32[384]{0:T(512)S(1)}, u32[]{:S(2)}) copy-start(f32[384]{0:T(512)S(1)} %add_rsqrt_fusion.1) | copy-start | bytes 4612
  15.7 87.6 %copy-start.12 = (s32[384]{0:T(512)}, s32[384]{0:T(512)S(1)}, u32[]{:S(2)}) copy-start(s32[384]{0:T(512)S(1)} %select_reduce_fusion.1) | copy-start | bytes 4612
  68.2 5.2 slice-start
  68.2 27.9 %copy-start.18 = (f32[1536]{0:T(1024)S(1)}, f32[1536]{0:T(1024)}, u32[]{:S(2)}) copy-start(f32[1536]{0:T(1024)} %param.23) | copy-start | bytes 18436
  103.3 7.2 %copy-start.11 = (s32[384,4]{0,1:T(4,128)S(1)}, s32[384,4]{0,1:T(4,128)}, u32[]{:S(2)}) copy-start(s32[384,4]{0,1:T(4,128)} %param.21) | copy-start | bytes 18436
  107.9 153.6 %all-gather.10.cloned.1.call-start = ((), (), s32[]{:S(2)}) async-start(), calls=%async_computation.4 | async-start | bytes 5308416 | tf_op jit(solution)/shard_map/all_gather | solution.py:208
  110.8 14.7 %copy-start.21 = (s32[16]{0:T(128)S(1)}, s32[16]{0:T(128)}, u32[]{:S(2)}) copy-start(s32[16]{0:T(128)} %copy-done.20) | copy-start | bytes 196
  111.7 19.4 %copy-start.4 = (bf16[8,49152]{1,0:T(8,128)(2,1)S(1)}, bf16[8,49152]{1,0:T(8,128)(2,1)}, u32[]{:S(2)}) copy-start(bf16[8,49152]{1,0:T(8,128)(2,1)} %get-tuple-element.8) | copy-start | bytes 2359300
  138.8 8.3 %copy-start.3 = (bf16[8,49152]{1,0:T(8,128)(2,1)S(1)}, bf16[8,49152]{1,0:T(8,128)(2,1)}, u32[]{:S(2)}) copy-start(bf16[8,49152]{1,0:T(8,128)(2,1)} %get-tuple-element.6) | copy-start | bytes 2359300
  168.6 92.9 %copy-start.1 = (bf16[384,1536]{1,0:T(8,128)(2,1)S(1)}, bf16[384,1536]{1,0:T(8,128)(2,1)}, u32[]{:S(2)}) copy-start(bf16[384,1536]{1,0:T(8,128)(2,1)} %param.18) | copy-start | bytes 3538948
  261.5 5.8 %copy-start.13 = (s32[384]{0:T(512)S(1)}, s32[384]{0:T(512)}, u32[]{:S(2)}) copy-start(s32[384]{0:T(512)} %copy-done.12) | copy-start | bytes 4612
  261.5 5.8 %copy-start.14 = (s32[256]{0:T(256)S(1)}, s32[256]{0:T(256)}, u32[]{:S(2)}) copy-start(s32[256]{0:T(256)} %eq.83) | copy-start | bytes 3076
  267.3 3.5 copy-start.15
  270.8 2.0 copy-start.7
  278.7 15.4 %copy-start.5 = (bf16[8,49152]{1,0:T(8,128)(2,1)S(1)}, bf16[8,49152]{1,0:T(8,128)(2,1)}, u32[]{:S(2)}) copy-start(bf16[8,49152]{1,0:T(8,128)(2,1)} %get-tuple-element.5) | copy-start | bytes 2359300
  278.7 142.3 %all-to-all-start = ((bf16[16,2,64,1792]{3,2,1,0:T(8,128)(2,1)}), bf16[16,2,64,1792]{3,2,1,0:T(8,128)(2,1)}, u32[]{:S(2)}, u32[]{:S(2)}) async-start(bf16[16,2,64,1792]{3,2,1,0:T(8,128)(2,1)} %bitcast.80), calls=%async_computation | async-start | bytes 14680064 | tf_op jit(solution)/shard_map/all_to_all | solution.py:248
  456.4 7.1 %copy-start.19 = (f32[384,4]{0,1:T(4,128)S(1)}, f32[384,4]{0,1:T(4,128)}, u32[]{:S(2)}) copy-start(f32[384,4]{0,1:T(4,128)} %param.22) | copy-start | bytes 18436
  456.4 90.3 %all-to-all-start.1 = ((bf16[16,2,64,1536]{3,2,1,0:T(8,128)(2,1)}), bf16[16,2,64,1536]{3,2,1,0:T(8,128)(2,1)}, u32[]{:S(2)}, u32[]{:S(2)}) async-start(bf16[16,2,64,1536]{3,2,1,0:T(8,128)(2,1)} %copy.139), calls=%async_computation.1 | async-start | bytes 12582912 | tf_op jit(solution)/shard_map/all_to_all | solution.py:262
  546.7 6.3 %copy-start.2 = (f32[384,2048]{1,0:T(8,128)S(1)}, f32[384,2048]{1,0:T(8,128)}, u32[]{:S(2)}) copy-start(f32[384,2048]{1,0:T(8,128)} %select_reduce_fusion) | copy-start | bytes 9437188
Sparse Core Ops, SparseCore 0:
  13.4 36.5 all-gather.11
  51.7 44.3 all-gather.5
  108.0 60.4 all-gather.7
  170.1 35.6 all-gather.9

commit v3 on v2

--- a/solution.py
+++ b/solution.py
@@ -33,21 +33,14 @@
     return token_adapter[:, None] == owners[None, :]
 
 
-def low_coords(inputs, select, first_factor):
-    adapter_count, inner_width, rank_size = first_factor.shape
-    joined = jnp.transpose(first_factor, (1, 0, 2)).reshape(inner_width, adapter_count * rank_size)
+def low_coords(inputs, select, joined):
     coords = jnp.dot(inputs, joined, preferred_element_type=jnp.float32)
     return jnp.where(select, coords, 0.0).astype(jnp.bfloat16)
 
 
-def low_rank(inputs, select, first_factor, second_factor):
-    coords = low_coords(inputs, select, first_factor)
-    adapter_count, rank_size, outer_width = second_factor.shape
-    return jnp.dot(
-        coords,
-        second_factor.reshape(adapter_count * rank_size, outer_width),
-        preferred_element_type=jnp.float32,
-    )
+def low_rank(inputs, select, joined, second):
+    coords = low_coords(inputs, select, joined)
+    return jnp.dot(coords, second, preferred_element_type=jnp.float32)
 
 
 KEY_BLOCK = 512
@@ -154,17 +147,35 @@
     ).reshape(tok_rows, HEADS * HD)
 
 
-def gather_factors(factors, axis_name):
-    flat = jnp.concatenate([f.reshape(-1) for f in factors])
-    gathered = lax.all_gather(flat, axis_name, axis=0, tiled=False)
-    held = []
+def gather_weights(attention_in, downs, ups, expert_up, axis_name):
+    inner_width = attention_in.shape[0]
+    in_width = attention_in.shape[1]
+    down_cols = [jnp.transpose(f, (1, 0, 2)).reshape(inner_width, -1) for f in downs]
+    local_adapters, local_experts, rank_size, hidden_width = expert_up.shape
+    up_rows = [f.reshape(-1, f.shape[2]) for f in ups] + [
+        jnp.transpose(expert_up, (0, 2, 1, 3)).reshape(local_adapters * rank_size, -1)
+    ]
+    wide = lax.all_gather(
+        jnp.concatenate([attention_in] + down_cols, axis=1), axis_name, axis=1, tiled=True
+    )
+    peers = wide.shape[1] // (in_width + sum(c.shape[1] for c in down_cols))
+    wide = wide.reshape(inner_width, peers, -1)
+    full_in = wide[:, :, :in_width].reshape(inner_width, -1)
+    joined = []
+    offset = in_width
+    for c in down_cols:
+        joined.append(wide[:, :, offset : offset + c.shape[1]].reshape(inner_width, -1))
+        offset += c.shape[1]
+    tall = lax.all_gather(jnp.concatenate(up_rows, axis=1), axis_name, axis=0, tiled=True)
+    seconds = []
     offset = 0
-    for f in factors:
-        size = f.size
-        piece = gathered[:, offset : offset + size].reshape((-1,) + f.shape[1:])
-        held.append(piece)
-        offset += size
-    return tuple(held)
+    for r in up_rows:
+        seconds.append(tall[:, offset : offset + r.shape[1]])
+        offset += r.shape[1]
+    bank = jnp.transpose(
+        seconds[-1].reshape(tall.shape[0], local_experts, hidden_width), (1, 0, 2)
+    )
+    return full_in, joined, seconds[:-1], bank
 
 
 def body(
@@ -195,18 +206,20 @@
     segments = segment_of(positions, lengths)
     matches = segments[:, None] == jnp.arange(segment_total, dtype=jnp.int32)[None, :]
     token_adapter = jnp.sum(jnp.where(matches, segment_adapters[0][None, :], 0), axis=1)
-    held_factors = gather_factors(
-        (adapter_in_down, adapter_in_up, adapter_out_down, adapter_out_up,
-         adapter_expert_down, adapter_expert_up),
+    adapter_count = adapter_in_down.shape[0] * lax.axis_size("req")
+    rank_size = adapter_in_down.shape[2]
+    select = adapter_select(token_adapter, adapter_count, rank_size)
+    normed = scaled_norm(tokens, attention_gain)
+    full_in, joined, seconds, adapter_bank = gather_weights(
+        attention_in,
+        (adapter_in_down, adapter_out_down, adapter_expert_down),
+        (adapter_in_up, adapter_out_up),
+        adapter_expert_up,
         "req",
     )
-    in_low, in_high, out_low, out_high, expert_low, expert_high = held_factors
-    select = adapter_select(token_adapter, in_low.shape[0], in_low.shape[2])
-    normed = scaled_norm(tokens, attention_gain)
-    full_in, full_out = (
-        lax.all_gather(attention_in, "req", axis=1, tiled=True),
-        lax.all_gather(attention_out, "req", axis=1, tiled=True),
-    )
+    in_low, out_low, expert_low = joined
+    in_high, out_high = seconds
+    full_out = lax.all_gather(attention_out, "req", axis=1, tiled=True)
     base_heads = jnp.dot(normed, full_in, preferred_element_type=jnp.float32)
     projected = (base_heads + low_rank(normed, select, in_low, in_high)).astype(jnp.bfloat16)
     group_size = HEADS // KVH
@@ -242,9 +255,6 @@
         jnp.concatenate([normed_two, low_parts], axis=1),
         preferred_element_type=jnp.float32,
     ).astype(jnp.bfloat16).reshape(peer_count, local_experts, CAP, -1)
-    adapter_bank = jnp.transpose(expert_high, (1, 0, 2, 3)).reshape(
-        local_experts, -1, expert_high.shape[3]
-    )
     arrived = lax.all_to_all(send, "exp", split_axis=0, concat_axis=0, tiled=True)
     arrived_rows = arrived[..., :row_width]
     arrived_low = arrived[..., row_width:]

time: 572 us -> 554 us (0.969)
  local copies, waits for them, and re-layouts: 81.1 us -> 28.7 us
  waiting for transfers between devices: 268 us -> 308 us
    all_gather x1, waiting for transfers between devices: 5.23 us -> 35.2 us  [body(): key_piece = lax.all_gather(key_value, 'exp', axis=0, tiled=True)]
    reshape x9 -> x1, local copies, waits for them, and re-layouts: 25.2 us -> 0.27 us  [gather_weights(): seconds[-1].reshape(tall.shape[0], local_experts, hidden_width)]
    transpose x4 -> x1, local copies, waits for them, and re-layouts: 17.4 us -> 0.08 us  [gather_weights(): jnp.transpose(expert_up, (0, 2, 1, 3))]
    all_gather x3, waiting for transfers between devices: 55.6 us -> 66.4 us  [the longest x1 49.2 us: gather_weights(): lax.all_gather(jnp.concatenate([attention_in] + down_cols, axis=1), axis_...]
    all_gather x1 -> x0, local copies, waits for them, and re-layouts: 6.69 us -> none  [gather_factors(): gathered = lax.all_gather(flat, axis_name, axis=0, tiled=False)]
  transfers between devices with their start and end apart: 6 -> 6, of which waited for: 5 -> 5; matrix products, arithmetic and copies ran while one was open for 15% -> 8% of each run, Pallas kernels for 16% -> 16%
where the time goes in v3:
time: 554 us; the launch traced here: 553 us
  waiting for transfers between devices  308 us (56%)
  Pallas kernels  91 us (16%)
  matrix products  66.2 us (12%)
  local copies, waits for them, and re-layouts  28.7 us (5%)
  other arithmetic  22.8 us (4%)
  starting transfers between devices  22.3 us (4%)
  between operations  13.5 us (2%)
    all_to_all x1, waiting for transfers between devices, body(): lax.all_to_all(send, 'exp', split_axis=0, concat_axis=0, tiled=True)  127 us
    pallas_call x1, Pallas kernels, window_attention(): pl.pallas_call(attention_kernel, grid_spec=grid_spec, out_shape=jax.Shape...  91 us
    all_to_all x1, waiting for transfers between devices, body(): lax.all_to_all(outputs, 'exp', split_axis=0, concat_axis=0, tiled=True)  79.4 us
    all_gather x1, waiting for transfers between devices, gather_weights(): lax.all_gather(jnp.concatenate([attention_in] + down_cols, axis=1), axis_...  49.2 us
    all_gather x1, waiting for transfers between devices, body(): key_piece = lax.all_gather(key_value, 'exp', axis=0, tiled=True)  35.2 us
    all_gather x1, waiting for transfers between devices, gather_weights(): lax.all_gather(jnp.concatenate(up_rows, axis=1), axis_name, axis=0, tiled...  17.1 us
    dot_general x1, matrix products, body(): jnp.einsum('necd,edf->necf', arrived_rows, expert_gate_up, preferred_elem...  17 us
    all_to_all x1, starting transfers between devices, body(): lax.all_to_all(send, 'exp', split_axis=0, concat_axis=0, tiled=True)  15.1 us
  transfers between devices with their start and end apart: 6, of which 5 were waited for; matrix products, arithmetic and copies ran while one was open for 8% of the time, Pallas kernels for 16%

profile of v3, /device:TPU:100, one launch (start us, length us, event | category | flops | bytes accessed | tf_op | source)
XLA Modules:
  0.0 552.9 jit_solution(6356030264322352028)
XLA Ops:
  6.5 1.5 copy.130
  8.0 2.1 pad_maximum_fusion
  13.1 49.2 %all-gather.5.cloned.1.call-done = bf16[1536,2816]{0,1:T(8,128)(2,1)} async-done(((bf16[1536,352]{0,1:T(8,128)(2,1)}), bf16[1536,2816]{0,1:T(8,128)(2,1)}) %all-gather.5.cloned.1.call-update) | async-done | bytes 8650768 | tf_op jit(solution)/shard_map/all_gather | solution.py:158
  62.4 3.5 slice.64
  65.9 3.0 fusion.56
  68.8 4.3 fusion.41
  73.1 17.1 %all-gather.7.cloned.1.call-done = bf16[256,5120]{1,0:T(8,128)(2,1)} async-done(((bf16[32,5120]{1,0:T(8,128)(2,1)}), bf16[256,5120]{1,0:T(8,128)(2,1)}) %all-gather.7.cloned.1.call-update) | async-done | bytes 2621456 | tf_op jit(solution)/shard_map/all_gather | solution.py:169
  90.3 4.1 add_convert_fusion
  94.3 0.8 slice.68
  95.7 0.8 broadcast_in_dim.72.qseg_ref
  96.5 1.2 slice.48.first_ref
  98.4 3.7 broadcast_in_dim.73.init_ref
  102.1 9.3 %reduce-window.19 = s32[32,12,128]{2,1,0:T(8,128)S(1)} reduce-window(s32[32,12,128]{2,1,0:T(8,128)S(1)} %fusion.43, s32[]{:T(128)} %constant.29.clone.1), window={size=1x1x128 pad=0_0x0_0x127_0}, to_apply=%region_5.6 | reduce-window | flops 6242304 | bytes 393220 | tf_op jit(solution)/shard_map/reduce-window.1
  112.3 0.8 convert_reduce_fusion
  113.1 4.9 fusion
  118.8 1.4 copy.134
  120.3 35.2 %all-gather.9.cloned.1.call-done.k_ref.v_ref = bf16[6144,512]{1,0:T(8,128)(2,1)} async-done(((bf16[384,512]{1,0:T(8,128)(2,1)}), bf16[6144,512]{1,0:T(8,128)(2,1)}) %all-gather.9.cloned.1.call-update) | async-done | bytes 6291472 | tf_op jit(solution)/shard_map/all_gather | solution.py:227
  155.5 91.0 %shard_map.172 = bf16[2,2304,128]{2,1,0:T(8,128)(2,1)} custom-call(s32[1]{0:T(128)} %slice.48.first_ref, bf16[2,2304,128]{2,1,0:T(8,128)(2,1)} %bitcast.94, bf16[6144,512]{1,0:T(8,128)(2,1)} %all-gather.9.cloned.1.call-done.k_ref.v_ref, bf16[6144,512]{1,0:T(8,128)(2,1)} %all-gather.9.cloned.1.call-done.k_ref.v_ref, s32[384,1]{1,0:T(8,128)} %broadcast_in_dim.72.qseg_ref, ...), custom_call_target="tpu_custom_call" | custom-call | tf_op jit(solution)/shard_map/pallas_call | solution.py:139
  246.5 2.0 copy.137
  248.5 5.8 %convert_add_fusion.1 = f32[384,1536]{1,0:T(8,128)} fusion(bf16[384,1536]{1,0:T(8,128)(2,1)S(1)} %copy-done.1, bf16[384,1536]{0,1:T(8,128)(2,1)S(1)} %bitcast.92, bf16[1536,1536]{0,1:T(8,128)(2,1)} %all-gather.11.cloned.1.call-done), kind=kOutput, calls=%fused_computation.18 | convolution fusion | flops 1813118976 | bytes 9437184 | tf_op jit(solution)/shard_map/dot_general | solution.py:231
  254.3 3.4 fusion.19
  259.4 6.0 %convolution_convert_fusion = bf16[2048,1792]{1,0:T(8,128)(2,1)} fusion(pred[2048,384]{1,0:T(8,128)(4,1)S(1)} %copy-done.4, bf16[384,256]{1,0:T(8,128)(2,1)S(1)} %fusion.27, bf16[384,1536]{1,0:T(8,128)(2,1)S(1)} %fusion.21), kind=kOutput, calls=%fused_computation.6 | convolution fusion | flops 2824994816 | bytes 9502720 | tf_op jit(solution)/shard_map/dot_general | solution.py:253
  265.4 15.1 %all-to-all-start = ((bf16[16,2,64,1792]{3,2,1,0:T(8,128)(2,1)}), bf16[16,2,64,1792]{3,2,1,0:T(8,128)(2,1)}, u32[]{:S(2)}, u32[]{:S(2)}) async-start(bf16[16,2,64,1792]{3,2,1,0:T(8,128)(2,1)} %bitcast.89), calls=%async_computation | async-start | bytes 14680064 | tf_op jit(solution)/shard_map/all_to_all | solution.py:258
  281.0 126.9 %all-to-all-done = bf16[16,2,64,1792]{3,2,1,0:T(8,128)(2,1)} async-done(((bf16[16,2,64,1792]{3,2,1,0:T(8,128)(2,1)}), bf16[16,2,64,1792]{3,2,1,0:T(8,128)(2,1)}, u32[]{:S(2)}, u32[]{:S(2)}) %all-to-all-start) | async-done | bytes 7340064 | tf_op jit(solution)/shard_map/all_to_all | solution.py:258
  407.9 17.0 %fusion.3 = f32[16,2,64,1536]{3,2,0,1:T(8,128)} fusion(bf16[2,1536,1536]{2,1,0:T(8,128)(2,1)} %param.28, bf16[16,2,64,1792]{3,2,1,0:T(8,128)(2,1)} %all-to-all-done), kind=kOutput, calls=%fused_computation.7 | convolution fusion | flops 9663676416 | bytes 28311552 | tf_op jit(solution)/shard_map/necd,edf->necf/dot_general | solution.py:262
  424.9 12.3 %convert_bitcast_fusion = bf16[16,2,64,1536]{3,2,0,1:T(8,128)(2,1)} fusion(bf16[2,768,1536]{2,1,0:T(8,128)(2,1)} %param.29, f32[16,2,64,1536]{3,2,0,1:T(8,128)} %fusion.3, bf16[256,2,768]{2,0,1:T(8,128)(2,1)S(1)} %copy.146, bf16[16,2,64,1792]{3,2,1,0:T(8,128)(2,1)} %all-to-all-done), kind=kOutput, calls=%fused_computation.13 | convolution fusion | flops 5646581760 | bytes 25427968 | tf_op jit(solution)/shard_map/necf,efd->necd/dot_general | solution.py:269
  437.2 6.1 %copy.148 = bf16[16,2,64,1536]{3,2,1,0:T(8,128)(2,1)} copy(bf16[16,2,64,1536]{3,2,0,1:T(8,128)(2,1)} %convert_bitcast_fusion) | data formatting | bytes 12582912 | tf_op jit(solution)/shard_map/convert_element_type | solution.py:271
  443.2 7.1 %all-to-all-start.1 = ((bf16[16,2,64,1536]{3,2,1,0:T(8,128)(2,1)}), bf16[16,2,64,1536]{3,2,1,0:T(8,128)(2,1)}, u32[]{:S(2)}, u32[]{:S(2)}) async-start(bf16[16,2,64,1536]{3,2,1,0:T(8,128)(2,1)} %copy.148), calls=%async_computation.1 | async-start | bytes 12582912 | tf_op jit(solution)/shard_map/all_to_all | solution.py:272
  450.3 3.7 select_reduce_fusion
  454.1 79.4 %all-to-all-done.1 = bf16[16,2,64,1536]{3,2,1,0:T(8,128)(2,1)} async-done(((bf16[16,2,64,1536]{3,2,1,0:T(8,128)(2,1)}), bf16[16,2,64,1536]{3,2,1,0:T(8,128)(2,1)}, u32[]{:S(2)}, u32[]{:S(2)}) %all-to-all-start.1) | async-done | bytes 6291488 | tf_op jit(solution)/shard_map/all_to_all | solution.py:272
  533.5 6.4 %fusion.35 = f32[384,1536]{1,0:T(8,128)S(1)} fusion(bf16[2048,1536]{1,0:T(8,128)(2,1)} %bitcast.38, f32[384,2048]{1,0:T(8,128)} %select_reduce_fusion), kind=kOutput, calls=%fused_computation.50 | convolution fusion | flops 2416705536 | bytes 11796480 | tf_op jit(solution)/shard_map/dot_general | solution.py:282
  539.9 6.5 %fusion.13 = bf16[384,1536]{1,0:T(8,128)(2,1)} fusion(f32[384,1536]{1,0:T(8,128)S(1)} %fusion.35, bf16[2048,1536]{1,0:T(8,128)(2,1)} %bitcast.38, bf16[384,1536]{1,0:T(8,128)(2,1)S(1)} %get-tuple-element.9, f32[384,2048]{1,0:T(8,128)S(1)} %copy-done.2), kind=kOutput, calls=%fused_computation.27 | convolution fusion | flops 2421424128 | bytes 14155776 | tf_op jit(solution)/shard_map/dot_general | solution.py:282
  (90 shorter events, 8.0 us)
Async XLA Ops:
  6.5 3.7 copy-start.7
  6.5 3.8 copy-start.5
  6.5 3.8 copy-start.6
  6.5 55.8 %all-gather.5.cloned.1.call-start = ((), (), s32[]{:S(2)}) async-start(), calls=%async_computation.2 | async-start | bytes 9732096 | tf_op jit(solution)/shard_map/all_gather | solution.py:158
  8.0 3.2 copy-start.19
  8.0 4.7 copy-start.20
  8.0 4.8 copy-start
  10.2 80.1 %all-gather.7.cloned.1.call-start = ((), (), s32[]{:S(2)}) async-start(), calls=%async_computation.3 | async-start | bytes 2949120 | tf_op jit(solution)/shard_map/all_gather | solution.py:169
  11.2 144.3 %all-gather.9.cloned.1.call-start = ((), (), s32[]{:S(2)}) async-start(), calls=%async_computation.4 | async-start | bytes 6684672 | tf_op jit(solution)/shard_map/all_gather | solution.py:227
  11.5 50.9 %copy-start.17 = (s32[16]{0:T(128)}, s32[16]{0:T(128)S(1)}, u32[]{:S(2)}) copy-start(s32[16]{0:T(128)S(1)} %reduce) | copy-start | bytes 196
  12.2 0.5 copy-start.14
  12.8 77.5 %copy-start.9 = (s32[384]{0:T(512)}, s32[384]{0:T(512)S(1)}, u32[]{:S(2)}) copy-start(s32[384]{0:T(512)S(1)} %select_reduce_fusion.1) | copy-start | bytes 4612
  13.1 55.7 %copy-start.13 = (f32[384]{0:T(512)}, f32[384]{0:T(512)S(1)}, u32[]{:S(2)}) copy-start(f32[384]{0:T(512)S(1)} %add_rsqrt_fusion.1) | copy-start | bytes 4612
  65.8 3.0 copy-start.15
  90.3 7.5 %copy-start.8 = (s32[384,4]{0,1:T(4,128)S(1)}, s32[384,4]{0,1:T(4,128)}, u32[]{:S(2)}) copy-start(s32[384,4]{0,1:T(4,128)} %param.21) | copy-start | bytes 18436
  94.3 3.9 copy-start.21
  95.2 153.3 %all-gather.11.cloned.1.call-start = ((), (), s32[]{:S(2)}) async-start(), calls=%async_computation.5 | async-start | bytes 5308416 | tf_op jit(solution)/shard_map/all_gather | solution.py:222
  98.4 14.0 %copy-start.18 = (s32[16]{0:T(128)S(1)}, s32[16]{0:T(128)}, u32[]{:S(2)}) copy-start(s32[16]{0:T(128)} %copy-done.17) | copy-start | bytes 196
  246.4 2.1 copy-start.1
  248.5 5.8 %copy-start.10 = (s32[384]{0:T(512)S(1)}, s32[384]{0:T(512)}, u32[]{:S(2)}) copy-start(s32[384]{0:T(512)} %copy-done.9) | copy-start | bytes 4612
  248.5 5.8 %copy-start.11 = (s32[256]{0:T(256)S(1)}, s32[256]{0:T(256)}, u32[]{:S(2)}) copy-start(s32[256]{0:T(256)} %eq.83) | copy-start | bytes 3076
  254.3 3.5 copy-start.12
  257.8 1.1 copy-start.3
  257.8 1.6 copy-start.4
  265.4 15.1 %slice-start = ((bf16[256,5120]{1,0:T(8,128)(2,1)}), bf16[256,1536]{1,0:T(8,128)(2,1)S(1)}, s32[]{:S(2)}) async-start(bf16[256,5120]{1,0:T(8,128)(2,1)} %all-gather.7.cloned.1.call-done), calls=%async_computation.6 | async-start | bytes 1572864 | tf_op jit(solution)/shard_map/slice | solution.py:173
  265.4 142.5 %all-to-all-start = ((bf16[16,2,64,1792]{3,2,1,0:T(8,128)(2,1)}), bf16[16,2,64,1792]{3,2,1,0:T(8,128)(2,1)}, u32[]{:S(2)}, u32[]{:S(2)}) async-start(bf16[16,2,64,1792]{3,2,1,0:T(8,128)(2,1)} %bitcast.89), calls=%async_computation | async-start | bytes 14680064 | tf_op jit(solution)/shard_map/all_to_all | solution.py:258
  443.2 7.1 %copy-start.16 = (f32[384,4]{0,1:T(4,128)S(1)}, f32[384,4]{0,1:T(4,128)}, u32[]{:S(2)}) copy-start(f32[384,4]{0,1:T(4,128)} %param.22) | copy-start | bytes 18436
  443.2 90.2 %all-to-all-start.1 = ((bf16[16,2,64,1536]{3,2,1,0:T(8,128)(2,1)}), bf16[16,2,64,1536]{3,2,1,0:T(8,128)(2,1)}, u32[]{:S(2)}, u32[]{:S(2)}) async-start(bf16[16,2,64,1536]{3,2,1,0:T(8,128)(2,1)} %copy.148), calls=%async_computation.1 | async-start | bytes 12582912 | tf_op jit(solution)/shard_map/all_to_all | solution.py:272
  533.5 6.4 %copy-start.2 = (f32[384,2048]{1,0:T(8,128)S(1)}, f32[384,2048]{1,0:T(8,128)}, u32[]{:S(2)}) copy-start(f32[384,2048]{1,0:T(8,128)} %select_reduce_fusion) | copy-start | bytes 9437188
Sparse Core Ops, SparseCore 0:
  10.3 52.0 all-gather.4
  64.0 26.1 all-gather.6
  95.3 60.1 all-gather.8
  157.0 35.6 all-gather.10

commit v4 on v3

--- a/solution.py
+++ b/solution.py
@@ -46,8 +46,8 @@
 KEY_BLOCK = 512
 
 
-def attention_kernel(first_ref, q_ref, k_ref, v_ref, qseg_ref, kseg_ref, init_ref, o_ref,
-                     max_ref, sum_ref, acc_ref):
+def attention_kernel(first_ref, bmin_ref, bmax_ref, qrange_ref, q_ref, k_ref, v_ref, qseg_ref,
+                     kseg_ref, init_ref, o_ref, max_ref, sum_ref, acc_ref):
     j = pl.program_id(1)
     tok_rows = qseg_ref.shape[0]
     rows = q_ref.shape[1]
@@ -62,9 +62,15 @@
         sum_ref[...] = jnp.ones_like(sum_ref)
         acc_ref[...] = jnp.zeros_like(acc_ref)
 
-    @pl.when(low + j <= high)
+    block = jnp.minimum(low + j, high)
+    seg_low = bmin_ref[block]
+    seg_high = bmax_ref[block]
+    shares_segment = (seg_low == 0) | (
+        (seg_high >= qrange_ref[0]) & (seg_low <= qrange_ref[1])
+    )
+
+    @pl.when((low + j <= high) & shares_segment)
     def _():
-        block = low + j
         scores = lax.dot_general(
             q_ref[0], k_ref[...], (((1,), (1,)), ((), ())),
             preferred_element_type=jnp.float32,
@@ -111,25 +117,29 @@
         sink_logits.reshape(KVH, group_size, 1, 1), (KVH, group_size, tok_rows, 1)
     ).reshape(KVH, rows, 1)
     first = positions[:1]
-
-    def key_block(h, j, first_ref):
+    block_seg = key_seg.reshape(block_total, KEY_BLOCK)
+    block_min = jnp.min(block_seg, axis=1)
+    block_max = jnp.max(block_seg, axis=1)
+    query_range = jnp.stack([segments[0], segments[-1]])
+
+    def key_block(h, j, first_ref, *_):
         f = first_ref[0]
         low = jnp.maximum(f - (WINDOW - 1), 0) // KEY_BLOCK
         high = (f + tok_rows - 1) // KEY_BLOCK
         return jnp.minimum(low + j, high)
 
     grid_spec = pltpu.PrefetchScalarGridSpec(
-        num_scalar_prefetch=1,
+        num_scalar_prefetch=4,
         grid=(KVH, steps),
         in_specs=[
-            pl.BlockSpec((1, rows, HD), lambda h, j, f: (h, 0, 0)),
-            pl.BlockSpec((KEY_BLOCK, HD), lambda h, j, f: (key_block(h, j, f), h)),
-            pl.BlockSpec((KEY_BLOCK, HD), lambda h, j, f: (key_block(h, j, f), KVH + h)),
-            pl.BlockSpec((tok_rows, 1), lambda h, j, f: (0, 0)),
-            pl.BlockSpec((1, KEY_BLOCK), lambda h, j, f: (0, key_block(h, j, f))),
-            pl.BlockSpec((1, rows, 1), lambda h, j, f: (h, 0, 0)),
+            pl.BlockSpec((1, rows, HD), lambda h, j, f, *_: (h, 0, 0)),
+            pl.BlockSpec((KEY_BLOCK, HD), lambda h, j, f, *_: (key_block(h, j, f), h)),
+            pl.BlockSpec((KEY_BLOCK, HD), lambda h, j, f, *_: (key_block(h, j, f), KVH + h)),
+            pl.BlockSpec((tok_rows, 1), lambda h, j, f, *_: (0, 0)),
+            pl.BlockSpec((1, KEY_BLOCK), lambda h, j, f, *_: (0, key_block(h, j, f))),
+            pl.BlockSpec((1, rows, 1), lambda h, j, f, *_: (h, 0, 0)),
         ],
-        out_specs=pl.BlockSpec((1, rows, HD), lambda h, j, f: (h, 0, 0)),
+        out_specs=pl.BlockSpec((1, rows, HD), lambda h, j, f, *_: (h, 0, 0)),
         scratch_shapes=[
             pltpu.VMEM((rows, 1), jnp.float32),
             pltpu.VMEM((rows, 1), jnp.float32),
@@ -141,7 +151,7 @@
         grid_spec=grid_spec,
         out_shape=jax.ShapeDtypeStruct((KVH, rows, HD), jnp.bfloat16),
         compiler_params=pltpu.CompilerParams(dimension_semantics=("arbitrary", "arbitrary")),
-    )(first, queries, key_piece, key_piece, query_seg, key_seg, init)
+    )(first, block_min, block_max, query_range, queries, key_piece, key_piece, query_seg, key_seg, init)
     return jnp.transpose(
         out.reshape(KVH, group_size, tok_rows, HD), (2, 0, 1, 3)
     ).reshape(tok_rows, HEADS * HD)

time: 554 us -> 530 us (0.957)
  the two profiles are of different devices: /device:TPU:100 before, /device:TPU:116 now
where the time goes in v4:
time: 530 us; the launch traced here: 529 us
  waiting for transfers between devices  306 us (58%)
  Pallas kernels  67.1 us (13%)
  matrix products  66.2 us (12%)
  local copies, waits for them, and re-layouts  29.3 us (6%)
  other arithmetic  24.6 us (5%)
  starting transfers between devices  22.3 us (4%)
  between operations  13.5 us (3%)
    all_to_all x1, waiting for transfers between devices, body(): lax.all_to_all(send, 'exp', split_axis=0, concat_axis=0, tiled=True)  127 us
    all_to_all x1, waiting for transfers between devices, body(): lax.all_to_all(outputs, 'exp', split_axis=0, concat_axis=0, tiled=True)  79.8 us
    pallas_call x1, Pallas kernels, window_attention(): pl.pallas_call(attention_kernel, grid_spec=grid_spec, out_shape=jax.Shape...  67.1 us
    all_gather x1, waiting for transfers between devices, gather_weights(): lax.all_gather(jnp.concatenate([attention_in] + down_cols, axis=1), axis_...  48 us
    all_gather x1, waiting for transfers between devices, body(): key_piece = lax.all_gather(key_value, 'exp', axis=0, tiled=True)  33.4 us
    all_gather x1, waiting for transfers between devices, gather_weights(): lax.all_gather(jnp.concatenate(up_rows, axis=1), axis_name, axis=0, tiled...  17.5 us
    dot_general x1, matrix products, body(): jnp.einsum('necd,edf->necf', arrived_rows, expert_gate_up, preferred_elem...  17 us
    all_to_all x1, starting transfers between devices, body(): lax.all_to_all(send, 'exp', split_axis=0, concat_axis=0, tiled=True)  15.1 us
  transfers between devices with their start and end apart: 6, of which 5 were waited for; matrix products, arithmetic and copies ran while one was open for 9% of the time, Pallas kernels for 13%

profile of v4, /device:TPU:116, one launch (start us, length us, event | category | flops | bytes accessed | tf_op | source)
XLA Modules:
  0.0 528.9 jit_solution(16900856381422021398)
XLA Ops:
  6.5 1.5 copy.131
  8.0 2.1 pad_maximum_fusion
  13.1 48.0 %all-gather.5.cloned.1.call-done = bf16[1536,2816]{0,1:T(8,128)(2,1)} async-done(((bf16[1536,352]{0,1:T(8,128)(2,1)}), bf16[1536,2816]{0,1:T(8,128)(2,1)}) %all-gather.5.cloned.1.call-update) | async-done | bytes 8650768 | tf_op jit(solution)/shard_map/all_gather | solution.py:168
  61.1 3.5 slice.72
  64.6 3.0 fusion.57
  67.6 4.3 fusion.41
  71.9 17.5 %all-gather.7.cloned.1.call-done = bf16[256,5120]{1,0:T(8,128)(2,1)} async-done(((bf16[32,5120]{1,0:T(8,128)(2,1)}), bf16[256,5120]{1,0:T(8,128)(2,1)}) %all-gather.7.cloned.1.call-update) | async-done | bytes 2621456 | tf_op jit(solution)/shard_map/all_gather | solution.py:179
  89.3 4.1 add_convert_fusion
  93.4 0.8 slice.76
  94.8 0.8 broadcast_in_dim.72.qseg_ref
  95.6 1.2 slice.54.first_ref
  97.6 3.7 broadcast_in_dim.73.init_ref
  101.3 9.3 %reduce-window.19 = s32[32,12,128]{2,1,0:T(8,128)S(1)} reduce-window(s32[32,12,128]{2,1,0:T(8,128)S(1)} %fusion.43, s32[]{:T(128)} %constant.14.clone.1), window={size=1x1x128 pad=0_0x0_0x127_0}, to_apply=%region_7.8 | reduce-window | flops 6242304 | bytes 393220 | tf_op jit(solution)/shard_map/reduce-window.1
  112.2 1.8 pad_add_fusion.qrange_ref
  114.6 4.9 fusion
  120.3 1.4 copy.134
  121.8 33.4 %all-gather.9.cloned.1.call-done.k_ref.v_ref = bf16[6144,512]{1,0:T(8,128)(2,1)} async-done(((bf16[384,512]{1,0:T(8,128)(2,1)}), bf16[6144,512]{1,0:T(8,128)(2,1)}) %all-gather.9.cloned.1.call-update) | async-done | bytes 6291472 | tf_op jit(solution)/shard_map/all_gather | solution.py:237
  155.2 67.1 %shard_map.172 = bf16[2,2304,128]{2,1,0:T(8,128)(2,1)} custom-call(s32[1]{0:T(128)} %slice.54.first_ref, s32[12]{0:T(128)} %get-tuple-element.6.bmin_ref, s32[12]{0:T(128)} %get-tuple-element.5.bmax_ref, s32[2]{0:T(128)} %pad_add_fusion.qrange_ref, bf16[2,2304,128]{2,1,0:T(8,128)(2,1)} %bitcast.91, ...), custom_call_target="tpu_custom_call" | custom-call | tf_op jit(solution)/shard_map/pallas_call | solution.py:149
  222.3 2.0 copy.137
  224.4 5.8 %convert_add_fusion.1 = f32[384,1536]{1,0:T(8,128)} fusion(bf16[384,1536]{1,0:T(8,128)(2,1)S(1)} %copy-done.1, bf16[384,1536]{0,1:T(8,128)(2,1)S(1)} %bitcast.94, bf16[1536,1536]{0,1:T(8,128)(2,1)} %all-gather.11.cloned.1.call-done), kind=kOutput, calls=%fused_computation.18 | convolution fusion | flops 1813118976 | bytes 9437184 | tf_op jit(solution)/shard_map/dot_general | solution.py:241
  230.2 3.4 fusion.19
  235.3 6.0 %convolution_convert_fusion = bf16[2048,1792]{1,0:T(8,128)(2,1)} fusion(pred[2048,384]{1,0:T(8,128)(4,1)S(1)} %copy-done.4, bf16[384,256]{1,0:T(8,128)(2,1)S(1)} %fusion.27, bf16[384,1536]{1,0:T(8,128)(2,1)S(1)} %fusion.21), kind=kOutput, calls=%fused_computation.6 | convolution fusion | flops 2824994816 | bytes 9502720 | tf_op jit(solution)/shard_map/dot_general | solution.py:263
  241.3 15.1 %all-to-all-start = ((bf16[16,2,64,1792]{3,2,1,0:T(8,128)(2,1)}), bf16[16,2,64,1792]{3,2,1,0:T(8,128)(2,1)}, u32[]{:S(2)}, u32[]{:S(2)}) async-start(bf16[16,2,64,1792]{3,2,1,0:T(8,128)(2,1)} %bitcast.89), calls=%async_computation | async-start | bytes 14680064 | tf_op jit(solution)/shard_map/all_to_all | solution.py:268
  257.0 126.5 %all-to-all-done = bf16[16,2,64,1792]{3,2,1,0:T(8,128)(2,1)} async-done(((bf16[16,2,64,1792]{3,2,1,0:T(8,128)(2,1)}), bf16[16,2,64,1792]{3,2,1,0:T(8,128)(2,1)}, u32[]{:S(2)}, u32[]{:S(2)}) %all-to-all-start) | async-done | bytes 7340064 | tf_op jit(solution)/shard_map/all_to_all | solution.py:268
  383.5 17.0 %fusion.3 = f32[16,2,64,1536]{3,2,0,1:T(8,128)} fusion(bf16[2,1536,1536]{2,1,0:T(8,128)(2,1)} %param.28, bf16[16,2,64,1792]{3,2,1,0:T(8,128)(2,1)} %all-to-all-done), kind=kOutput, calls=%fused_computation.7 | convolution fusion | flops 9663676416 | bytes 28311552 | tf_op jit(solution)/shard_map/necd,edf->necf/dot_general | solution.py:272
  400.5 12.2 %convert_bitcast_fusion = bf16[16,2,64,1536]{3,2,0,1:T(8,128)(2,1)} fusion(bf16[2,768,1536]{2,1,0:T(8,128)(2,1)} %param.29, f32[16,2,64,1536]{3,2,0,1:T(8,128)} %fusion.3, bf16[256,2,768]{2,0,1:T(8,128)(2,1)S(1)} %copy.146, bf16[16,2,64,1792]{3,2,1,0:T(8,128)(2,1)} %all-to-all-done), kind=kOutput, calls=%fused_computation.13 | convolution fusion | flops 5646581760 | bytes 25427968 | tf_op jit(solution)/shard_map/necf,efd->necd/dot_general | solution.py:279
  412.7 6.1 %copy.148 = bf16[16,2,64,1536]{3,2,1,0:T(8,128)(2,1)} copy(bf16[16,2,64,1536]{3,2,0,1:T(8,128)(2,1)} %convert_bitcast_fusion) | data formatting | bytes 12582912 | tf_op jit(solution)/shard_map/convert_element_type | solution.py:281
  418.8 7.1 %all-to-all-start.1 = ((bf16[16,2,64,1536]{3,2,1,0:T(8,128)(2,1)}), bf16[16,2,64,1536]{3,2,1,0:T(8,128)(2,1)}, u32[]{:S(2)}, u32[]{:S(2)}) async-start(bf16[16,2,64,1536]{3,2,1,0:T(8,128)(2,1)} %copy.148), calls=%async_computation.1 | async-start | bytes 12582912 | tf_op jit(solution)/shard_map/all_to_all | solution.py:282
  425.9 3.7 select_reduce_fusion
  429.6 79.8 %all-to-all-done.1 = bf16[16,2,64,1536]{3,2,1,0:T(8,128)(2,1)} async-done(((bf16[16,2,64,1536]{3,2,1,0:T(8,128)(2,1)}), bf16[16,2,64,1536]{3,2,1,0:T(8,128)(2,1)}, u32[]{:S(2)}, u32[]{:S(2)}) %all-to-all-start.1) | async-done | bytes 6291488 | tf_op jit(solution)/shard_map/all_to_all | solution.py:282
  509.5 6.4 %fusion.35 = f32[384,1536]{1,0:T(8,128)S(1)} fusion(bf16[2048,1536]{1,0:T(8,128)(2,1)} %bitcast.38, f32[384,2048]{1,0:T(8,128)} %select_reduce_fusion), kind=kOutput, calls=%fused_computation.50 | convolution fusion | flops 2416705536 | bytes 11796480 | tf_op jit(solution)/shard_map/dot_general | solution.py:292
  515.9 6.5 %fusion.13 = bf16[384,1536]{1,0:T(8,128)(2,1)} fusion(f32[384,1536]{1,0:T(8,128)S(1)} %fusion.35, bf16[2048,1536]{1,0:T(8,128)(2,1)} %bitcast.38, bf16[384,1536]{1,0:T(8,128)(2,1)S(1)} %get-tuple-element.13, f32[384,2048]{1,0:T(8,128)S(1)} %copy-done.2), kind=kOutput, calls=%fused_computation.27 | convolution fusion | flops 2421424128 | bytes 14155776 | tf_op jit(solution)/shard_map/dot_general | solution.py:292
  (96 shorter events, 9.5 us)
Async XLA Ops:
  6.5 3.7 copy-start.8
  6.5 3.8 copy-start.6
  6.5 3.8 copy-start.7
  6.5 54.5 %all-gather.5.cloned.1.call-start = ((), (), s32[]{:S(2)}) async-start(), calls=%async_computation.2 | async-start | bytes 9732096 | tf_op jit(solution)/shard_map/all_gather | solution.py:168
  8.0 3.2 copy-start.20
  8.0 4.7 copy-start.21
  8.0 4.8 copy-start
  10.2 79.1 %all-gather.7.cloned.1.call-start = ((), (), s32[]{:S(2)}) async-start(), calls=%async_computation.3 | async-start | bytes 2949120 | tf_op jit(solution)/shard_map/all_gather | solution.py:179
  11.2 144.0 %all-gather.9.cloned.1.call-start = ((), (), s32[]{:S(2)}) async-start(), calls=%async_computation.4 | async-start | bytes 6684672 | tf_op jit(solution)/shard_map/all_gather | solution.py:237
  11.5 49.6 %copy-start.18 = (s32[16]{0:T(128)}, s32[16]{0:T(128)S(1)}, u32[]{:S(2)}) copy-start(s32[16]{0:T(128)S(1)} %reduce) | copy-start | bytes 196
  12.1 0.6 copy-start.15
  12.8 76.5 %copy-start.10 = (s32[384]{0:T(512)}, s32[384]{0:T(512)S(1)}, u32[]{:S(2)}) copy-start(s32[384]{0:T(512)S(1)} %select_reduce_fusion.1) | copy-start | bytes 4612
  13.1 54.5 %copy-start.14 = (f32[384]{0:T(512)}, f32[384]{0:T(512)S(1)}, u32[]{:S(2)}) copy-start(f32[384]{0:T(512)S(1)} %add_rsqrt_fusion.1) | copy-start | bytes 4612
  64.6 3.0 copy-start.16
  89.3 7.5 %copy-start.9 = (s32[384,4]{0,1:T(4,128)S(1)}, s32[384,4]{0,1:T(4,128)}, u32[]{:S(2)}) copy-start(s32[384,4]{0,1:T(4,128)} %param.21) | copy-start | bytes 18436
  93.4 3.8 copy-start.19
  93.4 4.0 copy-start.22
  94.2 130.1 %all-gather.11.cloned.1.call-start = ((), (), s32[]{:S(2)}) async-start(), calls=%async_computation.5 | async-start | bytes 5308416 | tf_op jit(solution)/shard_map/all_gather | solution.py:232
  97.4 3.9 copy-start.5
  222.3 2.1 copy-start.1
  224.4 5.8 %copy-start.11 = (s32[384]{0:T(512)S(1)}, s32[384]{0:T(512)}, u32[]{:S(2)}) copy-start(s32[384]{0:T(512)} %copy-done.10) | copy-start | bytes 4612
  224.4 5.8 %copy-start.12 = (s32[256]{0:T(256)S(1)}, s32[256]{0:T(256)}, u32[]{:S(2)}) copy-start(s32[256]{0:T(256)} %eq.83) | copy-start | bytes 3076
  230.2 3.5 copy-start.13
  233.7 1.1 copy-start.3
  233.7 1.6 copy-start.4
  241.3 15.1 %slice-start = ((bf16[256,5120]{1,0:T(8,128)(2,1)}), bf16[256,1536]{1,0:T(8,128)(2,1)S(1)}, s32[]{:S(2)}) async-start(bf16[256,5120]{1,0:T(8,128)(2,1)} %all-gather.7.cloned.1.call-done), calls=%async_computation.6 | async-start | bytes 1572864 | tf_op jit(solution)/shard_map/slice | solution.py:183
  241.3 142.2 %all-to-all-start = ((bf16[16,2,64,1792]{3,2,1,0:T(8,128)(2,1)}), bf16[16,2,64,1792]{3,2,1,0:T(8,128)(2,1)}, u32[]{:S(2)}, u32[]{:S(2)}) async-start(bf16[16,2,64,1792]{3,2,1,0:T(8,128)(2,1)} %bitcast.89), calls=%async_computation | async-start | bytes 14680064 | tf_op jit(solution)/shard_map/all_to_all | solution.py:268
  418.8 7.1 %copy-start.17 = (f32[384,4]{0,1:T(4,128)S(1)}, f32[384,4]{0,1:T(4,128)}, u32[]{:S(2)}) copy-start(f32[384,4]{0,1:T(4,128)} %param.22) | copy-start | bytes 18436
  418.8 90.6 %all-to-all-start.1 = ((bf16[16,2,64,1536]{3,2,1,0:T(8,128)(2,1)}), bf16[16,2,64,1536]{3,2,1,0:T(8,128)(2,1)}, u32[]{:S(2)}, u32[]{:S(2)}) async-start(bf16[16,2,64,1536]{3,2,1,0:T(8,128)(2,1)} %copy.148), calls=%async_computation.1 | async-start | bytes 12582912 | tf_op jit(solution)/shard_map/all_to_all | solution.py:282
  509.5 6.4 %copy-start.2 = (f32[384,2048]{1,0:T(8,128)S(1)}, f32[384,2048]{1,0:T(8,128)}, u32[]{:S(2)}) copy-start(f32[384,2048]{1,0:T(8,128)} %select_reduce_fusion) | copy-start | bytes 9437188
Sparse Core Ops, SparseCore 0:
  10.3 50.7 all-gather.4
  62.8 26.5 all-gather.6
  94.4 60.7 all-gather.8
  156.7 34.3 all-gather.10

commit v5 on v4

--- a/solution.py
+++ b/solution.py
@@ -157,35 +157,31 @@
     ).reshape(tok_rows, HEADS * HD)
 
 
-def gather_weights(attention_in, downs, ups, expert_up, axis_name):
-    inner_width = attention_in.shape[0]
-    in_width = attention_in.shape[1]
+def gather_columns(first, downs, axis_name):
+    inner_width = first.shape[0]
+    first_width = first.shape[1]
     down_cols = [jnp.transpose(f, (1, 0, 2)).reshape(inner_width, -1) for f in downs]
-    local_adapters, local_experts, rank_size, hidden_width = expert_up.shape
-    up_rows = [f.reshape(-1, f.shape[2]) for f in ups] + [
-        jnp.transpose(expert_up, (0, 2, 1, 3)).reshape(local_adapters * rank_size, -1)
-    ]
     wide = lax.all_gather(
-        jnp.concatenate([attention_in] + down_cols, axis=1), axis_name, axis=1, tiled=True
-    )
-    peers = wide.shape[1] // (in_width + sum(c.shape[1] for c in down_cols))
+        jnp.concatenate([first] + down_cols, axis=1), axis_name, axis=1, tiled=True
+    )
+    peers = wide.shape[1] // (first_width + sum(c.shape[1] for c in down_cols))
     wide = wide.reshape(inner_width, peers, -1)
-    full_in = wide[:, :, :in_width].reshape(inner_width, -1)
-    joined = []
-    offset = in_width
+    held = [wide[:, :, :first_width].reshape(inner_width, -1)]
+    offset = first_width
     for c in down_cols:
-        joined.append(wide[:, :, offset : offset + c.shape[1]].reshape(inner_width, -1))
+        held.append(wide[:, :, offset : offset + c.shape[1]].reshape(inner_width, -1))
         offset += c.shape[1]
-    tall = lax.all_gather(jnp.concatenate(up_rows, axis=1), axis_name, axis=0, tiled=True)
-    seconds = []
+    return held
+
+
+def gather_rows(rows, axis_name):
+    tall = lax.all_gather(jnp.concatenate(rows, axis=1), axis_name, axis=0, tiled=True)
+    held = []
     offset = 0
-    for r in up_rows:
-        seconds.append(tall[:, offset : offset + r.shape[1]])
+    for r in rows:
+        held.append(tall[:, offset : offset + r.shape[1]])
         offset += r.shape[1]
-    bank = jnp.transpose(
-        seconds[-1].reshape(tall.shape[0], local_experts, hidden_width), (1, 0, 2)
-    )
-    return full_in, joined, seconds[:-1], bank
+    return held
 
 
 def body(
@@ -220,21 +216,34 @@
     rank_size = adapter_in_down.shape[2]
     select = adapter_select(token_adapter, adapter_count, rank_size)
     normed = scaled_norm(tokens, attention_gain)
-    full_in, joined, seconds, adapter_bank = gather_weights(
-        attention_in,
-        (adapter_in_down, adapter_out_down, adapter_expert_down),
-        (adapter_in_up, adapter_out_up),
-        adapter_expert_up,
-        "req",
-    )
-    in_low, out_low, expert_low = joined
-    in_high, out_high = seconds
-    full_out = lax.all_gather(attention_out, "req", axis=1, tiled=True)
+    full_in, in_low = gather_columns(attention_in, (adapter_in_down,), "req")
+    (in_high,) = gather_rows((adapter_in_up.reshape(-1, adapter_in_up.shape[2]),), "req")
     base_heads = jnp.dot(normed, full_in, preferred_element_type=jnp.float32)
     projected = (base_heads + low_rank(normed, select, in_low, in_high)).astype(jnp.bfloat16)
     group_size = HEADS // KVH
     key_value = projected[:, HEADS * HD :]
     key_piece = lax.all_gather(key_value, "exp", axis=0, tiled=True)
+    late_factors = (
+        attention_out, adapter_out_down, adapter_expert_down, adapter_out_up, adapter_expert_up
+    )
+    late_factors, key_piece = lax.optimization_barrier((late_factors, key_piece))
+    attention_out, adapter_out_down, adapter_expert_down, adapter_out_up, adapter_expert_up = (
+        late_factors
+    )
+    full_out, out_low, expert_low = gather_columns(
+        attention_out, (adapter_out_down, adapter_expert_down), "req"
+    )
+    local_adapters, local_experts, _, hidden_width = adapter_expert_up.shape
+    out_high, bank_rows = gather_rows(
+        (
+            adapter_out_up.reshape(-1, adapter_out_up.shape[2]),
+            jnp.transpose(adapter_expert_up, (0, 2, 1, 3)).reshape(local_adapters * rank_size, -1),
+        ),
+        "req",
+    )
+    adapter_bank = jnp.transpose(
+        bank_rows.reshape(bank_rows.shape[0], local_experts, hidden_width), (1, 0, 2)
+    )
     attended = window_attention(
         projected[:, : HEADS * HD], key_piece, positions, segments, lengths, sink_logits
     )

time: 530 us -> 521 us (0.983)
  the two profiles are of different devices: /device:TPU:116 before, /device:TPU:100 now
where the time goes in v5:
time: 521 us; the launch traced here: 514 us
  waiting for transfers between devices  272 us (52%)
  Pallas kernels  75 us (14%)
  matrix products  63.8 us (12%)
  local copies, waits for them, and re-layouts  32.1 us (6%)
  starting transfers between devices  31.2 us (6%)
  other arithmetic  26.5 us (5%)
  between operations  13.5 us (3%)
    all_to_all x1, waiting for transfers between devices, body(): lax.all_to_all(send, 'exp', split_axis=0, concat_axis=0, tiled=True)  92.4 us
    pallas_call x1, Pallas kernels, window_attention(): pl.pallas_call(attention_kernel, grid_spec=grid_spec, out_shape=jax.Shape...  75 us
    all_gather x1, waiting for transfers between devices, body(): key_piece = lax.all_gather(key_value, 'exp', axis=0, tiled=True)  59.7 us
    all_to_all x1, waiting for transfers between devices, body(): lax.all_to_all(outputs, 'exp', split_axis=0, concat_axis=0, tiled=True)  59.3 us
    all_gather x2, waiting for transfers between devices, gather_columns(): lax.all_gather(jnp.concatenate([first] + down_cols, axis=1), axis_name, a...  43.5 us
    dot_general x1, matrix products, body(): jnp.einsum('necd,edf->necf', arrived_rows, expert_gate_up, preferred_elem...  17.1 us
    all_to_all x1, starting transfers between devices, body(): lax.all_to_all(send, 'exp', split_axis=0, concat_axis=0, tiled=True)  16.5 us
    all_gather x2, waiting for transfers between devices, gather_rows(): lax.all_gather(jnp.concatenate(rows, axis=1), axis_name, axis=0, tiled=True)  16.1 us
  transfers between devices with their start and end apart: 7, of which 5 were waited for; matrix products, arithmetic and copies ran while one was open for 10% of the time, Pallas kernels for 15%

profile of v5, /device:TPU:100, one launch (start us, length us, event | category | flops | bytes accessed | tf_op | source)
XLA Modules:
  0.0 513.9 jit_solution(4278769522967152668)
XLA Ops:
  6.5 1.5 copy.106
  8.1 1.9 pad_maximum_fusion
  12.1 43.5 %all-gather.6.cloned.1.call-done = bf16[1536,2304]{0,1:T(8,128)(2,1)} async-done(((bf16[1536,288]{0,1:T(8,128)(2,1)}), bf16[1536,2304]{0,1:T(8,128)(2,1)}) %all-gather.6.cloned.1.call-update) | async-done | bytes 7077904 | tf_op jit(solution)/shard_map/all_gather | solution.py:164
  55.6 3.5 slice.72
  60.3 4.3 fusion.40
  64.6 16.1 %all-gather.8.cloned.1.call-done = bf16[256,2048]{1,0:T(8,128)(2,1)} async-done(((bf16[32,2048]{1,0:T(8,128)(2,1)}), bf16[256,2048]{1,0:T(8,128)(2,1)}) %all-gather.8.cloned.1.call-update) | async-done | bytes 1048592 | tf_op jit(solution)/shard_map/all_gather | solution.py:178
  80.7 3.8 add_convert_fusion
  85.3 59.7 %all-gather.10.cloned.1.call-done.k_ref.v_ref = bf16[6144,512]{1,0:T(8,128)(2,1)} async-done(((bf16[384,512]{1,0:T(8,128)(2,1)}), bf16[6144,512]{1,0:T(8,128)(2,1)}) %all-gather.10.cloned.1.call-update) | async-done | bytes 6291472 | tf_op jit(solution)/shard_map/all_gather | solution.py:225
  145.1 2.1 pad_maximum_fusion.1
  148.9 1.2 slice.54.first_ref
  150.9 3.7 broadcast_in_dim.73.init_ref
  154.6 9.3 %reduce-window.19 = s32[32,12,128]{2,1,0:T(8,128)S(1)} reduce-window(s32[32,12,128]{2,1,0:T(8,128)S(1)} %fusion.42, s32[]{:T(128)} %constant.14.clone.1), window={size=1x1x128 pad=0_0x0_0x127_0}, to_apply=%region_7.8 | reduce-window | flops 6242304 | bytes 393220 | tf_op jit(solution)/shard_map/reduce-window.1
  165.5 1.9 pad_add_fusion.qrange_ref
  168.0 4.8 fusion
  173.7 1.4 copy.108
  175.1 75.0 %shard_map.172 = bf16[2,2304,128]{2,1,0:T(8,128)(2,1)} custom-call(s32[1]{0:T(128)} %slice.54.first_ref, s32[12]{0:T(128)} %get-tuple-element.18.bmin_ref, s32[12]{0:T(128)} %get-tuple-element.17.bmax_ref, s32[2]{0:T(128)} %pad_add_fusion.qrange_ref, bf16[2,2304,128]{2,1,0:T(8,128)(2,1)} %bitcast.96, ...), custom_call_target="tpu_custom_call" | custom-call | tf_op jit(solution)/shard_map/pallas_call | solution.py:149
  250.1 1.9 copy.111
  252.1 2.6 slice.76
  254.8 2.5 fusion.56
  257.3 3.6 convert_add_fusion.1
  260.8 3.4 fusion.19
  265.9 6.0 %convolution_convert_fusion = bf16[2048,1792]{1,0:T(8,128)(2,1)} fusion(pred[2048,384]{1,0:T(8,128)(4,1)S(1)} %copy-done.3, bf16[384,256]{1,0:T(8,128)(2,1)S(1)} %fusion.27, bf16[384,1536]{1,0:T(8,128)(2,1)S(1)} %fusion.21), kind=kOutput, calls=%fused_computation.6 | convolution fusion | flops 2824994816 | bytes 9502720 | tf_op jit(solution)/shard_map/dot_general | solution.py:272
  271.9 16.5 %all-to-all-start = ((bf16[16,2,64,1792]{3,2,1,0:T(8,128)(2,1)}), bf16[16,2,64,1792]{3,2,1,0:T(8,128)(2,1)}, u32[]{:S(2)}, u32[]{:S(2)}) async-start(bf16[16,2,64,1792]{3,2,1,0:T(8,128)(2,1)} %bitcast.90), calls=%async_computation | async-start | bytes 14680064 | tf_op jit(solution)/shard_map/all_to_all | solution.py:277
  288.9 92.4 %all-to-all-done = bf16[16,2,64,1792]{3,2,1,0:T(8,128)(2,1)} async-done(((bf16[16,2,64,1792]{3,2,1,0:T(8,128)(2,1)}), bf16[16,2,64,1792]{3,2,1,0:T(8,128)(2,1)}, u32[]{:S(2)}, u32[]{:S(2)}) %all-to-all-start) | async-done | bytes 7340064 | tf_op jit(solution)/shard_map/all_to_all | solution.py:277
  381.3 17.1 %fusion.3 = f32[16,2,64,1536]{3,2,0,1:T(8,128)} fusion(bf16[2,1536,1536]{2,1,0:T(8,128)(2,1)} %param.28, bf16[16,2,64,1792]{3,2,1,0:T(8,128)(2,1)} %all-to-all-done), kind=kOutput, calls=%fused_computation.7 | convolution fusion | flops 9663676416 | bytes 28311552 | tf_op jit(solution)/shard_map/necd,edf->necf/dot_general | solution.py:281
  398.4 12.2 %convert_bitcast_fusion = bf16[16,2,64,1536]{3,2,0,1:T(8,128)(2,1)} fusion(bf16[2,768,1536]{2,1,0:T(8,128)(2,1)} %param.29, f32[16,2,64,1536]{3,2,0,1:T(8,128)} %fusion.3, bf16[256,2,768]{2,0,1:T(8,128)(2,1)S(1)} %copy.121, bf16[16,2,64,1792]{3,2,1,0:T(8,128)(2,1)} %all-to-all-done), kind=kOutput, calls=%fused_computation.13 | convolution fusion | flops 5646581760 | bytes 25427968 | tf_op jit(solution)/shard_map/necf,efd->necd/dot_general | solution.py:288
  410.6 6.1 %copy.123 = bf16[16,2,64,1536]{3,2,1,0:T(8,128)(2,1)} copy(bf16[16,2,64,1536]{3,2,0,1:T(8,128)(2,1)} %convert_bitcast_fusion) | data formatting | bytes 12582912 | tf_op jit(solution)/shard_map/convert_element_type | solution.py:290
  416.7 14.6 %all-to-all-start.1 = ((bf16[16,2,64,1536]{3,2,1,0:T(8,128)(2,1)}), bf16[16,2,64,1536]{3,2,1,0:T(8,128)(2,1)}, u32[]{:S(2)}, u32[]{:S(2)}) async-start(bf16[16,2,64,1536]{3,2,1,0:T(8,128)(2,1)} %copy.123), calls=%async_computation.1 | async-start | bytes 12582912 | tf_op jit(solution)/shard_map/all_to_all | solution.py:291
  431.3 3.8 select_reduce_fusion
  435.0 59.3 %all-to-all-done.1 = bf16[16,2,64,1536]{3,2,1,0:T(8,128)(2,1)} async-done(((bf16[16,2,64,1536]{3,2,1,0:T(8,128)(2,1)}), bf16[16,2,64,1536]{3,2,1,0:T(8,128)(2,1)}, u32[]{:S(2)}, u32[]{:S(2)}) %all-to-all-start.1) | async-done | bytes 6291488 | tf_op jit(solution)/shard_map/all_to_all | solution.py:291
  494.4 6.5 %fusion.34 = f32[384,1536]{1,0:T(8,128)S(1)} fusion(bf16[2048,1536]{1,0:T(8,128)(2,1)} %bitcast.40, f32[384,2048]{1,0:T(8,128)} %select_reduce_fusion), kind=kOutput, calls=%fused_computation.50 | convolution fusion | flops 2416705536 | bytes 11796480 | tf_op jit(solution)/shard_map/dot_general | solution.py:301
  500.8 6.5 %fusion.13 = bf16[384,1536]{1,0:T(8,128)(2,1)} fusion(f32[384,1536]{1,0:T(8,128)S(1)} %fusion.34, bf16[2048,1536]{1,0:T(8,128)(2,1)} %bitcast.40, bf16[384,1536]{1,0:T(8,128)(2,1)S(1)} %get-tuple-element.24, f32[384,2048]{1,0:T(8,128)S(1)} %copy-done.2), kind=kOutput, calls=%fused_computation.27 | convolution fusion | flops 2421424128 | bytes 14155776 | tf_op jit(solution)/shard_map/dot_general | solution.py:301
  (92 shorter events, 11.8 us)
Async XLA Ops:
  6.5 4.2 copy-start.15
  6.5 5.1 copy-start.16
  6.5 5.2 %copy-start = (bf16[384,1536]{1,0:T(8,128)(2,1)S(1)}, bf16[384,1536]{1,0:T(8,128)(2,1)}, u32[]{:S(2)}) copy-start(bf16[384,1536]{1,0:T(8,128)(2,1)} %param.18) | copy-start | bytes 3538948
  6.5 49.0 %all-gather.6.cloned.1.call-start = ((), (), s32[]{:S(2)}) async-start(), calls=%async_computation.2 | async-start | bytes 7962624 | tf_op jit(solution)/shard_map/all_gather | solution.py:164
  9.9 70.7 %all-gather.8.cloned.1.call-start = ((), (), s32[]{:S(2)}) async-start(), calls=%async_computation.3 | async-start | bytes 1179648 | tf_op jit(solution)/shard_map/all_gather | solution.py:178
  10.7 134.4 %all-gather.10.cloned.1.call-start = ((), (), s32[]{:S(2)}) async-start(), calls=%async_computation.4 | async-start | bytes 6684672 | tf_op jit(solution)/shard_map/all_gather | solution.py:225
  11.0 0.7 copy-start.13
  11.1 0.6 copy-start.10
  55.6 4.7 copy-start.11
  84.5 62.8 %copy-start.6 = (bf16[2,2,16,768]{3,2,1,0:T(8,128)(2,1)S(1)}, bf16[2,2,16,768]{3,2,1,0:T(8,128)(2,1)}, u32[]{:S(2)}) copy-start(bf16[2,2,16,768]{3,2,1,0:T(8,128)(2,1)} %param.35) | copy-start | bytes 294916
  84.5 62.9 %copy-start.7 = (bf16[2,16,1536]{2,1,0:T(8,128)(2,1)S(1)}, bf16[2,16,1536]{2,1,0:T(8,128)(2,1)}, u32[]{:S(2)}) copy-start(bf16[2,16,1536]{2,1,0:T(8,128)(2,1)} %param.33) | copy-start | bytes 294916
  84.5 65.7 %copy-start.8 = (s32[384,4]{0,1:T(4,128)S(1)}, s32[384,4]{0,1:T(4,128)}, u32[]{:S(2)}) copy-start(s32[384,4]{0,1:T(4,128)} %param.21) | copy-start | bytes 18436
  85.3 65.3 %copy-start.14 = (s32[16]{0:T(128)S(1)}, s32[16]{0:T(128)}, u32[]{:S(2)}) copy-start(s32[16]{0:T(128)} %copy-done.13) | copy-start | bytes 196
  85.3 65.5 %copy-start.17 = (f32[12]{0:T(128)S(1)}, f32[12]{0:T(128)}, u32[]{:S(2)}) copy-start(f32[12]{0:T(128)} %param.25) | copy-start | bytes 148
  85.3 166.8 %all-gather.12.cloned.1.call-start = ((), (), s32[]{:S(2)}) async-start(), calls=%async_computation.5 | async-start | bytes 7077888 | tf_op jit(solution)/shard_map/all_gather | solution.py:164
  147.2 113.6 %all-gather.14.cloned.1.call-start = ((), (), s32[]{:S(2)}) async-start(), calls=%async_computation.6 | async-start | bytes 1769472 | tf_op jit(solution)/shard_map/all_gather | solution.py:178
  150.7 13.8 %copy-start.5 = (s32[6144]{0:T(1024)}, s32[6144]{0:T(1024)S(1)}, u32[]{:S(2)}) copy-start(s32[6144]{0:T(1024)S(1)} %convert_reduce_fusion) | copy-start | bytes 73732
  254.7 2.5 copy-start.1
  260.8 3.5 copy-start.9
  264.2 1.1 copy-start.4
  264.3 1.6 copy-start.3
  271.8 16.5 %slice-start = ((bf16[256,3072]{1,0:T(8,128)(2,1)}), bf16[256,1536]{1,0:T(8,128)(2,1)S(1)}, s32[]{:S(2)}) async-start(bf16[256,3072]{1,0:T(8,128)(2,1)} %all-gather.14.cloned.1.call-done), calls=%async_computation.7 | async-start | bytes 1572864 | tf_op jit(solution)/shard_map/slice | solution.py:182
  271.9 109.4 %all-to-all-start = ((bf16[16,2,64,1792]{3,2,1,0:T(8,128)(2,1)}), bf16[16,2,64,1792]{3,2,1,0:T(8,128)(2,1)}, u32[]{:S(2)}, u32[]{:S(2)}) async-start(bf16[16,2,64,1792]{3,2,1,0:T(8,128)(2,1)} %bitcast.90), calls=%async_computation | async-start | bytes 14680064 | tf_op jit(solution)/shard_map/all_to_all | solution.py:277
  416.7 14.6 %copy-start.12 = (f32[384,4]{0,1:T(4,128)S(1)}, f32[384,4]{0,1:T(4,128)}, u32[]{:S(2)}) copy-start(f32[384,4]{0,1:T(4,128)} %param.22) | copy-start | bytes 18436
  416.7 77.7 %all-to-all-start.1 = ((bf16[16,2,64,1536]{3,2,1,0:T(8,128)(2,1)}), bf16[16,2,64,1536]{3,2,1,0:T(8,128)(2,1)}, u32[]{:S(2)}, u32[]{:S(2)}) async-start(bf16[16,2,64,1536]{3,2,1,0:T(8,128)(2,1)} %copy.123), calls=%async_computation.1 | async-start | bytes 12582912 | tf_op jit(solution)/shard_map/all_to_all | solution.py:291
  494.4 6.5 %copy-start.2 = (f32[384,2048]{1,0:T(8,128)S(1)}, f32[384,2048]{1,0:T(8,128)}, u32[]{:S(2)}) copy-start(f32[384,2048]{1,0:T(8,128)} %select_reduce_fusion) | copy-start | bytes 9437188
Sparse Core Ops, SparseCore 0:
  10.1 45.4 all-gather.5
  57.3 23.3 all-gather.7
  85.4 59.5 all-gather.9
  147.3 42.2 all-gather.11
  191.1 24.3 all-gather.13

commit v6 on v4

--- a/solution.py
+++ b/solution.py
@@ -265,21 +265,28 @@
         jnp.concatenate([normed_two, low_parts], axis=1),
         preferred_element_type=jnp.float32,
     ).astype(jnp.bfloat16).reshape(peer_count, local_experts, CAP, -1)
-    arrived = lax.all_to_all(send, "exp", split_axis=0, concat_axis=0, tiled=True)
-    arrived_rows = arrived[..., :row_width]
-    arrived_low = arrived[..., row_width:]
     hidden_width = expert_down.shape[1]
-    gate_up = jnp.einsum(
-        "necd,edf->necf", arrived_rows, expert_gate_up, preferred_element_type=jnp.float32
-    )
-    up_part = gate_up[..., hidden_width:] + jnp.einsum(
-        "necr,erf->necf", arrived_low, adapter_bank, preferred_element_type=jnp.float32
-    )
-    hidden = (jax.nn.relu(gate_up[..., :hidden_width]) * up_part).astype(jnp.bfloat16)
-    outputs = jnp.einsum(
-        "necf,efd->necd", hidden, expert_down, preferred_element_type=jnp.float32
-    ).astype(jnp.bfloat16)
-    returned = lax.all_to_all(outputs, "exp", split_axis=0, concat_axis=0, tiled=True)
+
+    def expert_chunk(chunk):
+        arrived = lax.all_to_all(chunk, "exp", split_axis=0, concat_axis=0, tiled=True)
+        arrived_rows = arrived[..., :row_width]
+        arrived_low = arrived[..., row_width:]
+        gate_up = jnp.einsum(
+            "necd,edf->necf", arrived_rows, expert_gate_up, preferred_element_type=jnp.float32
+        )
+        up_part = gate_up[..., hidden_width:] + jnp.einsum(
+            "necr,erf->necf", arrived_low, adapter_bank, preferred_element_type=jnp.float32
+        )
+        hidden = (jax.nn.relu(gate_up[..., :hidden_width]) * up_part).astype(jnp.bfloat16)
+        outputs = jnp.einsum(
+            "necf,efd->necd", hidden, expert_down, preferred_element_type=jnp.float32
+        ).astype(jnp.bfloat16)
+        return lax.all_to_all(outputs, "exp", split_axis=0, concat_axis=0, tiled=True)
+
+    half = CAP // 2
+    returned = jnp.concatenate(
+        [expert_chunk(send[:, :, :half]), expert_chunk(send[:, :, half:])], axis=2
+    )
     flat_back = returned.reshape(EXPERTS * CAP, -1)
     gate_grid = jnp.sum(
         jnp.where(

time: 530 us -> 489 us (0.923)
  the two profiles are of different devices: /device:TPU:116 before, /device:TPU:84 now
where the time goes in v6:
time: 489 us; the launch traced here: 482 us
  waiting for transfers between devices  183 us (37%)
  Pallas kernels  84.1 us (17%)
  matrix products  68.9 us (14%)
  blocking collectives  44.1 us (9%)
  local copies, waits for them, and re-layouts  32.3 us (7%)
  starting transfers between devices  28.3 us (6%)
  other arithmetic  28.1 us (6%)
  between operations  13.7 us (3%)
    pallas_call x1, Pallas kernels, window_attention(): pl.pallas_call(attention_kernel, grid_spec=grid_spec, out_shape=jax.Shape...  84.1 us
    all_to_all x2, waiting for transfers between devices, expert_chunk(): lax.all_to_all(outputs, 'exp', split_axis=0, concat_axis=0, tiled=True)  65.3 us
    all_gather x1, waiting for transfers between devices, gather_weights(): lax.all_gather(jnp.concatenate([attention_in] + down_cols, axis=1), axis_...  48.4 us
    all_to_all x1, blocking collectives, expert_chunk(): lax.all_to_all(chunk, 'exp', split_axis=0, concat_axis=0, tiled=True)  44.1 us
    all_gather x1, waiting for transfers between devices, body(): key_piece = lax.all_gather(key_value, 'exp', axis=0, tiled=True)  32 us
    dot_general x2, matrix products, expert_chunk(): jnp.einsum('necd,edf->necf', arrived_rows, expert_gate_up, preferred_elem...  22.1 us
    all_to_all x2, starting transfers between devices, expert_chunk(): lax.all_to_all(outputs, 'exp', split_axis=0, concat_axis=0, tiled=True)  20.8 us
    all_to_all x1, waiting for transfers between devices, expert_chunk(): lax.all_to_all(chunk, 'exp', split_axis=0, concat_axis=0, tiled=True)  19.1 us
  transfers between devices with their start and end apart: 7, of which 6 were waited for; matrix products, arithmetic and copies ran while one was open for 19% of the time, Pallas kernels for 17%

profile of v6, /device:TPU:84, one launch (start us, length us, event | category | flops | bytes accessed | tf_op | source)
XLA Modules:
  0.0 482.3 jit_solution(10413484854927486918)
XLA Ops:
  8.1 2.0 pad_maximum_fusion.1
  13.1 48.4 %all-gather.5.cloned.1.call-done = bf16[1536,2816]{0,1:T(8,128)(2,1)} async-done(((bf16[1536,352]{0,1:T(8,128)(2,1)}), bf16[1536,2816]{0,1:T(8,128)(2,1)}) %all-gather.5.cloned.1.call-update) | async-done | bytes 8650768 | tf_op jit(solution)/shard_map/all_gather | solution.py:168
  61.5 3.5 slice.96
  65.0 3.0 fusion.81
  67.9 4.3 fusion.64
  72.2 17.5 %all-gather.7.cloned.1.call-done = bf16[256,5120]{1,0:T(8,128)(2,1)} async-done(((bf16[32,5120]{1,0:T(8,128)(2,1)}), bf16[256,5120]{1,0:T(8,128)(2,1)}) %all-gather.7.cloned.1.call-update) | async-done | bytes 2621456 | tf_op jit(solution)/shard_map/all_gather | solution.py:179
  89.7 4.1 add_convert_fusion
  99.1 3.7 broadcast_in_dim.73.init_ref
  102.9 9.5 %reduce-window.19 = s32[32,12,128]{2,1,0:T(8,128)S(1)} reduce-window(s32[32,12,128]{2,1,0:T(8,128)S(1)} %fusion.66, s32[]{:T(128)} %constant.16.clone.1), window={size=1x1x128 pad=0_0x0_0x127_0}, to_apply=%region_7.8 | reduce-window | flops 6242304 | bytes 393220 | tf_op jit(solution)/shard_map/reduce-window.1
  116.5 4.8 %fusion = pred[2048,384]{1,0:T(8,128)(4,1)} fusion(s32[384,4]{0,1:T(4,128)S(1)} %multiply_add_fusion), kind=kLoop, calls=%fused_computation.3 | loop fusion | flops 5505024 | bytes 792576 | tf_op jit(solution)/shard_map/reduce_or | solution.py:257
  123.7 32.0 %all-gather.9.cloned.1.call-done.k_ref.v_ref = bf16[6144,512]{1,0:T(8,128)(2,1)} async-done(((bf16[384,512]{1,0:T(8,128)(2,1)}), bf16[6144,512]{1,0:T(8,128)(2,1)}) %all-gather.9.cloned.1.call-update) | async-done | bytes 6291472 | tf_op jit(solution)/shard_map/all_gather | solution.py:237
  155.7 84.1 %shard_map.172 = bf16[2,2304,128]{2,1,0:T(8,128)(2,1)} custom-call(s32[1]{0:T(128)} %slice.72.first_ref, s32[12]{0:T(128)} %get-tuple-element.6.bmin_ref, s32[12]{0:T(128)} %get-tuple-element.5.bmax_ref, s32[2]{0:T(128)} %pad_add_fusion.qrange_ref, bf16[2,2304,128]{2,1,0:T(8,128)(2,1)} %bitcast.119, ...), custom_call_target="tpu_custom_call" | custom-call | tf_op jit(solution)/shard_map/pallas_call | solution.py:149
  241.8 5.8 %convert_add_fusion.1 = f32[384,1536]{1,0:T(8,128)} fusion(bf16[384,1536]{1,0:T(8,128)(2,1)S(1)} %copy-done.1, bf16[384,1536]{0,1:T(8,128)(2,1)S(1)} %bitcast.122, bf16[1536,1536]{0,1:T(8,128)(2,1)} %all-gather.11.cloned.1.call-done), kind=kOutput, calls=%fused_computation.21 | convolution fusion | flops 1813118976 | bytes 9437184 | tf_op jit(solution)/shard_map/dot_general | solution.py:241
  247.6 3.4 fusion.38
  253.3 4.1 convolution_convert_fusion
  257.5 2.4 fusion.82
  259.9 44.1 %all_to_all.20 = bf16[16,2,32,1792]{3,2,1,0:T(8,128)(2,1)} all-to-all(bf16[16,2,32,1792]{3,2,1,0:T(8,128)(2,1)S(1)} %get-tuple-element.10), channel_id=1, replica_groups=mesh['req'=8,'exp'=16] {'exp'}, dimensions={0} | all-to-all | bytes 7340032 | tf_op jit(solution)/shard_map/all_to_all | solution.py:271
  303.9 7.4 %all-to-all-start.2 = ((bf16[16,2,32,1792]{3,2,1,0:T(8,128)(2,1)}), bf16[16,2,32,1792]{3,2,1,0:T(8,128)(2,1)}, u32[]{:S(2)}, u32[]{:S(2)}) async-start(bf16[16,2,32,1792]{3,2,1,0:T(8,128)(2,1)} %get-tuple-element.11), calls=%async_computation.2 | async-start | bytes 7340032 | tf_op jit(solution)/shard_map/all_to_all | solution.py:271
  312.7 11.0 %fusion.9 = f32[16,2,32,1536]{3,2,0,1:T(8,128)} fusion(bf16[2,1536,1536]{2,1,0:T(8,128)(2,1)} %param.28, bf16[16,2,32,1792]{3,2,1,0:T(8,128)(2,1)} %all_to_all.20), kind=kOutput, calls=%fused_computation.14 | convolution fusion | flops 4831838208 | bytes 18874368 | tf_op jit(solution)/shard_map/necd,edf->necf/dot_general | solution.py:274
  323.8 7.7 %fusion.24 = bf16[16,2,32,1536]{3,2,0,1:T(8,128)(2,1)S(1)} fusion(bf16[2,768,1536]{2,1,0:T(8,128)(2,1)} %param.29, f32[16,2,32,1536]{3,2,0,1:T(8,128)} %fusion.9, bf16[256,2,768]{2,0,1:T(8,128)(2,1)} %copy.160, bf16[16,2,32,1792]{3,2,1,0:T(8,128)(2,1)} %all_to_all.20), kind=kOutput, calls=%fused_computation.25 | convolution fusion | flops 2823290880 | bytes 15466496 | tf_op jit(solution)/shard_map/necf,efd->necd/dot_general | solution.py:281
  333.3 19.1 %all-to-all-done.2 = bf16[16,2,32,1792]{3,2,1,0:T(8,128)(2,1)} async-done(((bf16[16,2,32,1792]{3,2,1,0:T(8,128)(2,1)}), bf16[16,2,32,1792]{3,2,1,0:T(8,128)(2,1)}, u32[]{:S(2)}, u32[]{:S(2)}) %all-to-all-start.2) | async-done | bytes 3670048 | tf_op jit(solution)/shard_map/all_to_all | solution.py:271
  352.4 13.6 %all-to-all-start.1 = ((bf16[16,2,32,1536]{3,2,1,0:T(8,128)(2,1)}), bf16[16,2,32,1536]{3,2,1,0:T(8,128)(2,1)S(1)}, u32[]{:S(2)}, u32[]{:S(2)}) async-start(bf16[16,2,32,1536]{3,2,1,0:T(8,128)(2,1)} %copy.162), calls=%async_computation.1 | async-start | bytes 6291456 | tf_op jit(solution)/shard_map/all_to_all | solution.py:284
  366.0 11.0 %fusion.12 = f32[16,2,32,1536]{3,2,0,1:T(8,128)} fusion(bf16[2,1536,1536]{2,1,0:T(8,128)(2,1)} %param.28, bf16[16,2,32,1792]{3,2,1,0:T(8,128)(2,1)} %all-to-all-done.2), kind=kOutput, calls=%fused_computation.15 | convolution fusion | flops 4831838208 | bytes 18874368 | tf_op jit(solution)/shard_map/necd,edf->necf/dot_general | solution.py:274
  377.0 9.3 %fusion.21 = bf16[16,2,32,1536]{3,2,0,1:T(8,128)(2,1)} fusion(bf16[2,768,1536]{2,1,0:T(8,128)(2,1)} %param.29, f32[16,2,32,1536]{3,2,0,1:T(8,128)} %fusion.12, bf16[256,2,768]{2,0,1:T(8,128)(2,1)} %copy.160, bf16[16,2,32,1792]{3,2,1,0:T(8,128)(2,1)} %all-to-all-done.2), kind=kOutput, calls=%fused_computation.24 | convolution fusion | flops 2823290880 | bytes 15466496 | tf_op jit(solution)/shard_map/necf,efd->necd/dot_general | solution.py:281
  386.4 3.9 copy.165
  390.2 22.0 %all-to-all-done.1 = bf16[16,2,32,1536]{3,2,1,0:T(8,128)(2,1)S(1)} async-done(((bf16[16,2,32,1536]{3,2,1,0:T(8,128)(2,1)}), bf16[16,2,32,1536]{3,2,1,0:T(8,128)(2,1)S(1)}, u32[]{:S(2)}, u32[]{:S(2)}) %all-to-all-start.1) | async-done | bytes 3145760 | tf_op jit(solution)/shard_map/all_to_all | solution.py:284
  412.2 7.2 %all-to-all-start.3 = ((bf16[16,2,32,1536]{3,2,1,0:T(8,128)(2,1)}), bf16[16,2,32,1536]{3,2,1,0:T(8,128)(2,1)}, u32[]{:S(2)}, u32[]{:S(2)}) async-start(bf16[16,2,32,1536]{3,2,1,0:T(8,128)(2,1)} %copy.165), calls=%async_computation.3 | async-start | bytes 6291456 | tf_op jit(solution)/shard_map/all_to_all | solution.py:284
  419.4 3.8 select_reduce_fusion
  423.2 43.3 %all-to-all-done.3 = bf16[16,2,32,1536]{3,2,1,0:T(8,128)(2,1)} async-done(((bf16[16,2,32,1536]{3,2,1,0:T(8,128)(2,1)}), bf16[16,2,32,1536]{3,2,1,0:T(8,128)(2,1)}, u32[]{:S(2)}, u32[]{:S(2)}) %all-to-all-start.3) | async-done | bytes 3145760 | tf_op jit(solution)/shard_map/all_to_all | solution.py:284
  466.5 2.6 pad_maximum_fusion
  469.3 2.6 fusion.54
  471.9 3.6 fusion.34
  (102 shorter events, 23.8 us)
Async XLA Ops:
  6.5 3.7 copy-start.9
  6.5 3.8 copy-start.7
  6.5 3.8 copy-start.8
  6.5 4.7 copy-start.20
  6.5 6.1 %copy-start.21 = (s32[1,16]{1,0:T(1,128)S(1)}, s32[1,16]{1,0:T(1,128)}, u32[]{:S(2)}) copy-start(s32[1,16]{1,0:T(1,128)} %param.20) | copy-start | bytes 196
  6.5 6.2 %copy-start = (bf16[384,1536]{1,0:T(8,128)(2,1)S(1)}, bf16[384,1536]{1,0:T(8,128)(2,1)}, u32[]{:S(2)}) copy-start(bf16[384,1536]{1,0:T(8,128)(2,1)} %param.18) | copy-start | bytes 3538948
  6.6 54.9 %all-gather.5.cloned.1.call-start = ((), (), s32[]{:S(2)}) async-start(), calls=%async_computation.4 | async-start | bytes 9732096 | tf_op jit(solution)/shard_map/all_gather | solution.py:168
  10.2 79.5 %all-gather.7.cloned.1.call-start = ((), (), s32[]{:S(2)}) async-start(), calls=%async_computation.5 | async-start | bytes 2949120 | tf_op jit(solution)/shard_map/all_gather | solution.py:179
  11.2 144.5 %all-gather.9.cloned.1.call-start = ((), (), s32[]{:S(2)}) async-start(), calls=%async_computation.6 | async-start | bytes 6684672 | tf_op jit(solution)/shard_map/all_gather | solution.py:237
  11.5 50.0 %copy-start.19 = (s32[16]{0:T(128)}, s32[16]{0:T(128)S(1)}, u32[]{:S(2)}) copy-start(s32[16]{0:T(128)S(1)} %reduce) | copy-start | bytes 196
  12.1 0.5 copy-start.16
  12.7 77.0 %copy-start.11 = (s32[384]{0:T(512)}, s32[384]{0:T(512)S(1)}, u32[]{:S(2)}) copy-start(s32[384]{0:T(512)S(1)} %select_reduce_fusion.1) | copy-start | bytes 4612
  13.1 54.9 %copy-start.15 = (f32[384]{0:T(512)}, f32[384]{0:T(512)S(1)}, u32[]{:S(2)}) copy-start(f32[384]{0:T(512)S(1)} %add_rsqrt_fusion.1) | copy-start | bytes 4612
  64.9 3.0 copy-start.17
  89.7 7.5 %copy-start.10 = (s32[384,4]{0,1:T(4,128)S(1)}, s32[384,4]{0,1:T(4,128)}, u32[]{:S(2)}) copy-start(s32[384,4]{0,1:T(4,128)} %param.21) | copy-start | bytes 18436
  94.6 147.1 %all-gather.11.cloned.1.call-start = ((), (), s32[]{:S(2)}) async-start(), calls=%async_computation.7 | async-start | bytes 5308416 | tf_op jit(solution)/shard_map/all_gather | solution.py:232
  98.3 4.6 copy-start.6
  155.7 86.0 %copy-start.1 = (bf16[384,1536]{1,0:T(8,128)(2,1)S(1)}, bf16[384,1536]{1,0:T(8,128)(2,1)}, u32[]{:S(2)}) copy-start(bf16[384,1536]{1,0:T(8,128)(2,1)} %param.18) | copy-start | bytes 3538948
  241.8 5.8 %copy-start.12 = (s32[384]{0:T(512)S(1)}, s32[384]{0:T(512)}, u32[]{:S(2)}) copy-start(s32[384]{0:T(512)} %copy-done.11) | copy-start | bytes 4612
  241.8 5.8 %copy-start.13 = (s32[256]{0:T(256)S(1)}, s32[256]{0:T(256)}, u32[]{:S(2)}) copy-start(s32[256]{0:T(256)} %eq.83) | copy-start | bytes 3076
  247.6 3.5 copy-start.14
  251.0 6.5 %copy-start.2 = (bf16[384,1536]{1,0:T(8,128)(2,1)}, bf16[384,1536]{1,0:T(8,128)(2,1)S(1)}, u32[]{:S(2)}) copy-start(bf16[384,1536]{1,0:T(8,128)(2,1)S(1)} %get-tuple-element.15) | copy-start | bytes 3538948
  251.0 2.3 copy-start.5
  303.9 7.4 %slice-start = ((bf16[256,5120]{1,0:T(8,128)(2,1)}), bf16[256,1536]{1,0:T(8,128)(2,1)S(1)}, s32[]{:S(2)}) async-start(bf16[256,5120]{1,0:T(8,128)(2,1)} %all-gather.7.cloned.1.call-done), calls=%async_computation.8 | async-start | bytes 1572864 | tf_op jit(solution)/shard_map/slice | solution.py:183
  303.9 48.4 %all-to-all-start.2 = ((bf16[16,2,32,1792]{3,2,1,0:T(8,128)(2,1)}), bf16[16,2,32,1792]{3,2,1,0:T(8,128)(2,1)}, u32[]{:S(2)}, u32[]{:S(2)}) async-start(bf16[16,2,32,1792]{3,2,1,0:T(8,128)(2,1)} %get-tuple-element.11), calls=%async_computation.2 | async-start | bytes 7340032 | tf_op jit(solution)/shard_map/all_to_all | solution.py:271
  352.4 59.8 %all-to-all-start.1 = ((bf16[16,2,32,1536]{3,2,1,0:T(8,128)(2,1)}), bf16[16,2,32,1536]{3,2,1,0:T(8,128)(2,1)S(1)}, u32[]{:S(2)}, u32[]{:S(2)}) async-start(bf16[16,2,32,1536]{3,2,1,0:T(8,128)(2,1)} %copy.162), calls=%async_computation.1 | async-start | bytes 6291456 | tf_op jit(solution)/shard_map/all_to_all | solution.py:284
  390.2 29.2 %copy-start.18 = (f32[384,4]{0,1:T(4,128)S(1)}, f32[384,4]{0,1:T(4,128)}, u32[]{:S(2)}) copy-start(f32[384,4]{0,1:T(4,128)} %param.22) | copy-start | bytes 18436
  412.2 54.3 %all-to-all-start.3 = ((bf16[16,2,32,1536]{3,2,1,0:T(8,128)(2,1)}), bf16[16,2,32,1536]{3,2,1,0:T(8,128)(2,1)}, u32[]{:S(2)}, u32[]{:S(2)}) async-start(bf16[16,2,32,1536]{3,2,1,0:T(8,128)(2,1)} %copy.165), calls=%async_computation.3 | async-start | bytes 6291456 | tf_op jit(solution)/shard_map/all_to_all | solution.py:284
  466.5 2.8 copy-start.4
  469.3 2.6 copy-start.3
Sparse Core Ops, SparseCore 0:
  10.3 51.0 all-gather.4
  63.1 26.5 all-gather.6
  94.7 60.9 all-gather.8
  157.2 34.2 all-gather.10

commit v7 on v6

--- a/solution.py
+++ b/solution.py
@@ -283,9 +283,10 @@
         ).astype(jnp.bfloat16)
         return lax.all_to_all(outputs, "exp", split_axis=0, concat_axis=0, tiled=True)
 
-    half = CAP // 2
+    chunk_count = 4
+    part = CAP // chunk_count
     returned = jnp.concatenate(
-        [expert_chunk(send[:, :, :half]), expert_chunk(send[:, :, half:])], axis=2
+        [expert_chunk(send[:, :, c * part : (c + 1) * part]) for c in range(chunk_count)], axis=2
     )
     flat_back = returned.reshape(EXPERTS * CAP, -1)
     gate_grid = jnp.sum(

time: 489 us -> 498 us (1.018)
  the two profiles are of different devices: /device:TPU:84 before, /device:TPU:24 now
where the time goes in v7:
time: 498 us; the launch traced here: 491 us
  waiting for transfers between devices  151 us (30%)
  blocking collectives  137 us (28%)
  matrix products  86.6 us (17%)
  local copies, waits for them, and re-layouts  35.5 us (7%)
  other arithmetic  28.1 us (6%)
  starting transfers between devices  20.7 us (4%)
  Pallas kernels  18.2 us (4%)
  between operations  13.9 us (3%)
    all_to_all x3, blocking collectives, expert_chunk(): lax.all_to_all(chunk, 'exp', split_axis=0, concat_axis=0, tiled=True)  137 us
    all_gather x1, waiting for transfers between devices, gather_weights(): lax.all_gather(jnp.concatenate([attention_in] + down_cols, axis=1), axis_...  48.8 us
    all_gather x1, waiting for transfers between devices, body(): key_piece = lax.all_gather(key_value, 'exp', axis=0, tiled=True)  34.9 us
    dot_general x4, matrix products, expert_chunk(): jnp.einsum('necd,edf->necf', arrived_rows, expert_gate_up, preferred_elem...  33.6 us
    all_to_all x4, waiting for transfers between devices, expert_chunk(): lax.all_to_all(outputs, 'exp', split_axis=0, concat_axis=0, tiled=True)  28.9 us
    dot_general x4, matrix products, expert_chunk(): jnp.einsum('necf,efd->necd', hidden, expert_down, preferred_element_type=...  24.5 us
    pallas_call x1, Pallas kernels, window_attention(): pl.pallas_call(attention_kernel, grid_spec=grid_spec, out_shape=jax.Shape...  18.2 us
    all_gather x1, waiting for transfers between devices, gather_weights(): lax.all_gather(jnp.concatenate(up_rows, axis=1), axis_name, axis=0, tiled...  18.2 us
  transfers between devices with their start and end apart: 9, of which 9 were waited for; matrix products, arithmetic and copies ran while one was open for 23% of the time, Pallas kernels for 4%

profile of v7, /device:TPU:24, one launch (start us, length us, event | category | flops | bytes accessed | tf_op | source)
XLA Modules:
  0.0 491.3 jit_solution(18436871121038417994)
XLA Ops:
  12.5 48.8 %all-gather.5.cloned.1.call-done = bf16[1536,2816]{0,1:T(8,128)(2,1)} async-done(((bf16[1536,352]{0,1:T(8,128)(2,1)}), bf16[1536,2816]{0,1:T(8,128)(2,1)}) %all-gather.5.cloned.1.call-update) | async-done | bytes 8650768 | tf_op jit(solution)/shard_map/all_gather | solution.py:168
  67.8 4.3 fusion.100
  72.1 18.2 %all-gather.7.cloned.1.call-done = bf16[256,5120]{1,0:T(8,128)(2,1)} async-done(((bf16[32,5120]{1,0:T(8,128)(2,1)}), bf16[256,5120]{1,0:T(8,128)(2,1)}) %all-gather.7.cloned.1.call-update) | async-done | bytes 2621456 | tf_op jit(solution)/shard_map/all_gather | solution.py:179
  90.3 4.0 add_convert_fusion
  102.2 9.6 %reduce-window.19 = s32[32,12,128]{2,1,0:T(8,128)S(1)} reduce-window(s32[32,12,128]{2,1,0:T(8,128)S(1)} %fusion.110, s32[]{:T(128)} %constant.31.clone.1), window={size=1x1x128 pad=0_0x0_0x127_0}, to_apply=%region_7.8 | reduce-window | flops 6242304 | bytes 393220 | tf_op jit(solution)/shard_map/reduce-window.1
  116.0 4.9 fusion
  123.2 34.9 %all-gather.9.cloned.1.call-done.k_ref.v_ref = bf16[6144,512]{1,0:T(8,128)(2,1)} async-done(((bf16[384,512]{1,0:T(8,128)(2,1)}), bf16[6144,512]{1,0:T(8,128)(2,1)}) %all-gather.9.cloned.1.call-update) | async-done | bytes 6291472 | tf_op jit(solution)/shard_map/all_gather | solution.py:237
  158.1 18.2 %shard_map.172 = bf16[2,2304,128]{2,1,0:T(8,128)(2,1)} custom-call(s32[1]{0:T(128)} %slice.102.first_ref, s32[12]{0:T(128)} %get-tuple-element.6.bmin_ref, s32[12]{0:T(128)} %get-tuple-element.5.bmax_ref, s32[2]{0:T(128)} %pad_add_fusion.qrange_ref, bf16[2,2304,128]{2,1,0:T(8,128)(2,1)} %bitcast.165, ...), custom_call_target="tpu_custom_call" | custom-call | tf_op jit(solution)/shard_map/pallas_call | solution.py:149
  178.3 13.2 %all-gather.11.cloned.1.call-done = bf16[1536,1536]{0,1:T(8,128)(2,1)} async-done(((bf16[1536,192]{0,1:T(8,128)(2,1)}), bf16[1536,1536]{0,1:T(8,128)(2,1)}) %all-gather.11.cloned.1.call-update) | async-done | bytes 4718608 | tf_op jit(solution)/shard_map/all_gather | solution.py:232
  191.6 5.8 %convert_add_fusion.1 = f32[384,1536]{1,0:T(8,128)} fusion(bf16[384,1536]{1,0:T(8,128)(2,1)S(1)} %copy-done.1, bf16[384,1536]{0,1:T(8,128)(2,1)S(1)} %bitcast.168, bf16[1536,1536]{0,1:T(8,128)(2,1)} %all-gather.11.cloned.1.call-done), kind=kOutput, calls=%fused_computation.25 | convolution fusion | flops 1813118976 | bytes 9437184 | tf_op jit(solution)/shard_map/dot_general | solution.py:241
  202.9 4.1 convolution_convert_fusion
  209.2 82.9 %all_to_all.40 = bf16[16,2,16,1792]{3,2,1,0:T(8,128)(2,1)} all-to-all(bf16[16,2,16,1792]{3,2,1,0:T(8,128)(2,1)S(1)} %get-tuple-element.10), channel_id=1, replica_groups=mesh['req'=8,'exp'=16] {'exp'}, dimensions={0} | all-to-all | bytes 3670016 | tf_op jit(solution)/shard_map/all_to_all | solution.py:271
  292.1 27.8 %all_to_all.41 = bf16[16,2,16,1792]{3,2,1,0:T(8,128)(2,1)} all-to-all(bf16[16,2,16,1792]{3,2,1,0:T(8,128)(2,1)S(1)} %get-tuple-element.13), channel_id=1, replica_groups=mesh['req'=8,'exp'=16] {'exp'}, dimensions={0} | all-to-all | bytes 3670016 | tf_op jit(solution)/shard_map/all_to_all | solution.py:271
  319.9 26.6 %all_to_all.42 = bf16[16,2,16,1792]{3,2,1,0:T(8,128)(2,1)} all-to-all(bf16[16,2,16,1792]{3,2,1,0:T(8,128)(2,1)S(1)} %get-tuple-element.12), channel_id=1, replica_groups=mesh['req'=8,'exp'=16] {'exp'}, dimensions={0} | all-to-all | bytes 3670016 | tf_op jit(solution)/shard_map/all_to_all | solution.py:271
  346.5 3.8 all-to-all-start.6
  351.9 8.4 %fusion.17 = f32[16,2,16,1536]{3,2,0,1:T(8,128)} fusion(bf16[2,1536,1536]{2,1,0:T(8,128)(2,1)} %param.28, bf16[16,2,16,1792]{3,2,1,0:T(8,128)(2,1)} %all_to_all.40), kind=kOutput, calls=%fused_computation.28 | convolution fusion | flops 2415919104 | bytes 14155776 | tf_op jit(solution)/shard_map/necd,edf->necf/dot_general | solution.py:274
  360.3 5.2 %fusion.52 = bf16[16,2,16,1536]{3,2,0,1:T(8,128)(2,1)S(1)} fusion(bf16[2,768,1536]{2,1,0:T(8,128)(2,1)} %param.29, f32[16,2,16,1536]{3,2,0,1:T(8,128)} %fusion.17, bf16[256,2,768]{2,0,1:T(8,128)(2,1)} %copy.188, bf16[16,2,16,1792]{3,2,1,0:T(8,128)(2,1)} %all_to_all.40), kind=kOutput, calls=%fused_computation.45 | convolution fusion | flops 1411645440 | bytes 10485760 | tf_op jit(solution)/shard_map/necf,efd->necd/dot_general | solution.py:281
  366.8 6.4 %all-to-all-done.6 = bf16[16,2,16,1792]{3,2,1,0:T(8,128)(2,1)S(1)} async-done(((bf16[16,2,16,1792]{3,2,1,0:T(8,128)(2,1)}), bf16[16,2,16,1792]{3,2,1,0:T(8,128)(2,1)S(1)}, u32[]{:S(2)}, u32[]{:S(2)}) %all-to-all-start.6) | async-done | bytes 1835040 | tf_op jit(solution)/shard_map/all_to_all | solution.py:271
  373.2 3.9 all-to-all-start.1
  377.1 8.4 %fusion.20 = f32[16,2,16,1536]{3,2,0,1:T(8,128)} fusion(bf16[2,1536,1536]{2,1,0:T(8,128)(2,1)} %param.28, bf16[16,2,16,1792]{3,2,1,0:T(8,128)(2,1)} %all_to_all.41), kind=kOutput, calls=%fused_computation.29 | convolution fusion | flops 2415919104 | bytes 14155776 | tf_op jit(solution)/shard_map/necd,edf->necf/dot_general | solution.py:274
  385.5 6.4 %fusion.49 = bf16[16,2,16,1536]{3,2,0,1:T(8,128)(2,1)} fusion(bf16[2,768,1536]{2,1,0:T(8,128)(2,1)} %param.29, f32[16,2,16,1536]{3,2,0,1:T(8,128)} %fusion.20, bf16[256,2,768]{2,0,1:T(8,128)(2,1)} %copy.188, bf16[16,2,16,1792]{3,2,1,0:T(8,128)(2,1)} %all_to_all.41), kind=kOutput, calls=%fused_computation.44 | convolution fusion | flops 1411645440 | bytes 10485760 | tf_op jit(solution)/shard_map/necf,efd->necd/dot_general | solution.py:281
  394.7 4.2 all-to-all-done.1
  398.9 3.7 all-to-all-start.3
  402.6 8.4 %fusion.23 = f32[16,2,16,1536]{3,2,0,1:T(8,128)} fusion(bf16[2,1536,1536]{2,1,0:T(8,128)(2,1)} %param.28, bf16[16,2,16,1792]{3,2,1,0:T(8,128)(2,1)} %all_to_all.42), kind=kOutput, calls=%fused_computation.30 | convolution fusion | flops 2415919104 | bytes 14155776 | tf_op jit(solution)/shard_map/necd,edf->necf/dot_general | solution.py:274
  411.0 6.4 %fusion.46 = bf16[16,2,16,1536]{3,2,0,1:T(8,128)(2,1)} fusion(bf16[2,768,1536]{2,1,0:T(8,128)(2,1)} %param.29, f32[16,2,16,1536]{3,2,0,1:T(8,128)} %fusion.23, bf16[256,2,768]{2,0,1:T(8,128)(2,1)} %copy.188, bf16[16,2,16,1792]{3,2,1,0:T(8,128)(2,1)} %all_to_all.42), kind=kOutput, calls=%fused_computation.43 | convolution fusion | flops 1411645440 | bytes 10485760 | tf_op jit(solution)/shard_map/necf,efd->necd/dot_general | solution.py:281
  420.1 4.5 all-to-all-done.3
  424.6 4.4 all-to-all-start.5
  429.0 8.4 %fusion.26 = f32[16,2,16,1536]{3,2,0,1:T(8,128)} fusion(bf16[2,1536,1536]{2,1,0:T(8,128)(2,1)} %param.28, bf16[16,2,16,1792]{3,2,1,0:T(8,128)(2,1)} %copy-done.5), kind=kOutput, calls=%fused_computation.31 | convolution fusion | flops 2415919104 | bytes 14155776 | tf_op jit(solution)/shard_map/necd,edf->necf/dot_general | solution.py:274
  437.4 6.5 %fusion.43 = bf16[16,2,16,1536]{3,2,0,1:T(8,128)(2,1)} fusion(bf16[2,768,1536]{2,1,0:T(8,128)(2,1)} %param.29, f32[16,2,16,1536]{3,2,0,1:T(8,128)} %fusion.26, bf16[256,2,768]{2,0,1:T(8,128)(2,1)} %copy.188, bf16[16,2,16,1792]{3,2,1,0:T(8,128)(2,1)} %copy-done.5), kind=kOutput, calls=%fused_computation.42 | convolution fusion | flops 1411645440 | bytes 10485760 | tf_op jit(solution)/shard_map/necf,efd->necd/dot_general | solution.py:281
  449.9 4.7 all-to-all-start.7
  454.6 3.7 select_reduce_fusion
  458.4 16.9 %all-to-all-done.7 = bf16[16,2,16,1536]{3,2,1,0:T(8,128)(2,1)} async-done(((bf16[16,2,16,1536]{3,2,1,0:T(8,128)(2,1)}), bf16[16,2,16,1536]{3,2,1,0:T(8,128)(2,1)}, u32[]{:S(2)}, u32[]{:S(2)}) %all-to-all-start.7) | async-done | bytes 1572896 | tf_op jit(solution)/shard_map/all_to_all | solution.py:284
  (114 shorter events, 59.7 us)
Async XLA Ops:
  6.5 54.8 %all-gather.5.cloned.1.call-start = ((), (), s32[]{:S(2)}) async-start(), calls=%async_computation.8 | async-start | bytes 9732096 | tf_op jit(solution)/shard_map/all_gather | solution.py:168
  7.9 2.3 copy-start.11
  8.0 2.4 copy-start.9
  8.0 2.4 copy-start.10
  8.0 3.3 copy-start.19
  8.0 4.1 copy-start.20
  8.0 4.2 copy-start
  10.2 80.1 %all-gather.7.cloned.1.call-start = ((), (), s32[]{:S(2)}) async-start(), calls=%async_computation.9 | async-start | bytes 2949120 | tf_op jit(solution)/shard_map/all_gather | solution.py:179
  11.2 146.9 %all-gather.9.cloned.1.call-start = ((), (), s32[]{:S(2)}) async-start(), calls=%async_computation.10 | async-start | bytes 6684672 | tf_op jit(solution)/shard_map/all_gather | solution.py:237
  11.5 0.6 copy-start.17
  11.6 0.6 copy-start.14
  64.8 3.0 copy-start.15
  94.3 3.4 copy-start.12
  94.3 3.9 copy-start.18
  94.4 4.0 copy-start.21
  95.2 96.4 %all-gather.11.cloned.1.call-start = ((), (), s32[]{:S(2)}) async-start(), calls=%async_computation.11 | async-start | bytes 5308416 | tf_op jit(solution)/shard_map/all_gather | solution.py:232
  98.4 3.8 copy-start.8
  176.3 15.3 %copy-start.1 = (bf16[384,1536]{1,0:T(8,128)(2,1)S(1)}, bf16[384,1536]{1,0:T(8,128)(2,1)}, u32[]{:S(2)}) copy-start(bf16[384,1536]{1,0:T(8,128)(2,1)} %param.18) | copy-start | bytes 3538948
  197.4 3.5 copy-start.13
  200.8 2.1 copy-start.2
  200.8 1.6 copy-start.6
  201.2 1.7 copy-start.7
  346.5 3.9 slice-start
  346.5 26.7 %all-to-all-start.6 = ((bf16[16,2,16,1792]{3,2,1,0:T(8,128)(2,1)}), bf16[16,2,16,1792]{3,2,1,0:T(8,128)(2,1)S(1)}, u32[]{:S(2)}, u32[]{:S(2)}) async-start(bf16[16,2,16,1792]{3,2,1,0:T(8,128)(2,1)} %get-tuple-element.11), calls=%async_computation.6 | async-start | bytes 3670016 | tf_op jit(solution)/shard_map/all_to_all | solution.py:271
  373.2 12.3 %copy-start.5 = (bf16[16,2,16,1792]{3,2,1,0:T(8,128)(2,1)}, bf16[16,2,16,1792]{3,2,1,0:T(8,128)(2,1)S(1)}, u32[]{:S(2)}) copy-start(bf16[16,2,16,1792]{3,2,1,0:T(8,128)(2,1)S(1)} %all-to-all-done.6) | copy-start | bytes 5505028
  373.2 25.7 %all-to-all-start.1 = ((bf16[16,2,16,1536]{3,2,1,0:T(8,128)(2,1)}), bf16[16,2,16,1536]{3,2,1,0:T(8,128)(2,1)S(1)}, u32[]{:S(2)}, u32[]{:S(2)}) async-start(bf16[16,2,16,1536]{3,2,1,0:T(8,128)(2,1)} %copy.190), calls=%async_computation.1 | async-start | bytes 3145728 | tf_op jit(solution)/shard_map/all_to_all | solution.py:284
  398.9 25.7 %all-to-all-start.3 = ((bf16[16,2,16,1536]{3,2,1,0:T(8,128)(2,1)}), bf16[16,2,16,1536]{3,2,1,0:T(8,128)(2,1)S(1)}, u32[]{:S(2)}, u32[]{:S(2)}) async-start(bf16[16,2,16,1536]{3,2,1,0:T(8,128)(2,1)} %copy.193), calls=%async_computation.3 | async-start | bytes 3145728 | tf_op jit(solution)/shard_map/all_to_all | solution.py:284
  424.6 25.4 %all-to-all-start.5 = ((bf16[16,2,16,1536]{3,2,1,0:T(8,128)(2,1)}), bf16[16,2,16,1536]{3,2,1,0:T(8,128)(2,1)}, u32[]{:S(2)}, u32[]{:S(2)}) async-start(bf16[16,2,16,1536]{3,2,1,0:T(8,128)(2,1)} %copy.196), calls=%async_computation.5 | async-start | bytes 3145728 | tf_op jit(solution)/shard_map/all_to_all | solution.py:284
  446.6 8.0 %copy-start.16 = (f32[384,4]{0,1:T(4,128)S(1)}, f32[384,4]{0,1:T(4,128)}, u32[]{:S(2)}) copy-start(f32[384,4]{0,1:T(4,128)} %param.22) | copy-start | bytes 18436
  449.9 25.3 %all-to-all-start.7 = ((bf16[16,2,16,1536]{3,2,1,0:T(8,128)(2,1)}), bf16[16,2,16,1536]{3,2,1,0:T(8,128)(2,1)}, u32[]{:S(2)}, u32[]{:S(2)}) async-start(bf16[16,2,16,1536]{3,2,1,0:T(8,128)(2,1)} %copy.199), calls=%async_computation.7 | async-start | bytes 3145728 | tf_op jit(solution)/shard_map/all_to_all | solution.py:284
  475.2 3.0 copy-start.4
  478.2 2.6 copy-start.3
Sparse Core Ops, SparseCore 0:
  10.3 50.9 all-gather.4
  63.0 27.2 all-gather.6
  95.3 62.6 all-gather.8
  159.6 31.9 all-gather.10

commit v8 on v6

--- a/solution.py
+++ b/solution.py
@@ -260,9 +260,22 @@
     peer_count = lax.axis_size("exp")
     local_experts = EXPERTS // peer_count
     row_width = normed_two.shape[1]
+    low_compact = jnp.sum(
+        low_parts.reshape(tok_rows, adapter_count, rank_size).astype(jnp.float32), axis=1
+    ).astype(jnp.bfloat16)
+    lane_pad = 128 - rank_size - 1
+    payload = jnp.concatenate(
+        [
+            normed_two,
+            low_compact,
+            token_adapter.astype(jnp.bfloat16)[:, None],
+            jnp.zeros((tok_rows, lane_pad), jnp.bfloat16),
+        ],
+        axis=1,
+    )
     send = jnp.dot(
         dispatch,
-        jnp.concatenate([normed_two, low_parts], axis=1),
+        payload,
         preferred_element_type=jnp.float32,
     ).astype(jnp.bfloat16).reshape(peer_count, local_experts, CAP, -1)
     hidden_width = expert_down.shape[1]
@@ -270,7 +283,12 @@
     def expert_chunk(chunk):
         arrived = lax.all_to_all(chunk, "exp", split_axis=0, concat_axis=0, tiled=True)
         arrived_rows = arrived[..., :row_width]
-        arrived_low = arrived[..., row_width:]
+        owner = arrived[..., row_width + rank_size : row_width + rank_size + 1]
+        arrived_low = jnp.where(
+            owner[..., None] == jnp.arange(adapter_count, dtype=jnp.int32)[:, None].astype(owner.dtype),
+            arrived[..., None, row_width : row_width + rank_size],
+            0,
+        ).reshape(arrived.shape[:-1] + (adapter_count * rank_size,))
         gate_up = jnp.einsum(
             "necd,edf->necf", arrived_rows, expert_gate_up, preferred_element_type=jnp.float32
         )

time: 489 us -> 496 us (1.014)
  the two profiles are of different devices: /device:TPU:84 before, /device:TPU:100 now
where the time goes in v8:
time: 496 us; the launch traced here: 488 us
  waiting for transfers between devices  165 us (33%)
  Pallas kernels  84.2 us (17%)
  matrix products  72.1 us (15%)
  local copies, waits for them, and re-layouts  51.4 us (10%)
  blocking collectives  45.1 us (9%)
  other arithmetic  32.6 us (7%)
  starting transfers between devices  23.2 us (5%)
  between operations  13.8 us (3%)
    pallas_call x1, Pallas kernels, window_attention(): pl.pallas_call(attention_kernel, grid_spec=grid_spec, out_shape=jax.Shape...  84.2 us
    all_gather x1, waiting for transfers between devices, gather_weights(): lax.all_gather(jnp.concatenate([attention_in] + down_cols, axis=1), axis_...  49.7 us
    all_to_all x1, blocking collectives, expert_chunk(): lax.all_to_all(chunk, 'exp', split_axis=0, concat_axis=0, tiled=True)  45.1 us
    all_to_all x2, waiting for transfers between devices, expert_chunk(): lax.all_to_all(outputs, 'exp', split_axis=0, concat_axis=0, tiled=True)  40.4 us
    all_gather x1, waiting for transfers between devices, body(): key_piece = lax.all_gather(key_value, 'exp', axis=0, tiled=True)  31.7 us
    all_to_all x1, waiting for transfers between devices, expert_chunk(): lax.all_to_all(chunk, 'exp', split_axis=0, concat_axis=0, tiled=True)  25.6 us
    dot_general x2, matrix products, expert_chunk(): jnp.einsum('necd,edf->necf', arrived_rows, expert_gate_up, preferred_elem...  22.1 us
    dot_general x2, matrix products, expert_chunk(): jnp.einsum('necf,efd->necd', hidden, expert_down, preferred_element_type=...  18.5 us
  transfers between devices with their start and end apart: 7, of which 6 were waited for; matrix products, arithmetic and copies ran while one was open for 17% of the time, Pallas kernels for 17%

profile of v8, /device:TPU:100, one launch (start us, length us, event | category | flops | bytes accessed | tf_op | source)
XLA Modules:
  0.0 487.6 jit_solution(316519758112313808)
XLA Ops:
  12.7 49.7 %all-gather.5.cloned.1.call-done = bf16[1536,2816]{0,1:T(8,128)(2,1)} async-done(((bf16[1536,352]{0,1:T(8,128)(2,1)}), bf16[1536,2816]{0,1:T(8,128)(2,1)}) %all-gather.5.cloned.1.call-update) | async-done | bytes 8650768 | tf_op jit(solution)/shard_map/all_gather | solution.py:168
  62.4 3.5 slice.104
  65.9 3.0 fusion.85
  68.8 4.3 fusion.69
  73.1 17.1 %all-gather.7.cloned.1.call-done = bf16[256,5120]{1,0:T(8,128)(2,1)} async-done(((bf16[32,5120]{1,0:T(8,128)(2,1)}), bf16[256,5120]{1,0:T(8,128)(2,1)}) %all-gather.7.cloned.1.call-update) | async-done | bytes 2621456 | tf_op jit(solution)/shard_map/all_gather | solution.py:179
  90.3 4.1 add_convert_fusion
  98.3 9.4 %reduce-window.19 = s32[32,12,128]{2,1,0:T(8,128)S(1)} reduce-window(s32[32,12,128]{2,1,0:T(8,128)S(1)} %fusion.71, s32[]{:T(128)} %constant.32.clone.1), window={size=1x1x128 pad=0_0x0_0x127_0}, to_apply=%region_7.8 | reduce-window | flops 6242304 | bytes 393220 | tf_op jit(solution)/shard_map/reduce-window.1
  109.0 3.6 broadcast_in_dim.122.init_ref
  116.5 4.9 fusion
  123.7 31.7 %all-gather.9.cloned.1.call-done.k_ref.v_ref = bf16[6144,512]{1,0:T(8,128)(2,1)} async-done(((bf16[384,512]{1,0:T(8,128)(2,1)}), bf16[6144,512]{1,0:T(8,128)(2,1)}) %all-gather.9.cloned.1.call-update) | async-done | bytes 6291472 | tf_op jit(solution)/shard_map/all_gather | solution.py:237
  155.4 84.2 %shard_map.172 = bf16[2,2304,128]{2,1,0:T(8,128)(2,1)} custom-call(s32[1]{0:T(128)} %slice.78.first_ref, s32[12]{0:T(128)} %get-tuple-element.6.bmin_ref, s32[12]{0:T(128)} %get-tuple-element.5.bmax_ref, s32[2]{0:T(128)} %pad_add_fusion.qrange_ref, bf16[2,2304,128]{2,1,0:T(8,128)(2,1)} %bitcast.125, ...), custom_call_target="tpu_custom_call" | custom-call | tf_op jit(solution)/shard_map/pallas_call | solution.py:149
  241.9 5.8 %convert_add_fusion.1 = f32[384,1536]{1,0:T(8,128)} fusion(bf16[384,1536]{1,0:T(8,128)(2,1)S(1)} %copy-done.1, bf16[384,1536]{0,1:T(8,128)(2,1)S(1)} %bitcast.128, bf16[1536,1536]{0,1:T(8,128)(2,1)} %all-gather.11.cloned.1.call-done), kind=kOutput, calls=%fused_computation.21 | convolution fusion | flops 1813118976 | bytes 9437184 | tf_op jit(solution)/shard_map/dot_general | solution.py:241
  247.7 3.4 fusion.38
  251.5 2.4 fusion.55
  257.1 5.3 %convolution_convert_fusion = bf16[2048,1664]{1,0:T(8,128)(2,1)S(1)} fusion(pred[2048,384]{1,0:T(8,128)(4,1)S(1)} %copy-done.6, bf16[384,1664]{1,0:T(8,128)(2,1)} %concatenate.14), kind=kOutput, calls=%fused_computation.8 | convolution fusion | flops 2620653568 | bytes 8880128 | tf_op jit(solution)/shard_map/dot_general | solution.py:276
  264.7 45.1 %all_to_all.20 = bf16[16,2,32,1664]{3,2,1,0:T(8,128)(2,1)S(1)} all-to-all(bf16[16,2,32,1664]{3,2,1,0:T(8,128)(2,1)S(1)} %get-tuple-element.10), channel_id=1, replica_groups=mesh['req'=8,'exp'=16] {'exp'}, dimensions={0} | all-to-all | bytes 6815744 | tf_op jit(solution)/shard_map/all_to_all | solution.py:284
  309.9 8.6 %all-to-all-start.2 = ((bf16[16,2,32,1664]{3,2,1,0:T(8,128)(2,1)}), bf16[16,2,32,1664]{3,2,1,0:T(8,128)(2,1)}, u32[]{:S(2)}, u32[]{:S(2)}) async-start(bf16[16,2,32,1664]{3,2,1,0:T(8,128)(2,1)} %get-tuple-element.11), calls=%async_computation.2 | async-start | bytes 6815744 | tf_op jit(solution)/shard_map/all_to_all | solution.py:284
  327.8 25.6 %all-to-all-done.2 = bf16[16,2,32,1664]{3,2,1,0:T(8,128)(2,1)} async-done(((bf16[16,2,32,1664]{3,2,1,0:T(8,128)(2,1)}), bf16[16,2,32,1664]{3,2,1,0:T(8,128)(2,1)}, u32[]{:S(2)}, u32[]{:S(2)}) %all-to-all-start.2) | async-done | bytes 3407904 | tf_op jit(solution)/shard_map/all_to_all | solution.py:284
  363.2 3.6 broadcast_select_fusion
  366.8 11.0 %fusion.12 = f32[16,2,32,1536]{3,2,0,1:T(8,128)} fusion(bf16[2,1536,1536]{2,1,0:T(8,128)(2,1)} %param.28, bf16[16,2,32,1664]{3,2,1,0:T(8,128)(2,1)} %all-to-all-done.2), kind=kOutput, calls=%fused_computation.15 | convolution fusion | flops 4831838208 | bytes 18874368 | tf_op jit(solution)/shard_map/necd,edf->necf/dot_general | solution.py:292
  377.8 8.4 %fusion.21 = bf16[16,2,32,1536]{3,2,0,1:T(8,128)(2,1)S(1)} fusion(bf16[2,768,1536]{2,1,0:T(8,128)(2,1)} %param.29, f32[16,2,32,1536]{3,2,0,1:T(8,128)} %fusion.12, bf16[16,2,32,256]{2,3,1,0:T(8,128)(2,1)} %bitcast.134, bf16[256,2,768]{2,0,1:T(8,128)(2,1)} %copy.208), kind=kOutput, calls=%fused_computation.24 | convolution fusion | flops 2823290880 | bytes 15466496 | tf_op jit(solution)/shard_map/necf,efd->necd/dot_general | solution.py:299
  388.2 7.5 %all-to-all-start.3 = ((bf16[16,2,32,1536]{3,2,1,0:T(8,128)(2,1)}), bf16[16,2,32,1536]{3,2,1,0:T(8,128)(2,1)S(1)}, u32[]{:S(2)}, u32[]{:S(2)}) async-start(bf16[16,2,32,1536]{3,2,1,0:T(8,128)(2,1)} %copy.219), calls=%async_computation.3 | async-start | bytes 6291456 | tf_op jit(solution)/shard_map/all_to_all | solution.py:302
  395.6 11.0 %fusion.9 = f32[16,2,32,1536]{3,2,0,1:T(8,128)} fusion(bf16[2,1536,1536]{2,1,0:T(8,128)(2,1)} %param.28, bf16[16,2,32,1664]{3,2,1,0:T(8,128)(2,1)} %copy-done.4), kind=kOutput, calls=%fused_computation.14 | convolution fusion | flops 4831838208 | bytes 18874368 | tf_op jit(solution)/shard_map/necd,edf->necf/dot_general | solution.py:292
  406.7 10.1 %fusion.24 = bf16[16,2,32,1536]{3,2,0,1:T(8,128)(2,1)} fusion(bf16[2,768,1536]{2,1,0:T(8,128)(2,1)} %param.29, f32[16,2,32,1536]{3,2,0,1:T(8,128)} %fusion.9, bf16[16,2,32,256]{2,3,1,0:T(8,128)(2,1)} %bitcast.133, bf16[256,2,768]{2,0,1:T(8,128)(2,1)} %copy.208), kind=kOutput, calls=%fused_computation.25 | convolution fusion | flops 2823290880 | bytes 15466496 | tf_op jit(solution)/shard_map/necf,efd->necd/dot_general | solution.py:299
  416.8 3.9 copy.213
  420.7 11.7 %all-to-all-done.3 = bf16[16,2,32,1536]{3,2,1,0:T(8,128)(2,1)S(1)} async-done(((bf16[16,2,32,1536]{3,2,1,0:T(8,128)(2,1)}), bf16[16,2,32,1536]{3,2,1,0:T(8,128)(2,1)S(1)}, u32[]{:S(2)}, u32[]{:S(2)}) %all-to-all-start.3) | async-done | bytes 3145760 | tf_op jit(solution)/shard_map/all_to_all | solution.py:302
  432.3 6.9 %all-to-all-start.1 = ((bf16[16,2,32,1536]{3,2,1,0:T(8,128)(2,1)}), bf16[16,2,32,1536]{3,2,1,0:T(8,128)(2,1)}, u32[]{:S(2)}, u32[]{:S(2)}) async-start(bf16[16,2,32,1536]{3,2,1,0:T(8,128)(2,1)} %copy.213), calls=%async_computation.1 | async-start | bytes 6291456 | tf_op jit(solution)/shard_map/all_to_all | solution.py:302
  439.3 3.8 select_reduce_fusion
  443.0 28.8 %all-to-all-done.1 = bf16[16,2,32,1536]{3,2,1,0:T(8,128)(2,1)} async-done(((bf16[16,2,32,1536]{3,2,1,0:T(8,128)(2,1)}), bf16[16,2,32,1536]{3,2,1,0:T(8,128)(2,1)}, u32[]{:S(2)}, u32[]{:S(2)}) %all-to-all-start.1) | async-done | bytes 3145760 | tf_op jit(solution)/shard_map/all_to_all | solution.py:302
  471.8 2.6 pad_maximum_fusion
  474.6 2.6 fusion.63
  477.2 3.7 fusion.34
  (127 shorter events, 46.5 us)
Async XLA Ops:
  6.5 3.7 copy-start.11
  6.5 3.8 copy-start.10
  6.5 3.8 copy-start.9
  6.5 55.8 %all-gather.5.cloned.1.call-start = ((), (), s32[]{:S(2)}) async-start(), calls=%async_computation.4 | async-start | bytes 9732096 | tf_op jit(solution)/shard_map/all_gather | solution.py:168
  8.0 3.2 copy-start.22
  8.0 4.2 copy-start.23
  8.0 4.3 copy-start
  10.2 80.1 %all-gather.7.cloned.1.call-start = ((), (), s32[]{:S(2)}) async-start(), calls=%async_computation.5 | async-start | bytes 2949120 | tf_op jit(solution)/shard_map/all_gather | solution.py:179
  11.2 144.2 %all-gather.9.cloned.1.call-start = ((), (), s32[]{:S(2)}) async-start(), calls=%async_computation.6 | async-start | bytes 6684672 | tf_op jit(solution)/shard_map/all_gather | solution.py:237
  11.5 50.9 %copy-start.20 = (s32[16]{0:T(128)}, s32[16]{0:T(128)S(1)}, u32[]{:S(2)}) copy-start(s32[16]{0:T(128)S(1)} %reduce.1) | copy-start | bytes 196
  12.2 50.2 %copy-start.17 = (s32[384]{0:T(512)}, s32[384]{0:T(512)S(1)}, u32[]{:S(2)}) copy-start(s32[384]{0:T(512)S(1)} %iota_add_fusion) | copy-start | bytes 4612
  12.7 56.2 %copy-start.16 = (f32[384]{0:T(512)}, f32[384]{0:T(512)S(1)}, u32[]{:S(2)}) copy-start(f32[384]{0:T(512)S(1)} %add_rsqrt_fusion.1) | copy-start | bytes 4612
  65.8 3.0 copy-start.18
  90.3 5.5 %copy-start.12 = (s32[384,4]{0,1:T(4,128)S(1)}, s32[384,4]{0,1:T(4,128)}, u32[]{:S(2)}) copy-start(s32[384,4]{0,1:T(4,128)} %param.21) | copy-start | bytes 18436
  94.3 14.3 %copy-start.21 = (s32[16]{0:T(128)S(1)}, s32[16]{0:T(128)}, u32[]{:S(2)}) copy-start(s32[16]{0:T(128)} %copy-done.20) | copy-start | bytes 196
  94.3 14.5 %copy-start.24 = (f32[12]{0:T(128)S(1)}, f32[12]{0:T(128)}, u32[]{:S(2)}) copy-start(f32[12]{0:T(128)} %param.25) | copy-start | bytes 148
  95.2 146.7 %all-gather.11.cloned.1.call-start = ((), (), s32[]{:S(2)}) async-start(), calls=%async_computation.7 | async-start | bytes 5308416 | tf_op jit(solution)/shard_map/all_gather | solution.py:232
  98.2 18.2 %copy-start.13 = (s32[384,4]{0,1:T(4,128)S(1)}, s32[384,4]{0,1:T(4,128)}, u32[]{:S(2)}) copy-start(s32[384,4]{0,1:T(4,128)} %param.21) | copy-start | bytes 18436
  108.8 7.7 %copy-start.8 = (s32[6144]{0:T(1024)}, s32[6144]{0:T(1024)S(1)}, u32[]{:S(2)}) copy-start(s32[6144]{0:T(1024)S(1)} %convert_reduce_fusion) | copy-start | bytes 73732
  155.4 86.5 %copy-start.1 = (bf16[384,1536]{1,0:T(8,128)(2,1)S(1)}, bf16[384,1536]{1,0:T(8,128)(2,1)}, u32[]{:S(2)}) copy-start(bf16[384,1536]{1,0:T(8,128)(2,1)} %param.18) | copy-start | bytes 3538948
  241.9 5.8 %copy-start.14 = (s32[256]{0:T(256)S(1)}, s32[256]{0:T(256)}, u32[]{:S(2)}) copy-start(s32[256]{0:T(256)} %eq.123) | copy-start | bytes 3076
  247.7 3.5 copy-start.15
  251.1 3.9 copy-start.2
  251.2 4.1 copy-start.7
  251.5 5.6 %copy-start.6 = (pred[2048,384]{1,0:T(8,128)(4,1)S(1)}, pred[2048,384]{1,0:T(8,128)(4,1)}, u32[]{:S(2)}) copy-start(pred[2048,384]{1,0:T(8,128)(4,1)} %fusion) | copy-start | bytes 2359300
  309.9 56.9 %copy-start.4 = (bf16[16,2,32,1664]{3,2,1,0:T(8,128)(2,1)}, bf16[16,2,32,1664]{3,2,1,0:T(8,128)(2,1)S(1)}, u32[]{:S(2)}) copy-start(bf16[16,2,32,1664]{3,2,1,0:T(8,128)(2,1)S(1)} %all_to_all.20) | copy-start | bytes 10223620
  309.9 43.5 %all-to-all-start.2 = ((bf16[16,2,32,1664]{3,2,1,0:T(8,128)(2,1)}), bf16[16,2,32,1664]{3,2,1,0:T(8,128)(2,1)}, u32[]{:S(2)}, u32[]{:S(2)}) async-start(bf16[16,2,32,1664]{3,2,1,0:T(8,128)(2,1)} %get-tuple-element.11), calls=%async_computation.2 | async-start | bytes 6815744 | tf_op jit(solution)/shard_map/all_to_all | solution.py:284
  388.2 44.2 %all-to-all-start.3 = ((bf16[16,2,32,1536]{3,2,1,0:T(8,128)(2,1)}), bf16[16,2,32,1536]{3,2,1,0:T(8,128)(2,1)S(1)}, u32[]{:S(2)}, u32[]{:S(2)}) async-start(bf16[16,2,32,1536]{3,2,1,0:T(8,128)(2,1)} %copy.219), calls=%async_computation.3 | async-start | bytes 6291456 | tf_op jit(solution)/shard_map/all_to_all | solution.py:302
  420.7 18.6 %copy-start.19 = (f32[384,4]{0,1:T(4,128)S(1)}, f32[384,4]{0,1:T(4,128)}, u32[]{:S(2)}) copy-start(f32[384,4]{0,1:T(4,128)} %param.22) | copy-start | bytes 18436
  432.3 39.5 %all-to-all-start.1 = ((bf16[16,2,32,1536]{3,2,1,0:T(8,128)(2,1)}), bf16[16,2,32,1536]{3,2,1,0:T(8,128)(2,1)}, u32[]{:S(2)}, u32[]{:S(2)}) async-start(bf16[16,2,32,1536]{3,2,1,0:T(8,128)(2,1)} %copy.213), calls=%async_computation.1 | async-start | bytes 6291456 | tf_op jit(solution)/shard_map/all_to_all | solution.py:302
  471.8 2.8 copy-start.5
  474.6 2.6 copy-start.3
Sparse Core Ops, SparseCore 0:
  10.3 52.0 all-gather.4
  64.0 26.1 all-gather.6
  95.3 60.0 all-gather.8
  156.9 35.6 all-gather.10

commit v9 on v6

--- a/solution.py
+++ b/solution.py
@@ -43,7 +43,7 @@
     return jnp.dot(coords, second, preferred_element_type=jnp.float32)
 
 
-KEY_BLOCK = 512
+KEY_BLOCK = 256
 
 
 def attention_kernel(first_ref, bmin_ref, bmax_ref, qrange_ref, q_ref, k_ref, v_ref, qseg_ref,

time: 489 us -> 511 us (1.045)
  the two profiles are of different devices: /device:TPU:84 before, /device:TPU:100 now
where the time goes in v9:
time: 511 us; the launch traced here: 502 us
  waiting for transfers between devices  145 us (28%)
  Pallas kernels  141 us (28%)
  matrix products  68.9 us (13%)
  blocking collectives  39.7 us (8%)
  starting transfers between devices  33.7 us (7%)
  local copies, waits for them, and re-layouts  32.3 us (6%)
  other arithmetic  27.6 us (5%)
  between operations  13.7 us (3%)
    pallas_call x1, Pallas kernels, window_attention(): pl.pallas_call(attention_kernel, grid_spec=grid_spec, out_shape=jax.Shape...  141 us
    all_gather x1, waiting for transfers between devices, gather_weights(): lax.all_gather(jnp.concatenate([attention_in] + down_cols, axis=1), axis_...  49.3 us
    all_to_all x1, blocking collectives, expert_chunk(): lax.all_to_all(chunk, 'exp', split_axis=0, concat_axis=0, tiled=True)  39.7 us
    all_to_all x2, waiting for transfers between devices, expert_chunk(): lax.all_to_all(outputs, 'exp', split_axis=0, concat_axis=0, tiled=True)  32.2 us
    all_gather x1, waiting for transfers between devices, body(): key_piece = lax.all_gather(key_value, 'exp', axis=0, tiled=True)  31.6 us
    dot_general x2, matrix products, expert_chunk(): jnp.einsum('necd,edf->necf', arrived_rows, expert_gate_up, preferred_elem...  22.1 us
    all_to_all x2, starting transfers between devices, expert_chunk(): lax.all_to_all(outputs, 'exp', split_axis=0, concat_axis=0, tiled=True)  21.6 us
    all_gather x1, waiting for transfers between devices, gather_weights(): lax.all_gather(jnp.concatenate(up_rows, axis=1), axis_name, axis=0, tiled...  17.1 us
  transfers between devices with their start and end apart: 7, of which 6 were waited for; matrix products, arithmetic and copies ran while one was open for 18% of the time, Pallas kernels for 28%

profile of v9, /device:TPU:100, one launch (start us, length us, event | category | flops | bytes accessed | tf_op | source)
XLA Modules:
  0.0 502.2 jit_solution(4728348537510599982)
XLA Ops:
  8.1 2.0 pad_maximum_fusion.1
  13.1 49.3 %all-gather.5.cloned.1.call-done = bf16[1536,2816]{0,1:T(8,128)(2,1)} async-done(((bf16[1536,352]{0,1:T(8,128)(2,1)}), bf16[1536,2816]{0,1:T(8,128)(2,1)}) %all-gather.5.cloned.1.call-update) | async-done | bytes 8650768 | tf_op jit(solution)/shard_map/all_gather | solution.py:168
  62.4 3.5 slice.96
  65.9 3.0 fusion.81
  68.8 4.3 fusion.64
  73.1 17.1 %all-gather.7.cloned.1.call-done = bf16[256,5120]{1,0:T(8,128)(2,1)} async-done(((bf16[32,5120]{1,0:T(8,128)(2,1)}), bf16[256,5120]{1,0:T(8,128)(2,1)}) %all-gather.7.cloned.1.call-update) | async-done | bytes 2621456 | tf_op jit(solution)/shard_map/all_gather | solution.py:179
  90.3 4.1 add_convert_fusion
  99.7 3.7 broadcast_in_dim.73.init_ref
  103.5 9.1 %reduce-window.19 = s32[32,12,128]{2,1,0:T(8,128)S(1)} reduce-window(s32[32,12,128]{2,1,0:T(8,128)S(1)} %fusion.66, s32[]{:T(128)} %constant.16.clone.1), window={size=1x1x128 pad=0_0x0_0x127_0}, to_apply=%region_7.8 | reduce-window | flops 6242304 | bytes 393220 | tf_op jit(solution)/shard_map/reduce-window.1
  116.7 4.8 fusion
  123.8 31.6 %all-gather.9.cloned.1.call-done.k_ref.v_ref = bf16[6144,512]{1,0:T(8,128)(2,1)} async-done(((bf16[384,512]{1,0:T(8,128)(2,1)}), bf16[6144,512]{1,0:T(8,128)(2,1)}) %all-gather.9.cloned.1.call-update) | async-done | bytes 6291472 | tf_op jit(solution)/shard_map/all_gather | solution.py:237
  155.4 140.8 %shard_map.172 = bf16[2,2304,128]{2,1,0:T(8,128)(2,1)} custom-call(s32[1]{0:T(128)} %slice.72.first_ref, s32[24]{0:T(128)} %get-tuple-element.6.bmin_ref, s32[24]{0:T(128)} %get-tuple-element.5.bmax_ref, s32[2]{0:T(128)} %pad_add_fusion.qrange_ref, bf16[2,2304,128]{2,1,0:T(8,128)(2,1)} %bitcast.119, ...), custom_call_target="tpu_custom_call" | custom-call | tf_op jit(solution)/shard_map/pallas_call | solution.py:149
  298.2 5.8 %convert_add_fusion.1 = f32[384,1536]{1,0:T(8,128)} fusion(bf16[384,1536]{1,0:T(8,128)(2,1)S(1)} %copy-done.1, bf16[384,1536]{0,1:T(8,128)(2,1)S(1)} %bitcast.122, bf16[1536,1536]{0,1:T(8,128)(2,1)} %all-gather.11.cloned.1.call-done), kind=kOutput, calls=%fused_computation.21 | convolution fusion | flops 1813118976 | bytes 9437184 | tf_op jit(solution)/shard_map/dot_general | solution.py:241
  304.0 3.4 fusion.38
  309.8 4.1 convolution_convert_fusion
  313.9 2.4 fusion.82
  316.3 39.7 %all_to_all.20 = bf16[16,2,32,1792]{3,2,1,0:T(8,128)(2,1)} all-to-all(bf16[16,2,32,1792]{3,2,1,0:T(8,128)(2,1)S(1)} %get-tuple-element.10), channel_id=1, replica_groups=mesh['req'=8,'exp'=16] {'exp'}, dimensions={0} | all-to-all | bytes 7340032 | tf_op jit(solution)/shard_map/all_to_all | solution.py:271
  356.0 11.5 %all-to-all-start.2 = ((bf16[16,2,32,1792]{3,2,1,0:T(8,128)(2,1)}), bf16[16,2,32,1792]{3,2,1,0:T(8,128)(2,1)}, u32[]{:S(2)}, u32[]{:S(2)}) async-start(bf16[16,2,32,1792]{3,2,1,0:T(8,128)(2,1)} %get-tuple-element.11), calls=%async_computation.2 | async-start | bytes 7340032 | tf_op jit(solution)/shard_map/all_to_all | solution.py:271
  368.9 11.0 %fusion.9 = f32[16,2,32,1536]{3,2,0,1:T(8,128)} fusion(bf16[2,1536,1536]{2,1,0:T(8,128)(2,1)} %param.28, bf16[16,2,32,1792]{3,2,1,0:T(8,128)(2,1)} %all_to_all.20), kind=kOutput, calls=%fused_computation.14 | convolution fusion | flops 4831838208 | bytes 18874368 | tf_op jit(solution)/shard_map/necd,edf->necf/dot_general | solution.py:274
  379.9 7.7 %fusion.24 = bf16[16,2,32,1536]{3,2,0,1:T(8,128)(2,1)S(1)} fusion(bf16[2,768,1536]{2,1,0:T(8,128)(2,1)} %param.29, f32[16,2,32,1536]{3,2,0,1:T(8,128)} %fusion.9, bf16[256,2,768]{2,0,1:T(8,128)(2,1)} %copy.160, bf16[16,2,32,1792]{3,2,1,0:T(8,128)(2,1)} %all_to_all.20), kind=kOutput, calls=%fused_computation.25 | convolution fusion | flops 2823290880 | bytes 15466496 | tf_op jit(solution)/shard_map/necf,efd->necd/dot_general | solution.py:281
  389.4 15.1 %all-to-all-done.2 = bf16[16,2,32,1792]{3,2,1,0:T(8,128)(2,1)} async-done(((bf16[16,2,32,1792]{3,2,1,0:T(8,128)(2,1)}), bf16[16,2,32,1792]{3,2,1,0:T(8,128)(2,1)}, u32[]{:S(2)}, u32[]{:S(2)}) %all-to-all-start.2) | async-done | bytes 3670048 | tf_op jit(solution)/shard_map/all_to_all | solution.py:271
  404.5 12.0 %all-to-all-start.1 = ((bf16[16,2,32,1536]{3,2,1,0:T(8,128)(2,1)}), bf16[16,2,32,1536]{3,2,1,0:T(8,128)(2,1)S(1)}, u32[]{:S(2)}, u32[]{:S(2)}) async-start(bf16[16,2,32,1536]{3,2,1,0:T(8,128)(2,1)} %copy.162), calls=%async_computation.1 | async-start | bytes 6291456 | tf_op jit(solution)/shard_map/all_to_all | solution.py:284
  416.5 11.0 %fusion.12 = f32[16,2,32,1536]{3,2,0,1:T(8,128)} fusion(bf16[2,1536,1536]{2,1,0:T(8,128)(2,1)} %param.28, bf16[16,2,32,1792]{3,2,1,0:T(8,128)(2,1)} %all-to-all-done.2), kind=kOutput, calls=%fused_computation.15 | convolution fusion | flops 4831838208 | bytes 18874368 | tf_op jit(solution)/shard_map/necd,edf->necf/dot_general | solution.py:274
  427.5 9.3 %fusion.21 = bf16[16,2,32,1536]{3,2,0,1:T(8,128)(2,1)} fusion(bf16[2,768,1536]{2,1,0:T(8,128)(2,1)} %param.29, f32[16,2,32,1536]{3,2,0,1:T(8,128)} %fusion.12, bf16[256,2,768]{2,0,1:T(8,128)(2,1)} %copy.160, bf16[16,2,32,1792]{3,2,1,0:T(8,128)(2,1)} %all-to-all-done.2), kind=kOutput, calls=%fused_computation.24 | convolution fusion | flops 2823290880 | bytes 15466496 | tf_op jit(solution)/shard_map/necf,efd->necd/dot_general | solution.py:281
  436.9 3.9 copy.165
  440.8 12.5 %all-to-all-done.1 = bf16[16,2,32,1536]{3,2,1,0:T(8,128)(2,1)S(1)} async-done(((bf16[16,2,32,1536]{3,2,1,0:T(8,128)(2,1)}), bf16[16,2,32,1536]{3,2,1,0:T(8,128)(2,1)S(1)}, u32[]{:S(2)}, u32[]{:S(2)}) %all-to-all-start.1) | async-done | bytes 3145760 | tf_op jit(solution)/shard_map/all_to_all | solution.py:284
  453.2 9.6 %all-to-all-start.3 = ((bf16[16,2,32,1536]{3,2,1,0:T(8,128)(2,1)}), bf16[16,2,32,1536]{3,2,1,0:T(8,128)(2,1)}, u32[]{:S(2)}, u32[]{:S(2)}) async-start(bf16[16,2,32,1536]{3,2,1,0:T(8,128)(2,1)} %copy.165), calls=%async_computation.3 | async-start | bytes 6291456 | tf_op jit(solution)/shard_map/all_to_all | solution.py:284
  462.9 3.8 select_reduce_fusion
  466.7 19.7 %all-to-all-done.3 = bf16[16,2,32,1536]{3,2,1,0:T(8,128)(2,1)} async-done(((bf16[16,2,32,1536]{3,2,1,0:T(8,128)(2,1)}), bf16[16,2,32,1536]{3,2,1,0:T(8,128)(2,1)}, u32[]{:S(2)}, u32[]{:S(2)}) %all-to-all-start.3) | async-done | bytes 3145760 | tf_op jit(solution)/shard_map/all_to_all | solution.py:284
  486.4 2.6 pad_maximum_fusion
  489.2 2.6 fusion.54
  491.8 3.7 fusion.34
  (102 shorter events, 23.8 us)
Async XLA Ops:
  6.5 3.7 copy-start.9
  6.5 3.8 copy-start.7
  6.5 3.8 copy-start.8
  6.5 4.7 copy-start.20
  6.5 6.1 %copy-start.21 = (s32[1,16]{1,0:T(1,128)S(1)}, s32[1,16]{1,0:T(1,128)}, u32[]{:S(2)}) copy-start(s32[1,16]{1,0:T(1,128)} %param.20) | copy-start | bytes 196
  6.5 6.2 %copy-start = (bf16[384,1536]{1,0:T(8,128)(2,1)S(1)}, bf16[384,1536]{1,0:T(8,128)(2,1)}, u32[]{:S(2)}) copy-start(bf16[384,1536]{1,0:T(8,128)(2,1)} %param.18) | copy-start | bytes 3538948
  6.6 55.8 %all-gather.5.cloned.1.call-start = ((), (), s32[]{:S(2)}) async-start(), calls=%async_computation.4 | async-start | bytes 9732096 | tf_op jit(solution)/shard_map/all_gather | solution.py:168
  10.2 80.1 %all-gather.7.cloned.1.call-start = ((), (), s32[]{:S(2)}) async-start(), calls=%async_computation.5 | async-start | bytes 2949120 | tf_op jit(solution)/shard_map/all_gather | solution.py:179
  11.2 144.3 %all-gather.9.cloned.1.call-start = ((), (), s32[]{:S(2)}) async-start(), calls=%async_computation.6 | async-start | bytes 6684672 | tf_op jit(solution)/shard_map/all_gather | solution.py:237
  11.5 50.9 %copy-start.19 = (s32[16]{0:T(128)}, s32[16]{0:T(128)S(1)}, u32[]{:S(2)}) copy-start(s32[16]{0:T(128)S(1)} %reduce) | copy-start | bytes 196
  12.1 0.5 copy-start.16
  12.7 77.5 %copy-start.11 = (s32[384]{0:T(512)}, s32[384]{0:T(512)S(1)}, u32[]{:S(2)}) copy-start(s32[384]{0:T(512)S(1)} %select_reduce_fusion.1) | copy-start | bytes 4612
  13.1 55.8 %copy-start.15 = (f32[384]{0:T(512)}, f32[384]{0:T(512)S(1)}, u32[]{:S(2)}) copy-start(f32[384]{0:T(512)S(1)} %add_rsqrt_fusion.1) | copy-start | bytes 4612
  65.9 3.0 copy-start.17
  90.3 7.5 %copy-start.10 = (s32[384,4]{0,1:T(4,128)S(1)}, s32[384,4]{0,1:T(4,128)}, u32[]{:S(2)}) copy-start(s32[384,4]{0,1:T(4,128)} %param.21) | copy-start | bytes 18436
  95.2 203.0 %all-gather.11.cloned.1.call-start = ((), (), s32[]{:S(2)}) async-start(), calls=%async_computation.7 | async-start | bytes 5308416 | tf_op jit(solution)/shard_map/all_gather | solution.py:232
  98.9 4.6 copy-start.6
  155.4 142.7 %copy-start.1 = (bf16[384,1536]{1,0:T(8,128)(2,1)S(1)}, bf16[384,1536]{1,0:T(8,128)(2,1)}, u32[]{:S(2)}) copy-start(bf16[384,1536]{1,0:T(8,128)(2,1)} %param.18) | copy-start | bytes 3538948
  298.2 5.8 %copy-start.12 = (s32[384]{0:T(512)S(1)}, s32[384]{0:T(512)}, u32[]{:S(2)}) copy-start(s32[384]{0:T(512)} %copy-done.11) | copy-start | bytes 4612
  298.2 5.8 %copy-start.13 = (s32[256]{0:T(256)S(1)}, s32[256]{0:T(256)}, u32[]{:S(2)}) copy-start(s32[256]{0:T(256)} %eq.83) | copy-start | bytes 3076
  304.0 3.5 copy-start.14
  307.4 6.5 %copy-start.2 = (bf16[384,1536]{1,0:T(8,128)(2,1)}, bf16[384,1536]{1,0:T(8,128)(2,1)S(1)}, u32[]{:S(2)}) copy-start(bf16[384,1536]{1,0:T(8,128)(2,1)S(1)} %get-tuple-element.15) | copy-start | bytes 3538948
  307.4 2.3 copy-start.5
  356.0 11.5 %slice-start = ((bf16[256,5120]{1,0:T(8,128)(2,1)}), bf16[256,1536]{1,0:T(8,128)(2,1)S(1)}, s32[]{:S(2)}) async-start(bf16[256,5120]{1,0:T(8,128)(2,1)} %all-gather.7.cloned.1.call-done), calls=%async_computation.8 | async-start | bytes 1572864 | tf_op jit(solution)/shard_map/slice | solution.py:183
  356.0 48.6 %all-to-all-start.2 = ((bf16[16,2,32,1792]{3,2,1,0:T(8,128)(2,1)}), bf16[16,2,32,1792]{3,2,1,0:T(8,128)(2,1)}, u32[]{:S(2)}, u32[]{:S(2)}) async-start(bf16[16,2,32,1792]{3,2,1,0:T(8,128)(2,1)} %get-tuple-element.11), calls=%async_computation.2 | async-start | bytes 7340032 | tf_op jit(solution)/shard_map/all_to_all | solution.py:271
  404.5 48.7 %all-to-all-start.1 = ((bf16[16,2,32,1536]{3,2,1,0:T(8,128)(2,1)}), bf16[16,2,32,1536]{3,2,1,0:T(8,128)(2,1)S(1)}, u32[]{:S(2)}, u32[]{:S(2)}) async-start(bf16[16,2,32,1536]{3,2,1,0:T(8,128)(2,1)} %copy.162), calls=%async_computation.1 | async-start | bytes 6291456 | tf_op jit(solution)/shard_map/all_to_all | solution.py:284
  440.8 22.1 %copy-start.18 = (f32[384,4]{0,1:T(4,128)S(1)}, f32[384,4]{0,1:T(4,128)}, u32[]{:S(2)}) copy-start(f32[384,4]{0,1:T(4,128)} %param.22) | copy-start | bytes 18436
  453.2 33.1 %all-to-all-start.3 = ((bf16[16,2,32,1536]{3,2,1,0:T(8,128)(2,1)}), bf16[16,2,32,1536]{3,2,1,0:T(8,128)(2,1)}, u32[]{:S(2)}, u32[]{:S(2)}) async-start(bf16[16,2,32,1536]{3,2,1,0:T(8,128)(2,1)} %copy.165), calls=%async_computation.3 | async-start | bytes 6291456 | tf_op jit(solution)/shard_map/all_to_all | solution.py:284
  486.4 2.8 copy-start.4
  489.2 2.6 copy-start.3
Sparse Core Ops, SparseCore 0:
  10.3 52.0 all-gather.4
  64.1 26.1 all-gather.6
  95.3 60.0 all-gather.8
  157.0 35.6 all-gather.10

commit v10 on v6

--- a/solution.py
+++ b/solution.py
@@ -267,25 +267,33 @@
     ).astype(jnp.bfloat16).reshape(peer_count, local_experts, CAP, -1)
     hidden_width = expert_down.shape[1]
 
-    def expert_chunk(chunk):
+    def expert_chunk(chunk, gate_up_weights, bank, down_weights):
         arrived = lax.all_to_all(chunk, "exp", split_axis=0, concat_axis=0, tiled=True)
         arrived_rows = arrived[..., :row_width]
         arrived_low = arrived[..., row_width:]
         gate_up = jnp.einsum(
-            "necd,edf->necf", arrived_rows, expert_gate_up, preferred_element_type=jnp.float32
+            "necd,edf->necf", arrived_rows, gate_up_weights, preferred_element_type=jnp.float32
         )
         up_part = gate_up[..., hidden_width:] + jnp.einsum(
-            "necr,erf->necf", arrived_low, adapter_bank, preferred_element_type=jnp.float32
+            "necr,erf->necf", arrived_low, bank, preferred_element_type=jnp.float32
         )
         hidden = (jax.nn.relu(gate_up[..., :hidden_width]) * up_part).astype(jnp.bfloat16)
         outputs = jnp.einsum(
-            "necf,efd->necd", hidden, expert_down, preferred_element_type=jnp.float32
+            "necf,efd->necd", hidden, down_weights, preferred_element_type=jnp.float32
         ).astype(jnp.bfloat16)
         return lax.all_to_all(outputs, "exp", split_axis=0, concat_axis=0, tiled=True)
 
-    half = CAP // 2
     returned = jnp.concatenate(
-        [expert_chunk(send[:, :, :half]), expert_chunk(send[:, :, half:])], axis=2
+        [
+            expert_chunk(
+                send[:, e : e + 1],
+                expert_gate_up[e : e + 1],
+                adapter_bank[e : e + 1],
+                expert_down[e : e + 1],
+            )
+            for e in range(local_experts)
+        ],
+        axis=1,
     )
     flat_back = returned.reshape(EXPERTS * CAP, -1)
     gate_grid = jnp.sum(

time: 489 us -> 476 us (0.973)
  the two profiles are of different devices: /device:TPU:84 before, /device:TPU:8 now
where the time goes in v10:
time: 476 us; the launch traced here: 470 us
  waiting for transfers between devices  201 us (42%)
  blocking collectives  102 us (21%)
  matrix products  66.5 us (14%)
  other arithmetic  28.2 us (6%)
  local copies, waits for them, and re-layouts  25.9 us (5%)
  Pallas kernels  18.4 us (4%)
  starting transfers between devices  14.5 us (3%)
  between operations  13.7 us (3%)
    all_to_all x1, blocking collectives, expert_chunk(): lax.all_to_all(chunk, 'exp', split_axis=0, concat_axis=0, tiled=True)  102 us
    all_to_all x2, waiting for transfers between devices, expert_chunk(): lax.all_to_all(outputs, 'exp', split_axis=0, concat_axis=0, tiled=True)  57.5 us
    all_gather x1, waiting for transfers between devices, gather_weights(): lax.all_gather(jnp.concatenate([attention_in] + down_cols, axis=1), axis_...  49.5 us
    all_gather x1, waiting for transfers between devices, body(): key_piece = lax.all_gather(key_value, 'exp', axis=0, tiled=True)  33.6 us
    all_to_all x1, waiting for transfers between devices, expert_chunk(): lax.all_to_all(chunk, 'exp', split_axis=0, concat_axis=0, tiled=True)  28.5 us
    dot_general x2, matrix products, expert_chunk(): jnp.einsum('necd,edf->necf', arrived_rows, gate_up_weights, preferred_ele...  19.8 us
    pallas_call x1, Pallas kernels, window_attention(): pl.pallas_call(attention_kernel, grid_spec=grid_spec, out_shape=jax.Shape...  18.4 us
    all_gather x1, waiting for transfers between devices, gather_weights(): lax.all_gather(jnp.concatenate(up_rows, axis=1), axis_name, axis=0, tiled...  17.2 us
  transfers between devices with their start and end apart: 7, of which 7 were waited for; matrix products, arithmetic and copies ran while one was open for 18% of the time, Pallas kernels for 4%

profile of v10, /device:TPU:8, one launch (start us, length us, event | category | flops | bytes accessed | tf_op | source)
XLA Modules:
  0.0 470.1 jit_solution(10644753291680362299)
XLA Ops:
  8.1 2.0 pad_maximum_fusion.1
  13.1 49.5 %all-gather.5.cloned.1.call-done = bf16[1536,2816]{0,1:T(8,128)(2,1)} async-done(((bf16[1536,352]{0,1:T(8,128)(2,1)}), bf16[1536,2816]{0,1:T(8,128)(2,1)}) %all-gather.5.cloned.1.call-update) | async-done | bytes 8650768 | tf_op jit(solution)/shard_map/all_gather | solution.py:168
  62.6 3.5 slice.120
  66.1 3.0 fusion.65
  69.1 4.3 fusion.48
  73.4 17.2 %all-gather.7.cloned.1.call-done = bf16[256,5120]{1,0:T(8,128)(2,1)} async-done(((bf16[32,5120]{1,0:T(8,128)(2,1)}), bf16[256,5120]{1,0:T(8,128)(2,1)}) %all-gather.7.cloned.1.call-update) | async-done | bytes 2621456 | tf_op jit(solution)/shard_map/all_gather | solution.py:179
  90.5 4.1 add_convert_fusion
  100.0 3.7 broadcast_in_dim.73.init_ref
  103.8 9.5 %reduce-window.19 = s32[32,12,128]{2,1,0:T(8,128)S(1)} reduce-window(s32[32,12,128]{2,1,0:T(8,128)S(1)} %fusion.50, s32[]{:T(128)} %constant.16.clone.1), window={size=1x1x128 pad=0_0x0_0x127_0}, to_apply=%region_7.8 | reduce-window | flops 6242304 | bytes 393220 | tf_op jit(solution)/shard_map/reduce-window.1
  117.6 4.9 %fusion = pred[2048,384]{1,0:T(8,128)(4,1)} fusion(s32[384,4]{0,1:T(4,128)S(1)} %multiply_add_fusion), kind=kLoop, calls=%fused_computation.3 | loop fusion | flops 5505024 | bytes 792576 | tf_op jit(solution)/shard_map/reduce_or | solution.py:257
  124.7 33.6 %all-gather.9.cloned.1.call-done.k_ref.v_ref = bf16[6144,512]{1,0:T(8,128)(2,1)} async-done(((bf16[384,512]{1,0:T(8,128)(2,1)}), bf16[6144,512]{1,0:T(8,128)(2,1)}) %all-gather.9.cloned.1.call-update) | async-done | bytes 6291472 | tf_op jit(solution)/shard_map/all_gather | solution.py:237
  158.3 18.4 %shard_map.172 = bf16[2,2304,128]{2,1,0:T(8,128)(2,1)} custom-call(s32[1]{0:T(128)} %slice.90.first_ref, s32[12]{0:T(128)} %get-tuple-element.6.bmin_ref, s32[12]{0:T(128)} %get-tuple-element.5.bmax_ref, s32[2]{0:T(128)} %pad_add_fusion.qrange_ref, bf16[2,2304,128]{2,1,0:T(8,128)(2,1)} %bitcast.165, ...), custom_call_target="tpu_custom_call" | custom-call | tf_op jit(solution)/shard_map/pallas_call | solution.py:149
  178.6 14.1 %all-gather.11.cloned.1.call-done = bf16[1536,1536]{0,1:T(8,128)(2,1)} async-done(((bf16[1536,192]{0,1:T(8,128)(2,1)}), bf16[1536,1536]{0,1:T(8,128)(2,1)}) %all-gather.11.cloned.1.call-update) | async-done | bytes 4718608 | tf_op jit(solution)/shard_map/all_gather | solution.py:232
  192.8 5.8 %convert_add_fusion.1 = f32[384,1536]{1,0:T(8,128)} fusion(bf16[384,1536]{1,0:T(8,128)(2,1)S(1)} %copy-done.1, bf16[384,1536]{0,1:T(8,128)(2,1)S(1)} %bitcast.168, bf16[1536,1536]{0,1:T(8,128)(2,1)} %all-gather.11.cloned.1.call-done), kind=kOutput, calls=%fused_computation.19 | convolution fusion | flops 1813118976 | bytes 9437184 | tf_op jit(solution)/shard_map/dot_general | solution.py:241
  198.6 3.4 fusion.24
  204.3 4.1 convolution_convert_fusion
  208.5 2.5 fusion.66
  211.0 101.8 %all_to_all.20 = bf16[16,1,64,1792]{3,2,1,0:T(8,128)(2,1)} all-to-all(bf16[16,1,64,1792]{3,2,1,0:T(8,128)(2,1)S(1)} %get-tuple-element.10), channel_id=1, replica_groups=mesh['req'=8,'exp'=16] {'exp'}, dimensions={0} | all-to-all | bytes 7340032 | tf_op jit(solution)/shard_map/all_to_all | solution.py:271
  312.8 4.6 all-to-all-start.2
  318.0 10.0 %fusion.7 = f32[16,1,64,1536]{3,2,0,1:T(8,128)} fusion(bf16[2,1536,1536]{2,1,0:T(8,128)(2,1)} %param.28, bf16[16,1,64,1792]{3,2,0,1:T(8,128)(2,1)} %bitcast.170), kind=kOutput, calls=%fused_computation.12 | convolution fusion | flops 4831838208 | bytes 14155776 | tf_op jit(solution)/shard_map/necd,edf->necf/dot_general | solution.py:274
  328.0 8.4 %fusion.13 = bf16[16,1,64,1536]{3,2,1,0:T(8,128)(2,1)} fusion(bf16[2,768,1536]{2,1,0:T(8,128)(2,1)} %param.29, f32[16,1,64,1536]{3,2,0,1:T(8,128)} %fusion.7, bf16[16,1,64,1792]{3,2,0,1:T(8,128)(2,1)} %bitcast.171, bf16[2,256,768]{2,1,0:T(8,128)(2,1)S(1)} %bitcast.177), kind=kOutput, calls=%fused_computation.22 | convolution fusion | flops 2823290880 | bytes 12713984 | tf_op jit(solution)/shard_map/necf,efd->necd/dot_general | solution.py:281
  336.4 28.5 %all-to-all-done.2 = bf16[16,1,64,1792]{3,2,1,0:T(8,128)(2,1)} async-done(((bf16[16,1,64,1792]{3,2,1,0:T(8,128)(2,1)}), bf16[16,1,64,1792]{3,2,1,0:T(8,128)(2,1)}, u32[]{:S(2)}, u32[]{:S(2)}) %all-to-all-start.2) | async-done | bytes 3670048 | tf_op jit(solution)/shard_map/all_to_all | solution.py:271
  364.9 4.2 all-to-all-start.1
  369.1 9.7 %fusion.10 = f32[16,1,64,1536]{3,2,0,1:T(8,128)} fusion(bf16[2,1536,1536]{2,1,0:T(8,128)(2,1)} %param.28, bf16[16,1,64,1792]{3,2,0,1:T(8,128)(2,1)} %bitcast.51), kind=kOutput, calls=%fused_computation.13 | convolution fusion | flops 4831838208 | bytes 14155776 | tf_op jit(solution)/shard_map/necd,edf->necf/dot_general | solution.py:274
  378.8 8.5 %fusion.14 = bf16[16,1,64,1536]{3,2,1,0:T(8,128)(2,1)} fusion(bf16[2,768,1536]{2,1,0:T(8,128)(2,1)} %param.29, f32[16,1,64,1536]{3,2,0,1:T(8,128)} %fusion.10, bf16[16,1,64,1792]{3,2,0,1:T(8,128)(2,1)} %bitcast.51, bf16[2,256,768]{2,1,0:T(8,128)(2,1)} %bitcast.178), kind=kOutput, calls=%fused_computation.23 | convolution fusion | flops 2823290880 | bytes 12713984 | tf_op jit(solution)/shard_map/necf,efd->necd/dot_general | solution.py:281
  387.4 19.4 %all-to-all-done.1 = bf16[16,1,64,1536]{3,2,1,0:T(8,128)(2,1)S(1)} async-done(((bf16[16,1,64,1536]{3,2,1,0:T(8,128)(2,1)}), bf16[16,1,64,1536]{3,2,1,0:T(8,128)(2,1)S(1)}, u32[]{:S(2)}, u32[]{:S(2)}) %all-to-all-start.1) | async-done | bytes 3145760 | tf_op jit(solution)/shard_map/all_to_all | solution.py:284
  406.8 5.6 %all-to-all-start.3 = ((bf16[16,1,64,1536]{3,2,1,0:T(8,128)(2,1)}), bf16[16,1,64,1536]{3,2,1,0:T(8,128)(2,1)}, u32[]{:S(2)}, u32[]{:S(2)}) async-start(bf16[16,1,64,1536]{3,2,1,0:T(8,128)(2,1)} %fusion.14), calls=%async_computation.3 | async-start | bytes 6291456 | tf_op jit(solution)/shard_map/all_to_all | solution.py:284
  412.4 3.8 select_reduce_fusion
  416.2 38.1 %all-to-all-done.3 = bf16[16,1,64,1536]{3,2,1,0:T(8,128)(2,1)} async-done(((bf16[16,1,64,1536]{3,2,1,0:T(8,128)(2,1)}), bf16[16,1,64,1536]{3,2,1,0:T(8,128)(2,1)}, u32[]{:S(2)}, u32[]{:S(2)}) %all-to-all-start.3) | async-done | bytes 3145760 | tf_op jit(solution)/shard_map/all_to_all | solution.py:284
  454.3 2.6 pad_maximum_fusion
  457.1 2.6 fusion.42
  459.7 3.7 fusion.20
  (102 shorter events, 21.3 us)
Async XLA Ops:
  6.5 3.7 copy-start.10
  6.5 3.8 copy-start.8
  6.5 3.8 copy-start.9
  6.5 4.7 %copy-start.21 = (s32[1,16]{1,0:T(1,128)S(1)}, s32[1,16]{1,0:T(1,128)}, u32[]{:S(2)}) copy-start(s32[1,16]{1,0:T(1,128)} %param.19) | copy-start | bytes 196
  6.5 6.2 %copy-start.22 = (s32[1,16]{1,0:T(1,128)S(1)}, s32[1,16]{1,0:T(1,128)}, u32[]{:S(2)}) copy-start(s32[1,16]{1,0:T(1,128)} %param.20) | copy-start | bytes 196
  6.5 6.3 %copy-start = (bf16[384,1536]{1,0:T(8,128)(2,1)S(1)}, bf16[384,1536]{1,0:T(8,128)(2,1)}, u32[]{:S(2)}) copy-start(bf16[384,1536]{1,0:T(8,128)(2,1)} %param.18) | copy-start | bytes 3538948
  6.6 56.1 %all-gather.5.cloned.1.call-start = ((), (), s32[]{:S(2)}) async-start(), calls=%async_computation.4 | async-start | bytes 9732096 | tf_op jit(solution)/shard_map/all_gather | solution.py:168
  10.2 80.3 %all-gather.7.cloned.1.call-start = ((), (), s32[]{:S(2)}) async-start(), calls=%async_computation.5 | async-start | bytes 2949120 | tf_op jit(solution)/shard_map/all_gather | solution.py:179
  11.2 147.1 %all-gather.9.cloned.1.call-start = ((), (), s32[]{:S(2)}) async-start(), calls=%async_computation.6 | async-start | bytes 6684672 | tf_op jit(solution)/shard_map/all_gather | solution.py:237
  11.5 51.1 %copy-start.20 = (s32[16]{0:T(128)}, s32[16]{0:T(128)S(1)}, u32[]{:S(2)}) copy-start(s32[16]{0:T(128)S(1)} %reduce) | copy-start | bytes 196
  12.2 0.5 copy-start.17
  12.8 77.7 %copy-start.12 = (s32[384]{0:T(512)}, s32[384]{0:T(512)S(1)}, u32[]{:S(2)}) copy-start(s32[384]{0:T(512)S(1)} %select_reduce_fusion.1) | copy-start | bytes 4612
  13.1 56.0 %copy-start.16 = (f32[384]{0:T(512)}, f32[384]{0:T(512)S(1)}, u32[]{:S(2)}) copy-start(f32[384]{0:T(512)S(1)} %add_rsqrt_fusion.1) | copy-start | bytes 4612
  66.1 3.0 copy-start.18
  90.5 7.5 %copy-start.11 = (s32[384,4]{0,1:T(4,128)S(1)}, s32[384,4]{0,1:T(4,128)}, u32[]{:S(2)}) copy-start(s32[384,4]{0,1:T(4,128)} %param.21) | copy-start | bytes 18436
  95.4 97.3 %all-gather.11.cloned.1.call-start = ((), (), s32[]{:S(2)}) async-start(), calls=%async_computation.7 | async-start | bytes 5308416 | tf_op jit(solution)/shard_map/all_gather | solution.py:232
  99.2 4.6 copy-start.7
  158.3 34.4 %copy-start.1 = (bf16[384,1536]{1,0:T(8,128)(2,1)S(1)}, bf16[384,1536]{1,0:T(8,128)(2,1)}, u32[]{:S(2)}) copy-start(bf16[384,1536]{1,0:T(8,128)(2,1)} %param.18) | copy-start | bytes 3538948
  192.8 5.8 %copy-start.13 = (s32[384]{0:T(512)S(1)}, s32[384]{0:T(512)}, u32[]{:S(2)}) copy-start(s32[384]{0:T(512)} %copy-done.12) | copy-start | bytes 4612
  192.8 5.8 %copy-start.14 = (s32[256]{0:T(256)S(1)}, s32[256]{0:T(256)}, u32[]{:S(2)}) copy-start(s32[256]{0:T(256)} %eq.83) | copy-start | bytes 3076
  198.6 3.5 copy-start.15
  202.0 6.5 %copy-start.2 = (bf16[384,1536]{1,0:T(8,128)(2,1)}, bf16[384,1536]{1,0:T(8,128)(2,1)S(1)}, u32[]{:S(2)}) copy-start(bf16[384,1536]{1,0:T(8,128)(2,1)S(1)} %get-tuple-element.15) | copy-start | bytes 3538948
  202.0 2.3 copy-start.5
  312.8 4.7 slice-start
  312.8 52.1 %all-to-all-start.2 = ((bf16[16,1,64,1792]{3,2,1,0:T(8,128)(2,1)}), bf16[16,1,64,1792]{3,2,1,0:T(8,128)(2,1)}, u32[]{:S(2)}, u32[]{:S(2)}) async-start(bf16[16,1,64,1792]{3,2,1,0:T(8,128)(2,1)} %get-tuple-element.11), calls=%async_computation.2 | async-start | bytes 7340032 | tf_op jit(solution)/shard_map/all_to_all | solution.py:271
  318.0 10.0 %copy-start.6 = (bf16[256,2,768]{2,0,1:T(8,128)(2,1)}, bf16[256,2,768]{2,0,1:T(8,128)(2,1)S(1)}, u32[]{:S(2)}) copy-start(bf16[256,2,768]{2,0,1:T(8,128)(2,1)S(1)} %copy.137) | copy-start | bytes 2359300
  364.9 41.9 %all-to-all-start.1 = ((bf16[16,1,64,1536]{3,2,1,0:T(8,128)(2,1)}), bf16[16,1,64,1536]{3,2,1,0:T(8,128)(2,1)S(1)}, u32[]{:S(2)}, u32[]{:S(2)}) async-start(bf16[16,1,64,1536]{3,2,1,0:T(8,128)(2,1)} %fusion.13), calls=%async_computation.1 | async-start | bytes 6291456 | tf_op jit(solution)/shard_map/all_to_all | solution.py:284
  387.4 25.0 %copy-start.19 = (f32[384,4]{0,1:T(4,128)S(1)}, f32[384,4]{0,1:T(4,128)}, u32[]{:S(2)}) copy-start(f32[384,4]{0,1:T(4,128)} %param.22) | copy-start | bytes 18436
  406.8 47.4 %all-to-all-start.3 = ((bf16[16,1,64,1536]{3,2,1,0:T(8,128)(2,1)}), bf16[16,1,64,1536]{3,2,1,0:T(8,128)(2,1)}, u32[]{:S(2)}, u32[]{:S(2)}) async-start(bf16[16,1,64,1536]{3,2,1,0:T(8,128)(2,1)} %fusion.14), calls=%async_computation.3 | async-start | bytes 6291456 | tf_op jit(solution)/shard_map/all_to_all | solution.py:284
  454.3 2.8 copy-start.4
  457.1 2.6 copy-start.3
Sparse Core Ops, SparseCore 0:
  10.3 52.2 all-gather.4
  64.3 26.1 all-gather.6
  95.6 62.7 all-gather.8
  159.9 32.8 all-gather.10

commit v11 on v9

--- a/solution.py
+++ b/solution.py
@@ -43,7 +43,7 @@
     return jnp.dot(coords, second, preferred_element_type=jnp.float32)
 
 
-KEY_BLOCK = 256
+KEY_BLOCK = 1024
 
 
 def attention_kernel(first_ref, bmin_ref, bmax_ref, qrange_ref, q_ref, k_ref, v_ref, qseg_ref,

time: 511 us -> 461 us (0.902)
  the two profiles are of different devices: /device:TPU:100 before, /device:TPU:8 now
where the time goes in v11:
time: 461 us; the launch traced here: 456 us
  waiting for transfers between devices  190 us (41%)
  blocking collectives  87.1 us (19%)
  matrix products  69.2 us (15%)
  local copies, waits for them, and re-layouts  32.1 us (7%)
  other arithmetic  27.6 us (6%)
  Pallas kernels  20.6 us (4%)
  starting transfers between devices  15.1 us (3%)
  between operations  13.8 us (3%)
    all_to_all x1, blocking collectives, expert_chunk(): lax.all_to_all(chunk, 'exp', split_axis=0, concat_axis=0, tiled=True)  87.1 us
    all_to_all x2, waiting for transfers between devices, expert_chunk(): lax.all_to_all(outputs, 'exp', split_axis=0, concat_axis=0, tiled=True)  51.5 us
    all_gather x1, waiting for transfers between devices, gather_weights(): lax.all_gather(jnp.concatenate([attention_in] + down_cols, axis=1), axis_...  49.6 us
    all_gather x1, waiting for transfers between devices, body(): key_piece = lax.all_gather(key_value, 'exp', axis=0, tiled=True)  34.2 us
    all_to_all x1, waiting for transfers between devices, expert_chunk(): lax.all_to_all(chunk, 'exp', split_axis=0, concat_axis=0, tiled=True)  25.5 us
    dot_general x2, matrix products, expert_chunk(): jnp.einsum('necd,edf->necf', arrived_rows, expert_gate_up, preferred_elem...  22.1 us
    pallas_call x1, Pallas kernels, window_attention(): pl.pallas_call(attention_kernel, grid_spec=grid_spec, out_shape=jax.Shape...  20.6 us
    all_gather x1, waiting for transfers between devices, gather_weights(): lax.all_gather(jnp.concatenate(up_rows, axis=1), axis_name, axis=0, tiled...  17.1 us
  transfers between devices with their start and end apart: 7, of which 7 were waited for; matrix products, arithmetic and copies ran while one was open for 20% of the time, Pallas kernels for 5%

profile of v11, /device:TPU:8, one launch (start us, length us, event | category | flops | bytes accessed | tf_op | source)
XLA Modules:
  0.0 455.5 jit_solution(387456736534228205)
XLA Ops:
  13.1 49.6 %all-gather.5.cloned.1.call-done = bf16[1536,2816]{0,1:T(8,128)(2,1)} async-done(((bf16[1536,352]{0,1:T(8,128)(2,1)}), bf16[1536,2816]{0,1:T(8,128)(2,1)}) %all-gather.5.cloned.1.call-update) | async-done | bytes 8650768 | tf_op jit(solution)/shard_map/all_gather | solution.py:168
  62.6 3.5 slice.96
  66.1 3.0 fusion.81
  69.1 4.3 fusion.64
  73.4 17.1 %all-gather.7.cloned.1.call-done = bf16[256,5120]{1,0:T(8,128)(2,1)} async-done(((bf16[32,5120]{1,0:T(8,128)(2,1)}), bf16[256,5120]{1,0:T(8,128)(2,1)}) %all-gather.7.cloned.1.call-update) | async-done | bytes 2621456 | tf_op jit(solution)/shard_map/all_gather | solution.py:179
  90.5 4.1 add_convert_fusion
  100.0 3.7 broadcast_in_dim.73.init_ref
  103.8 9.1 %reduce-window.19 = s32[32,12,128]{2,1,0:T(8,128)S(1)} reduce-window(s32[32,12,128]{2,1,0:T(8,128)S(1)} %fusion.66, s32[]{:T(128)} %constant.16.clone.1), window={size=1x1x128 pad=0_0x0_0x127_0}, to_apply=%region_7.8 | reduce-window | flops 6242304 | bytes 393220 | tf_op jit(solution)/shard_map/reduce-window.1
  117.0 4.8 %fusion = pred[2048,384]{1,0:T(8,128)(4,1)} fusion(s32[384,4]{0,1:T(4,128)S(1)} %multiply_add_fusion), kind=kLoop, calls=%fused_computation.3 | loop fusion | flops 5505024 | bytes 792576 | tf_op jit(solution)/shard_map/reduce_or | solution.py:257
  124.1 34.2 %all-gather.9.cloned.1.call-done.k_ref.v_ref = bf16[6144,512]{1,0:T(8,128)(2,1)} async-done(((bf16[384,512]{1,0:T(8,128)(2,1)}), bf16[6144,512]{1,0:T(8,128)(2,1)}) %all-gather.9.cloned.1.call-update) | async-done | bytes 6291472 | tf_op jit(solution)/shard_map/all_gather | solution.py:237
  158.3 20.6 %shard_map.172 = bf16[2,2304,128]{2,1,0:T(8,128)(2,1)} custom-call(s32[1]{0:T(128)} %slice.72.first_ref, s32[6]{0:T(128)} %get-tuple-element.6.bmin_ref, s32[6]{0:T(128)} %get-tuple-element.5.bmax_ref, s32[2]{0:T(128)} %pad_add_fusion.qrange_ref, bf16[2,2304,128]{2,1,0:T(8,128)(2,1)} %bitcast.119, ...), custom_call_target="tpu_custom_call" | custom-call | tf_op jit(solution)/shard_map/pallas_call | solution.py:149
  180.6 12.1 %all-gather.11.cloned.1.call-done = bf16[1536,1536]{0,1:T(8,128)(2,1)} async-done(((bf16[1536,192]{0,1:T(8,128)(2,1)}), bf16[1536,1536]{0,1:T(8,128)(2,1)}) %all-gather.11.cloned.1.call-update) | async-done | bytes 4718608 | tf_op jit(solution)/shard_map/all_gather | solution.py:232
  192.7 5.8 %convert_add_fusion.1 = f32[384,1536]{1,0:T(8,128)} fusion(bf16[384,1536]{1,0:T(8,128)(2,1)S(1)} %copy-done.1, bf16[384,1536]{0,1:T(8,128)(2,1)S(1)} %bitcast.122, bf16[1536,1536]{0,1:T(8,128)(2,1)} %all-gather.11.cloned.1.call-done), kind=kOutput, calls=%fused_computation.21 | convolution fusion | flops 1813118976 | bytes 9437184 | tf_op jit(solution)/shard_map/dot_general | solution.py:241
  198.5 3.4 fusion.38
  204.3 4.3 convolution_convert_fusion
  208.6 2.4 fusion.82
  211.0 87.1 %all_to_all.20 = bf16[16,2,32,1792]{3,2,1,0:T(8,128)(2,1)} all-to-all(bf16[16,2,32,1792]{3,2,1,0:T(8,128)(2,1)S(1)} %get-tuple-element.10), channel_id=1, replica_groups=mesh['req'=8,'exp'=16] {'exp'}, dimensions={0} | all-to-all | bytes 7340032 | tf_op jit(solution)/shard_map/all_to_all | solution.py:271
  298.1 4.6 %all-to-all-start.2 = ((bf16[16,2,32,1792]{3,2,1,0:T(8,128)(2,1)}), bf16[16,2,32,1792]{3,2,1,0:T(8,128)(2,1)}, u32[]{:S(2)}, u32[]{:S(2)}) async-start(bf16[16,2,32,1792]{3,2,1,0:T(8,128)(2,1)} %get-tuple-element.11), calls=%async_computation.2 | async-start | bytes 7340032 | tf_op jit(solution)/shard_map/all_to_all | solution.py:271
  304.2 11.0 %fusion.9 = f32[16,2,32,1536]{3,2,0,1:T(8,128)} fusion(bf16[2,1536,1536]{2,1,0:T(8,128)(2,1)} %param.28, bf16[16,2,32,1792]{3,2,1,0:T(8,128)(2,1)} %all_to_all.20), kind=kOutput, calls=%fused_computation.14 | convolution fusion | flops 4831838208 | bytes 18874368 | tf_op jit(solution)/shard_map/necd,edf->necf/dot_general | solution.py:274
  315.2 7.7 %fusion.24 = bf16[16,2,32,1536]{3,2,0,1:T(8,128)(2,1)S(1)} fusion(bf16[2,768,1536]{2,1,0:T(8,128)(2,1)} %param.29, f32[16,2,32,1536]{3,2,0,1:T(8,128)} %fusion.9, bf16[256,2,768]{2,0,1:T(8,128)(2,1)} %copy.160, bf16[16,2,32,1792]{3,2,1,0:T(8,128)(2,1)} %all_to_all.20), kind=kOutput, calls=%fused_computation.25 | convolution fusion | flops 2823290880 | bytes 15466496 | tf_op jit(solution)/shard_map/necf,efd->necd/dot_general | solution.py:281
  324.7 25.5 %all-to-all-done.2 = bf16[16,2,32,1792]{3,2,1,0:T(8,128)(2,1)} async-done(((bf16[16,2,32,1792]{3,2,1,0:T(8,128)(2,1)}), bf16[16,2,32,1792]{3,2,1,0:T(8,128)(2,1)}, u32[]{:S(2)}, u32[]{:S(2)}) %all-to-all-start.2) | async-done | bytes 3670048 | tf_op jit(solution)/shard_map/all_to_all | solution.py:271
  350.2 4.2 all-to-all-start.1
  354.4 11.0 %fusion.12 = f32[16,2,32,1536]{3,2,0,1:T(8,128)} fusion(bf16[2,1536,1536]{2,1,0:T(8,128)(2,1)} %param.28, bf16[16,2,32,1792]{3,2,1,0:T(8,128)(2,1)} %all-to-all-done.2), kind=kOutput, calls=%fused_computation.15 | convolution fusion | flops 4831838208 | bytes 18874368 | tf_op jit(solution)/shard_map/necd,edf->necf/dot_general | solution.py:274
  365.5 9.3 %fusion.21 = bf16[16,2,32,1536]{3,2,0,1:T(8,128)(2,1)} fusion(bf16[2,768,1536]{2,1,0:T(8,128)(2,1)} %param.29, f32[16,2,32,1536]{3,2,0,1:T(8,128)} %fusion.12, bf16[256,2,768]{2,0,1:T(8,128)(2,1)} %copy.160, bf16[16,2,32,1792]{3,2,1,0:T(8,128)(2,1)} %all-to-all-done.2), kind=kOutput, calls=%fused_computation.24 | convolution fusion | flops 2823290880 | bytes 15466496 | tf_op jit(solution)/shard_map/necf,efd->necd/dot_general | solution.py:281
  374.8 3.9 copy.165
  378.7 13.4 %all-to-all-done.1 = bf16[16,2,32,1536]{3,2,1,0:T(8,128)(2,1)S(1)} async-done(((bf16[16,2,32,1536]{3,2,1,0:T(8,128)(2,1)}), bf16[16,2,32,1536]{3,2,1,0:T(8,128)(2,1)S(1)}, u32[]{:S(2)}, u32[]{:S(2)}) %all-to-all-start.1) | async-done | bytes 3145760 | tf_op jit(solution)/shard_map/all_to_all | solution.py:284
  392.1 5.6 %all-to-all-start.3 = ((bf16[16,2,32,1536]{3,2,1,0:T(8,128)(2,1)}), bf16[16,2,32,1536]{3,2,1,0:T(8,128)(2,1)}, u32[]{:S(2)}, u32[]{:S(2)}) async-start(bf16[16,2,32,1536]{3,2,1,0:T(8,128)(2,1)} %copy.165), calls=%async_computation.3 | async-start | bytes 6291456 | tf_op jit(solution)/shard_map/all_to_all | solution.py:284
  397.8 3.8 select_reduce_fusion
  401.5 38.1 %all-to-all-done.3 = bf16[16,2,32,1536]{3,2,1,0:T(8,128)(2,1)} async-done(((bf16[16,2,32,1536]{3,2,1,0:T(8,128)(2,1)}), bf16[16,2,32,1536]{3,2,1,0:T(8,128)(2,1)}, u32[]{:S(2)}, u32[]{:S(2)}) %all-to-all-start.3) | async-done | bytes 3145760 | tf_op jit(solution)/shard_map/all_to_all | solution.py:284
  439.6 2.6 pad_maximum_fusion
  442.5 2.6 fusion.54
  445.1 3.7 fusion.34
  (102 shorter events, 25.7 us)
Async XLA Ops:
  6.5 3.7 copy-start.9
  6.5 3.8 copy-start.7
  6.5 3.8 copy-start.8
  6.5 4.7 %copy-start.20 = (s32[1,16]{1,0:T(1,128)S(1)}, s32[1,16]{1,0:T(1,128)}, u32[]{:S(2)}) copy-start(s32[1,16]{1,0:T(1,128)} %param.19) | copy-start | bytes 196
  6.5 6.1 %copy-start.21 = (s32[1,16]{1,0:T(1,128)S(1)}, s32[1,16]{1,0:T(1,128)}, u32[]{:S(2)}) copy-start(s32[1,16]{1,0:T(1,128)} %param.20) | copy-start | bytes 196
  6.5 6.2 %copy-start = (bf16[384,1536]{1,0:T(8,128)(2,1)S(1)}, bf16[384,1536]{1,0:T(8,128)(2,1)}, u32[]{:S(2)}) copy-start(bf16[384,1536]{1,0:T(8,128)(2,1)} %param.18) | copy-start | bytes 3538948
  6.6 56.1 %all-gather.5.cloned.1.call-start = ((), (), s32[]{:S(2)}) async-start(), calls=%async_computation.4 | async-start | bytes 9732096 | tf_op jit(solution)/shard_map/all_gather | solution.py:168
  10.2 80.3 %all-gather.7.cloned.1.call-start = ((), (), s32[]{:S(2)}) async-start(), calls=%async_computation.5 | async-start | bytes 2949120 | tf_op jit(solution)/shard_map/all_gather | solution.py:179
  11.2 147.1 %all-gather.9.cloned.1.call-start = ((), (), s32[]{:S(2)}) async-start(), calls=%async_computation.6 | async-start | bytes 6684672 | tf_op jit(solution)/shard_map/all_gather | solution.py:237
  11.5 51.1 %copy-start.19 = (s32[16]{0:T(128)}, s32[16]{0:T(128)S(1)}, u32[]{:S(2)}) copy-start(s32[16]{0:T(128)S(1)} %reduce) | copy-start | bytes 196
  12.1 0.5 copy-start.16
  12.7 77.8 %copy-start.11 = (s32[384]{0:T(512)}, s32[384]{0:T(512)S(1)}, u32[]{:S(2)}) copy-start(s32[384]{0:T(512)S(1)} %select_reduce_fusion.1) | copy-start | bytes 4612
  13.1 56.0 %copy-start.15 = (f32[384]{0:T(512)}, f32[384]{0:T(512)S(1)}, u32[]{:S(2)}) copy-start(f32[384]{0:T(512)S(1)} %add_rsqrt_fusion.1) | copy-start | bytes 4612
  66.1 3.0 copy-start.17
  90.5 7.5 %copy-start.10 = (s32[384,4]{0,1:T(4,128)S(1)}, s32[384,4]{0,1:T(4,128)}, u32[]{:S(2)}) copy-start(s32[384,4]{0,1:T(4,128)} %param.21) | copy-start | bytes 18436
  95.4 97.3 %all-gather.11.cloned.1.call-start = ((), (), s32[]{:S(2)}) async-start(), calls=%async_computation.7 | async-start | bytes 5308416 | tf_op jit(solution)/shard_map/all_gather | solution.py:232
  99.2 4.6 %copy-start.6 = (s32[6144]{0:T(1024)}, s32[6144]{0:T(1024)S(1)}, u32[]{:S(2)}) copy-start(s32[6144]{0:T(1024)S(1)} %convert_reduce_fusion) | copy-start | bytes 73732
  158.3 34.4 %copy-start.1 = (bf16[384,1536]{1,0:T(8,128)(2,1)S(1)}, bf16[384,1536]{1,0:T(8,128)(2,1)}, u32[]{:S(2)}) copy-start(bf16[384,1536]{1,0:T(8,128)(2,1)} %param.18) | copy-start | bytes 3538948
  192.7 5.8 %copy-start.12 = (s32[384]{0:T(512)S(1)}, s32[384]{0:T(512)}, u32[]{:S(2)}) copy-start(s32[384]{0:T(512)} %copy-done.11) | copy-start | bytes 4612
  192.7 5.8 %copy-start.13 = (s32[256]{0:T(256)S(1)}, s32[256]{0:T(256)}, u32[]{:S(2)}) copy-start(s32[256]{0:T(256)} %eq.83) | copy-start | bytes 3076
  198.5 3.5 copy-start.14
  201.9 6.7 %copy-start.2 = (bf16[384,1536]{1,0:T(8,128)(2,1)}, bf16[384,1536]{1,0:T(8,128)(2,1)S(1)}, u32[]{:S(2)}) copy-start(bf16[384,1536]{1,0:T(8,128)(2,1)S(1)} %get-tuple-element.15) | copy-start | bytes 3538948
  201.9 2.3 copy-start.5
  298.1 4.7 %slice-start = ((bf16[256,5120]{1,0:T(8,128)(2,1)}), bf16[256,1536]{1,0:T(8,128)(2,1)S(1)}, s32[]{:S(2)}) async-start(bf16[256,5120]{1,0:T(8,128)(2,1)} %all-gather.7.cloned.1.call-done), calls=%async_computation.8 | async-start | bytes 1572864 | tf_op jit(solution)/shard_map/slice | solution.py:183
  298.1 52.1 %all-to-all-start.2 = ((bf16[16,2,32,1792]{3,2,1,0:T(8,128)(2,1)}), bf16[16,2,32,1792]{3,2,1,0:T(8,128)(2,1)}, u32[]{:S(2)}, u32[]{:S(2)}) async-start(bf16[16,2,32,1792]{3,2,1,0:T(8,128)(2,1)} %get-tuple-element.11), calls=%async_computation.2 | async-start | bytes 7340032 | tf_op jit(solution)/shard_map/all_to_all | solution.py:271
  350.2 41.9 %all-to-all-start.1 = ((bf16[16,2,32,1536]{3,2,1,0:T(8,128)(2,1)}), bf16[16,2,32,1536]{3,2,1,0:T(8,128)(2,1)S(1)}, u32[]{:S(2)}, u32[]{:S(2)}) async-start(bf16[16,2,32,1536]{3,2,1,0:T(8,128)(2,1)} %copy.162), calls=%async_computation.1 | async-start | bytes 6291456 | tf_op jit(solution)/shard_map/all_to_all | solution.py:284
  378.7 19.1 %copy-start.18 = (f32[384,4]{0,1:T(4,128)S(1)}, f32[384,4]{0,1:T(4,128)}, u32[]{:S(2)}) copy-start(f32[384,4]{0,1:T(4,128)} %param.22) | copy-start | bytes 18436
  392.1 47.5 %all-to-all-start.3 = ((bf16[16,2,32,1536]{3,2,1,0:T(8,128)(2,1)}), bf16[16,2,32,1536]{3,2,1,0:T(8,128)(2,1)}, u32[]{:S(2)}, u32[]{:S(2)}) async-start(bf16[16,2,32,1536]{3,2,1,0:T(8,128)(2,1)} %copy.165), calls=%async_computation.3 | async-start | bytes 6291456 | tf_op jit(solution)/shard_map/all_to_all | solution.py:284
  439.6 2.8 copy-start.4
  442.5 2.6 copy-start.3
Sparse Core Ops, SparseCore 0:
  10.3 52.2 all-gather.4
  64.3 26.1 all-gather.6
  95.6 62.6 all-gather.8
  159.8 32.8 all-gather.10
